TPU v7x, 256 devices: a whole 4x4x8 slice. The times are simulated.
256 devices in a mesh: dp: 64 (over z, y, core), mp: 4 (over x).
Axes of the slice: x: 4, y: 4, z: 8, core: 2. Of those that a mesh axis runs over, the one named last changes fastest.
Arguments:
- attention: bfloat16 [8192, 2048], P('dp', 'mp'), may hold values from -6 to 6
- residual: bfloat16 [8192, 2048], P('dp', 'mp'), may hold values from -6 to 6
- out_weight: bfloat16 [2048, 2048], P('mp', 'dp'), may hold values from -0.125 to 0.125
- ffn_gain: float32 [2048], P('mp'), may hold values from 0.1 to 1.9
- shared_gate: bfloat16 [2048, 2816], P('dp', 'mp'), may hold values from -0.125 to 0.125
- shared_up: bfloat16 [2048, 2816], P('dp', 'mp'), may hold values from -0.125 to 0.125
- shared_down: bfloat16 [2816, 2048], P('mp', 'dp'), may hold values from -0.109375 to 0.109375
- expert_gate: bfloat16 [64, 2048, 1408], P('dp', None, 'mp'), may hold values from -0.125 to 0.125
- expert_up: bfloat16 [64, 2048, 1408], P('dp', None, 'mp'), may hold values from -0.125 to 0.125
- expert_down: bfloat16 [64, 1408, 2048], P('dp', 'mp'), may hold values from -0.15625 to 0.15625
- route_ids: int32 [8192, 6], P('dp'), may hold values from 0 to 63, all different within a row; in each aligned block of 128 rows (0 to 127, 128 to 255, ...) at most 16 rows name the same one
- route_scores: float32 [8192, 6], P('dp'), may hold values from 0.05 to 1
- placement: int32 [64], replicated, may hold values from 0 to 63, each once
- next_gain: float32 [2048], P('mp'), may hold values from 0.1 to 1.9
Outputs:
- final: bfloat16 [8192, 2048], P('dp', 'mp')
- next_normed: bfloat16 [8192, 2048], P('dp', 'mp')
Inputs may be any that keep to these rules, and one draw needn't show every extreme that they name: `route_ids`: A token's 6 experts differ. In each aligned block of 128 rows (the rows of one index of dp) no expert is named by more than 16 rows, a bound that some block reaches. `placement`: each storage index is used by exactly one expert.
All inputs are finite; a program needn't handle non-finite values.
Results may differ from a plain program's by a relative error of at most 0.0075.
Values may be sent and summed in bfloat16 or wider, within the bound.
A program may use at most 128 MiB of HBM per device.

v0:
```python
import jax
import jax.numpy as jnp
from jax import lax
from jax.sharding import PartitionSpec as P

D = 2048


EPSILON = 1e-06


def matmul(left, right):
    return jnp.dot(left, right, preferred_element_type=jnp.float32)


def local(
    attention,
    residual,
    out_weight,
    ffn_gain,
    shared_gate,
    shared_up,
    shared_down,
    expert_gate,
    expert_up,
    expert_down,
    route_ids,
    route_scores,
    placement,
    next_gain,
):
    tok_rows = attention.shape[0]
    top_count = route_ids.shape[1]
    mp_count = lax.axis_size("mp")
    mp_index = lax.axis_index("mp")
    experts = lax.axis_size("dp")
    capacity = min(tok_rows, 8 * tok_rows // experts)
    model_width = D
    partial_value = matmul(attention, lax.all_gather(out_weight, "dp", axis=1, tiled=True))
    projected = lax.psum_scatter(partial_value, "mp", scatter_dimension=1, tiled=True)
    hidden = (residual.astype(jnp.float32) + projected).astype(jnp.bfloat16)
    hidden_float = hidden.astype(jnp.float32)
    squares = lax.psum(jnp.sum(hidden_float * hidden_float, axis=1), "mp")
    normed = (hidden_float * lax.rsqrt(squares / model_width + EPSILON)[:, None] * ffn_gain).astype(
        jnp.bfloat16
    )
    whole_rows = lax.all_gather(normed, "mp", axis=1, tiled=True)
    pieces = (
        lax.all_gather(shared_gate, "dp", axis=0, tiled=True),
        lax.all_gather(shared_up, "dp", axis=0, tiled=True),
    )
    shared_gval = matmul(whole_rows, pieces[0])
    shared_uval = matmul(whole_rows, pieces[1])
    shared_act = (jax.nn.silu(shared_gval) * shared_uval).astype(jnp.bfloat16)
    shared_part = matmul(shared_act, lax.all_gather(shared_down, "dp", axis=1, tiled=True))
    flat_ids = route_ids.reshape(-1)
    expert_iota = jnp.arange(experts, dtype=jnp.int32)
    one_hot = (flat_ids[:, None] == expert_iota[None, :]).astype(jnp.int32)
    target = jnp.sum(one_hot * placement[None, :], axis=1)
    slot = jnp.sum((jnp.cumsum(one_hot, axis=0) - one_hot) * one_hot, axis=1)
    token_of = jnp.arange(flat_ids.shape[0], dtype=jnp.int32) // top_count
    flat_scores = route_scores.reshape(-1)
    gate_local = expert_gate[0]
    up_local = expert_up[0]
    down_local = expert_down[0]
    quarter = capacity // mp_count
    owned = slot // quarter == mp_index
    position = jnp.where(owned, target * quarter + slot % quarter, experts * quarter)
    outgoing = (
        jnp.zeros((experts * quarter, model_width), jnp.bfloat16)
        .at[position]
        .set(whole_rows[token_of], mode="drop")
    )
    arrived = lax.all_to_all(
        outgoing.reshape(experts, quarter, model_width),
        "dp",
        split_axis=0,
        concat_axis=0,
        tiled=True,
    )
    in_rows = arrived.reshape(experts * quarter, model_width)
    pieces = (
        lax.all_gather(gate_local, "mp", axis=1, tiled=True),
        lax.all_gather(up_local, "mp", axis=1, tiled=True),
    )
    gate_val = matmul(in_rows, pieces[0])
    up_val = matmul(in_rows, pieces[1])
    activated = (jax.nn.silu(gate_val) * up_val).astype(jnp.bfloat16)
    outputs = matmul(activated, lax.all_gather(down_local, "mp", axis=0, tiled=True)).astype(
        jnp.bfloat16
    )
    returned = lax.all_to_all(
        outputs.reshape(experts, quarter, model_width),
        "dp",
        split_axis=0,
        concat_axis=0,
        tiled=True,
    )
    returned = returned.reshape(experts * quarter, model_width)
    bounded = jnp.minimum(position, experts * quarter - 1)
    weight = jnp.where(owned, flat_scores, 0.0)
    picked = returned[bounded].astype(jnp.float32) * weight[:, None]
    routed = jnp.sum(picked.reshape(tok_rows, top_count, model_width), axis=1)
    mixture = lax.psum_scatter(routed + shared_part, "mp", scatter_dimension=1, tiled=True)
    final = (hidden_float + mixture).astype(jnp.bfloat16)
    final_float = final.astype(jnp.float32)
    final_squares = lax.psum(jnp.sum(final_float * final_float, axis=1), "mp")
    next_normed = (
        final_float * lax.rsqrt(final_squares / model_width + EPSILON)[:, None] * next_gain
    ).astype(jnp.bfloat16)
    return (final, next_normed)


def solution(mesh):
    in_specs = (
        P("dp", "mp"),
        P("dp", "mp"),
        P("mp", "dp"),
        P("mp"),
        P("dp", "mp"),
        P("dp", "mp"),
        P("mp", "dp"),
        P("dp", None, "mp"),
        P("dp", None, "mp"),
        P("dp", "mp", None),
        P("dp", None),
        P("dp", None),
        P(),
        P("mp"),
    )
    out_specs = (P("dp", "mp"), P("dp", "mp"))
    return jax.shard_map(local, mesh=mesh, in_specs=in_specs, out_specs=out_specs, check_vma=False)
```

profile of v0, /device:TPU:8, one launch (start us, length us, event | category | flops | bytes accessed | tf_op | source)
XLA Modules:
  0.0 608.2 jit_solution(1089432544255874928)
XLA Ops:
  7.2 0.7 all-gather.11.cloned.1.call-update
  8.0 82.0 %all-gather.11.cloned.1.call-done = bf16[512,2048]{0,1:T(8,128)(2,1)} async-done(((bf16[512,32]{0,1:T(8,128)(2,1)}), bf16[512,2048]{0,1:T(8,128)(2,1)}) %all-gather.11.cloned.1.call-update) | async-done | bytes 2097168 | tf_op jit(solution)/shard_map/all_gather | solution.py:39
  90.0 3.4 fusion.50
  93.4 0.7 all-gather.19.cloned.1.call-update
  94.2 0.5 all-gather.21.cloned.1.call-update
  94.8 0.5 all-gather.23.cloned.1.call-update
  95.3 0.5 all-gather.13.cloned.1.call-update
  95.9 0.7 all-gather.15.cloned.1.call-update
  96.6 0.1 copy.24
  96.7 0.1 eq.55
  96.9 0.1 eq.51
  97.0 1.8 reduce-window.6
  98.8 0.3 slice_reduce_fusion
  99.2 0.1 fusion.36
  99.4 18.8 %reduce-scatter.3.cloned.1.call-done = f32[128,512]{1,0:T(8,128)} async-done(((f32[128,2048]{1,0:T(8,128)}), f32[128,512]{1,0:T(8,128)}) %reduce-scatter.3.cloned.1.call-update) | async-done | bytes 262160 | tf_op jit(solution)/shard_map/reduce_scatter | solution.py:40
  118.2 1.1 fusion.30
  119.3 8.5 %psum.14 = f32[128]{0:T(128)S(1)} all-reduce(f32[128]{0:T(128)S(1)} %get-tuple-element.8), channel_id=1, replica_groups=mesh['dp'=64,'mp'=4] {'mp'}, use_global_device_ids=true, to_apply=%region_6.7 | all-reduce | flops 128 | bytes 1024 | tf_op jit(solution)/shard_map/psum | solution.py:43
  127.8 0.1 fusion.32
  127.9 14.2 %all_gather.25 = bf16[128,2048]{1,0:T(8,128)(2,1)S(1)} all-gather(bf16[128,512]{1,0:T(8,128)(2,1)S(1)} %fusion.32), channel_id=1, replica_groups=mesh['dp'=64,'mp'=4] {'mp'}, dimensions={1}, use_global_device_ids=true | all-gather | bytes 655360 | tf_op jit(solution)/shard_map/all_gather | solution.py:47
  142.1 20.4 %scatter_custom_fusion = bf16[256,2048]{1,0:T(8,128)(2,1)S(1)} fusion(s32[768]{0:T(1024)S(1)} %get-tuple-element.5, bf16[128,2048]{1,0:T(8,128)(2,1)S(1)} %all_gather.25, s32[1024]{0:T(1024)S(1)} %pad_clamp_fusion.1, bf16[]{:T(256)} %constant.52.clone.1), kind=kCustom, calls=%fused_computation.10 | custom fusion | bytes 1048578 | tf_op jit(solution)/shard_map/scatter | solution.py:72
  162.5 1.3 reshape.214
  163.8 10.6 %all-to-all-start = ((bf16[64,4,2048]{2,1,0:T(4,128)(2,1)}), bf16[64,4,2048]{2,1,0:T(4,128)(2,1)S(1)}, u32[]{:S(2)}, u32[]{:S(2)}) async-start(bf16[64,4,2048]{2,1,0:T(4,128)(2,1)} %reshape.214), calls=%async_computation.1 | async-start | bytes 2097152 | tf_op jit(solution)/shard_map/all_to_all | solution.py:74
  174.4 0.7 all-gather.17.cloned.1.call-update
  175.1 28.0 %all-to-all-done = bf16[64,4,2048]{2,1,0:T(4,128)(2,1)S(1)} async-done(((bf16[64,4,2048]{2,1,0:T(4,128)(2,1)}), bf16[64,4,2048]{2,1,0:T(4,128)(2,1)S(1)}, u32[]{:S(2)}, u32[]{:S(2)}) %all-to-all-start) | async-done | bytes 1048608 | tf_op jit(solution)/shard_map/all_to_all | solution.py:74
  203.1 0.3 reshape.215
  203.4 5.6 fusion.4
  209.0 41.9 %all-gather.21.cloned.1.call-done = bf16[1,2048,1408]{1,2,0:T(8,128)(2,1)} async-done(((bf16[1,2048,352]{1,2,0:T(8,128)(2,1)}), bf16[1,2048,1408]{1,2,0:T(8,128)(2,1)}) %all-gather.21.cloned.1.call-update) | async-done | bytes 5767184 | tf_op jit(solution)/shard_map/all_gather | solution.py:84
  250.9 66.3 %all-gather.23.cloned.1.call-done = bf16[1,1408,2048]{2,1,0:T(8,128)(2,1)} async-done(((bf16[1,352,2048]{2,1,0:T(8,128)(2,1)}), bf16[1,1408,2048]{2,1,0:T(8,128)(2,1)}) %all-gather.23.cloned.1.call-update) | async-done | bytes 5767184 | tf_op jit(solution)/shard_map/all_gather | solution.py:89
  317.2 8.3 %fusion.14 = bf16[256,2048]{1,0:T(8,128)(2,1)S(1)} fusion(bf16[1,1408,2048]{2,1,0:T(8,128)(2,1)} %all-gather.23.cloned.1.call-done, bf16[256,2048]{1,0:T(8,128)(2,1)S(1)} %reshape.215, bf16[1,2048,1408]{1,2,0:T(8,128)(2,1)} %all-gather.21.cloned.1.call-done, f32[256,1408]{1,0:T(8,128)} %fusion.4), kind=kOutput, calls=%fused_computation.14 | convolution fusion | flops 2955476992 | bytes 15073280 | tf_op jit(solution)/shard_map/dot_general | solution.py:13
  325.5 1.2 reshape.216
  326.8 10.6 %all-to-all-start.1 = ((bf16[64,4,2048]{2,1,0:T(4,128)(2,1)}), bf16[64,4,2048]{2,1,0:T(4,128)(2,1)S(1)}, u32[]{:S(2)}, u32[]{:S(2)}) async-start(bf16[64,4,2048]{2,1,0:T(4,128)(2,1)} %reshape.216), calls=%async_computation.2 | async-start | bytes 2097152 | tf_op jit(solution)/shard_map/all_to_all | solution.py:92
  337.3 0.3 reduce-scatter.5.cloned.1.call-start
  337.6 0.1 reduce_sum.53
  337.7 0.1 copy.27
  337.8 0.1 copy.31
  338.0 63.4 %all-gather.13.cloned.1.call-done = bf16[2048,704]{1,0:T(8,128)(2,1)} async-done(((bf16[32,704]{1,0:T(8,128)(2,1)}), bf16[2048,704]{1,0:T(8,128)(2,1)}) %all-gather.13.cloned.1.call-update) | async-done | bytes 2883600 | tf_op jit(solution)/shard_map/all_gather | solution.py:49
  401.4 3.2 fusion.51
  404.6 0.3 reshape.217
  404.8 4.3 gather_fusion
  409.2 6.6 %reshape.218 = f32[128,6,2048]{2,1,0:T(8,128)} reshape(bf16[768,2048]{1,0:T(8,128)(2,1)} %gather_fusion) | data formatting | bytes 9437184 | tf_op jit(solution)/shard_map/convert_element_type | solution.py:102
  415.7 6.6 %multiply_reduce_fusion = f32[128,2048]{1,0:T(8,128)S(1)} fusion(f32[128,6,2048]{2,1,0:T(8,128)} %reshape.218, f32[128,6]{1,0:T(8,128)S(1)} %copy.31), kind=kLoop, calls=%fused_computation.3 | loop fusion | flops 2883584 | bytes 7343104 | tf_op jit(solution)/shard_map/reduce_sum | solution.py:103
  422.3 58.0 %all-gather.15.cloned.1.call-done = bf16[2048,704]{1,0:T(8,128)(2,1)} async-done(((bf16[32,704]{1,0:T(8,128)(2,1)}), bf16[2048,704]{1,0:T(8,128)(2,1)}) %all-gather.15.cloned.1.call-update) | async-done | bytes 2883600 | tf_op jit(solution)/shard_map/all_gather | solution.py:50
  480.3 78.9 %all-gather.17.cloned.1.call-done = bf16[704,2048]{0,1:T(8,128)(2,1)} async-done(((bf16[704,32]{0,1:T(8,128)(2,1)}), bf16[704,2048]{0,1:T(8,128)(2,1)}) %all-gather.17.cloned.1.call-update) | async-done | bytes 2883600 | tf_op jit(solution)/shard_map/all_gather | solution.py:55
  559.2 7.2 %convolution_add_fusion = f32[128,2048]{1,0:T(8,128)} fusion(f32[128,2048]{1,0:T(8,128)S(1)} %multiply_reduce_fusion, bf16[704,2048]{0,1:T(8,128)(2,1)} %all-gather.17.cloned.1.call-done, bf16[128,2048]{1,0:T(8,128)(2,1)S(1)} %all_gather.25, bf16[2048,704]{1,0:T(8,128)(2,1)} %all-gather.15.cloned.1.call-done, f32[128,704]{0,1:T(8,128)S(1)} %fusion.51), kind=kOutput, calls=%fused_computation.15 | convolution fusion | flops 739000320 | bytes 8749056 | tf_op jit(solution)/shard_map/dot_general | solution.py:13
  566.5 24.9 %reduce-scatter.5.cloned.1.call-done = f32[128,512]{1,0:T(8,128)} async-done(((f32[128,2048]{1,0:T(8,128)}), f32[128,512]{1,0:T(8,128)}) %reduce-scatter.5.cloned.1.call-update) | async-done | bytes 262160 | tf_op jit(solution)/shard_map/reduce_scatter | solution.py:104
  591.3 1.1 fusion.27
  592.4 8.5 %psum.15 = f32[128]{0:T(128)S(1)} all-reduce(f32[128]{0:T(128)S(1)} %get-tuple-element.6), channel_id=1, replica_groups=mesh['dp'=64,'mp'=4] {'mp'}, use_global_device_ids=true, to_apply=%region_11.12 | all-reduce | flops 128 | bytes 1024 | tf_op jit(solution)/shard_map/psum | solution.py:107
  600.9 0.8 fusion.29
  (38 shorter events, 0.6 us)
Async XLA Ops:
  7.2 82.8 %copy-start = (bf16[128,512]{1,0:T(8,128)(2,1)S(1)}, bf16[128,512]{1,0:T(8,128)(2,1)}, u32[]{:S(2)}) copy-start(bf16[128,512]{1,0:T(8,128)(2,1)} %param.14) | copy-start | bytes 393220
  7.2 82.8 %all-gather.11.cloned.1.call-start = ((), (), s32[]{:S(2)}) async-start(), calls=%async_computation.4 | async-start | bytes 2129920 | tf_op jit(solution)/shard_map/all_gather | solution.py:39
  7.9 110.3 %reduce-scatter.3.cloned.1.call-start = ((), (), s32[]{:S(2)}) async-start(), calls=%async_computation.5 | async-start | bytes 1310720 | tf_op jit(solution)/shard_map/reduce_scatter | solution.py:40
  93.3 3.3 copy-start.3
  93.4 5.8 copy-start.7
  93.4 24.9 %copy-start.2 = (bf16[128,512]{1,0:T(8,128)(2,1)S(1)}, bf16[128,512]{1,0:T(8,128)(2,1)}, u32[]{:S(2)}) copy-start(bf16[128,512]{1,0:T(8,128)(2,1)} %param.15) | copy-start | bytes 393220
  93.4 34.4 %copy-start.5 = (f32[512]{0:T(512)S(1)}, f32[512]{0:T(512)}, u32[]{:S(2)}) copy-start(f32[512]{0:T(512)} %param.17) | copy-start | bytes 6148
  93.4 110.0 %all-gather.19.cloned.1.call-start = ((), (), s32[]{:S(2)}) async-start(), calls=%async_computation.10 | async-start | bytes 7208960 | tf_op jit(solution)/shard_map/all_gather | solution.py:83
  94.1 156.8 %all-gather.21.cloned.1.call-start = ((), (), s32[]{:S(2)}) async-start(), calls=%async_computation.11 | async-start | bytes 7208960 | tf_op jit(solution)/shard_map/all_gather | solution.py:84
  94.7 222.5 %all-gather.23.cloned.1.call-start = ((), (), s32[]{:S(2)}) async-start(), calls=%async_computation.12 | async-start | bytes 7208960 | tf_op jit(solution)/shard_map/all_gather | solution.py:89
  95.3 306.1 %all-gather.13.cloned.1.call-start = ((), (), s32[]{:S(2)}) async-start(), calls=%async_computation.6 | async-start | bytes 3194880 | tf_op jit(solution)/shard_map/all_gather | solution.py:49
  95.9 384.4 %all-gather.15.cloned.1.call-start = ((), (), s32[]{:S(2)}) async-start(), calls=%async_computation.7 | async-start | bytes 3194880 | tf_op jit(solution)/shard_map/all_gather | solution.py:50
  163.8 39.4 %all-to-all-start = ((bf16[64,4,2048]{2,1,0:T(4,128)(2,1)}), bf16[64,4,2048]{2,1,0:T(4,128)(2,1)S(1)}, u32[]{:S(2)}, u32[]{:S(2)}) async-start(bf16[64,4,2048]{2,1,0:T(4,128)(2,1)} %reshape.214), calls=%async_computation.1 | async-start | bytes 2097152 | tf_op jit(solution)/shard_map/all_to_all | solution.py:74
  174.3 384.9 %all-gather.17.cloned.1.call-start = ((), (), s32[]{:S(2)}) async-start(), calls=%async_computation.8 | async-start | bytes 3194880 | tf_op jit(solution)/shard_map/all_gather | solution.py:55
  325.5 12.3 %copy-start.4 = (f32[128,6]{0,1:T(8,128)S(1)}, f32[128,6]{0,1:T(8,128)}, u32[]{:S(2)}) copy-start(f32[128,6]{0,1:T(8,128)} %param.25) | copy-start | bytes 9220
  326.8 77.8 %all-to-all-start.1 = ((bf16[64,4,2048]{2,1,0:T(4,128)(2,1)}), bf16[64,4,2048]{2,1,0:T(4,128)(2,1)S(1)}, u32[]{:S(2)}, u32[]{:S(2)}) async-start(bf16[64,4,2048]{2,1,0:T(4,128)(2,1)} %reshape.216), calls=%async_computation.2 | async-start | bytes 2097152 | tf_op jit(solution)/shard_map/all_to_all | solution.py:92
  337.3 254.0 %reduce-scatter.5.cloned.1.call-start = ((), (), s32[]{:S(2)}) async-start(), calls=%async_computation.9 | async-start | bytes 1310720 | tf_op jit(solution)/shard_map/reduce_scatter | solution.py:104
  422.3 178.6 %copy-start.6 = (f32[512]{0:T(512)S(1)}, f32[512]{0:T(512)}, u32[]{:S(2)}) copy-start(f32[512]{0:T(512)} %param.27) | copy-start | bytes 6148
  592.4 9.3 %copy-start.1 = (bf16[128,512]{1,0:T(8,128)(2,1)}, bf16[128,512]{1,0:T(8,128)(2,1)S(1)}, u32[]{:S(2)}) copy-start(bf16[128,512]{1,0:T(8,128)(2,1)S(1)} %get-tuple-element.7) | copy-start | bytes 393220
Sparse Core Ops, SparseCore 0:
  10.8 79.1 all-gather.10
  93.5 24.6 reduce-scatter.2
  120.2 64.3 all-gather.18
  186.4 64.4 all-gather.20
  252.7 64.4 all-gather.22
  320.2 81.0 all-gather.12
  404.5 75.7 all-gather.14
  483.4 75.7 all-gather.16
  566.6 24.7 reduce-scatter.4
where the time goes:
time: 609 us; the launch traced here: 608 us
  waiting for transfers between devices  467 us (77%)
  local copies, waits for them, and re-layouts  35.3 us (6%)
  blocking collectives  31.2 us (5%)
  matrix products  27.6 us (5%)
  starting transfers between devices  21.7 us (4%)
  between operations  14.1 us (2%)
  other arithmetic  11.7 us (2%)
    all_gather x1, waiting for transfers between devices, local(): lax.all_gather(out_weight, 'dp', axis=1, tiled=True)  82 us
    all_gather x1, waiting for transfers between devices, local(): lax.all_gather(shared_down, 'dp', axis=1, tiled=True)  78.9 us
    all_gather x1, waiting for transfers between devices, local(): lax.all_gather(down_local, 'mp', axis=0, tiled=True)  66.3 us
    all_gather x1, waiting for transfers between devices, local(): lax.all_gather(shared_gate, 'dp', axis=0, tiled=True)  63.4 us
    all_gather x1, waiting for transfers between devices, local(): lax.all_gather(shared_up, 'dp', axis=0, tiled=True)  58 us
    all_gather x1, waiting for transfers between devices, local(): lax.all_gather(up_local, 'mp', axis=1, tiled=True)  41.9 us
    all_to_all x1, waiting for transfers between devices, local(): lax.all_to_all(outgoing.reshape(experts, quarter, model_width), 'dp', spl...  28 us
    dot_general x5, matrix products, matmul(): return jnp.dot(left, right, preferred_element_type=jnp.float32)  27.6 us
  transfers between devices with their start and end apart: 11, of which 9 were waited for; matrix products, arithmetic and copies ran while one was open for 10% of the time, Pallas kernels for 0%

commit v1 on v0

v1 whole, which is shorter than its diff:
```python
import jax
import jax.numpy as jnp
from jax import lax
from jax.sharding import PartitionSpec as P

D = 2048


EPSILON = 1e-06


def matmul(left, right):
    return jnp.dot(left, right, preferred_element_type=jnp.float32)


def local(
    attention,
    residual,
    out_weight,
    ffn_gain,
    shared_gate,
    shared_up,
    shared_down,
    expert_gate,
    expert_up,
    expert_down,
    route_ids,
    route_scores,
    placement,
    next_gain,
):
    tok_rows = attention.shape[0]
    top_count = route_ids.shape[1]
    experts = lax.axis_size("dp")
    capacity = min(tok_rows, 8 * tok_rows // experts)
    model_width = D
    partial_value = matmul(attention, lax.all_gather(out_weight, "dp", axis=1, tiled=True))
    projected = lax.psum_scatter(partial_value, "mp", scatter_dimension=1, tiled=True)
    hidden = (residual.astype(jnp.float32) + projected).astype(jnp.bfloat16)
    hidden_float = hidden.astype(jnp.float32)
    squares = lax.psum(jnp.sum(hidden_float * hidden_float, axis=1), "mp")
    normed = (hidden_float * lax.rsqrt(squares / model_width + EPSILON)[:, None] * ffn_gain).astype(
        jnp.bfloat16
    )
    whole_rows = lax.all_gather(normed, "mp", axis=1, tiled=True)

    flat_ids = route_ids.reshape(-1)
    expert_iota = jnp.arange(experts, dtype=jnp.int32)
    one_hot = (flat_ids[:, None] == expert_iota[None, :]).astype(jnp.int32)
    target = jnp.sum(one_hot * placement[None, :], axis=1)
    slot = jnp.sum((jnp.cumsum(one_hot, axis=0) - one_hot) * one_hot, axis=1)
    dest = target * capacity + slot
    slots = experts * capacity
    hit = (dest[:, None] == jnp.arange(slots, dtype=jnp.int32)[None, :]).reshape(
        tok_rows, top_count, slots
    )
    flat_scores = route_scores.reshape(tok_rows, top_count)
    combine = jnp.sum(jnp.where(hit, flat_scores[:, :, None], 0.0), axis=1)
    pick = jnp.any(hit, axis=1).astype(jnp.bfloat16)
    outgoing = matmul(pick.T, whole_rows).astype(jnp.bfloat16)
    arrived = lax.all_to_all(
        outgoing.reshape(experts, capacity, model_width),
        "dp",
        split_axis=0,
        concat_axis=0,
        tiled=True,
    )
    in_rows = arrived.reshape(slots, model_width)
    gate_val = matmul(in_rows, expert_gate[0])
    up_val = matmul(in_rows, expert_up[0])
    activated = (jax.nn.silu(gate_val) * up_val).astype(jnp.bfloat16)
    partial_out = matmul(activated, expert_down[0]).astype(jnp.bfloat16)
    returned = lax.all_to_all(
        partial_out.reshape(experts, capacity, model_width),
        "dp",
        split_axis=0,
        concat_axis=0,
        tiled=True,
    ).reshape(slots, model_width)
    routed = jnp.dot(
        combine,
        returned.astype(jnp.float32),
        precision=lax.Precision.HIGHEST,
        preferred_element_type=jnp.float32,
    )

    pieces = (
        lax.all_gather(shared_gate, "dp", axis=0, tiled=True),
        lax.all_gather(shared_up, "dp", axis=0, tiled=True),
    )
    shared_gval = matmul(whole_rows, pieces[0])
    shared_uval = matmul(whole_rows, pieces[1])
    shared_act = (jax.nn.silu(shared_gval) * shared_uval).astype(jnp.bfloat16)
    shared_part = matmul(shared_act, lax.all_gather(shared_down, "dp", axis=1, tiled=True))
    mixture = lax.psum_scatter(routed + shared_part, "mp", scatter_dimension=1, tiled=True)
    final = (hidden_float + mixture).astype(jnp.bfloat16)
    final_float = final.astype(jnp.float32)
    final_squares = lax.psum(jnp.sum(final_float * final_float, axis=1), "mp")
    next_normed = (
        final_float * lax.rsqrt(final_squares / model_width + EPSILON)[:, None] * next_gain
    ).astype(jnp.bfloat16)
    return (final, next_normed)


def solution(mesh):
    in_specs = (
        P("dp", "mp"),
        P("dp", "mp"),
        P("mp", "dp"),
        P("mp"),
        P("dp", "mp"),
        P("dp", "mp"),
        P("mp", "dp"),
        P("dp", None, "mp"),
        P("dp", None, "mp"),
        P("dp", "mp", None),
        P("dp", None),
        P("dp", None),
        P(),
        P("mp"),
    )
    out_specs = (P("dp", "mp"), P("dp", "mp"))
    return jax.shard_map(local, mesh=mesh, in_specs=in_specs, out_specs=out_specs, check_vma=False)
```

time: 609 us -> 477 us (0.78)
  waiting for transfers between devices: 467 us -> 372 us
  local copies, waits for them, and re-layouts: 35.3 us -> 0.9 us
  matrix products: 27.6 us -> 36 us
    all_to_all x2, waiting for transfers between devices: 28 us -> 203 us  [the longest x1 104 us: local(): lax.all_to_all(outgoing.reshape(experts, capacity, model_width), 'dp', sp...]
    all_gather x3 -> x0, waiting for transfers between devices: 108 us -> none  [the longest x1 66.3 us: local(): lax.all_gather(down_local, 'mp', axis=0, tiled=True)]
    all_gather x1, waiting for transfers between devices: 78.9 us -> 0.02 us  [local(): lax.all_gather(shared_down, 'dp', axis=1, tiled=True)]
    all_gather x1, waiting for transfers between devices: 63.4 us -> 0.02 us  [local(): lax.all_gather(shared_gate, 'dp', axis=0, tiled=True)]
    scatter x1 -> x0, local copies, waits for them, and re-layouts: 20.4 us -> none  [local(): outgoing = jnp.zeros((experts * quarter, model_width), jnp.bfloat16).at[p...]
    all_gather x1, waiting for transfers between devices: 58 us -> 38.4 us  [local(): lax.all_gather(shared_up, 'dp', axis=0, tiled=True)]
    convert_element_type x1 -> x0, local copies, waits for them, and re-layouts: 6.55 us -> none  [local(): picked = returned[bounded].astype(jnp.float32) * weight[:, None]]
    reduce_sum x2, other arithmetic: 6.7 us -> 0.56 us  [the longest x1 0.41 us: local(): combine = jnp.sum(jnp.where(hit, flat_scores[:, :, None], 0.0), axis=1)]
  transfers between devices with their start and end apart: 11 -> 8, of which waited for: 9 -> 6; matrix products, arithmetic and copies ran while one was open for 10% -> 5% of each run, Pallas kernels for 0% -> 0%
where the time goes in v1:
time: 477 us; the launch traced here: 476 us
  waiting for transfers between devices  372 us (78%)
  matrix products  36 us (8%)
  blocking collectives  30.3 us (6%)
  starting transfers between devices  16.8 us (4%)
  between operations  14.3 us (3%)
  other arithmetic  5.93 us (1%)
    all_to_all x1, waiting for transfers between devices, local(): lax.all_to_all(outgoing.reshape(experts, capacity, model_width), 'dp', sp...  104 us
    all_to_all x1, waiting for transfers between devices, local(): lax.all_to_all(partial_out.reshape(experts, capacity, model_width), 'dp',...  98.6 us
    all_gather x1, waiting for transfers between devices, local(): lax.all_gather(out_weight, 'dp', axis=1, tiled=True)  82 us
    all_gather x1, waiting for transfers between devices, local(): lax.all_gather(shared_up, 'dp', axis=0, tiled=True)  38.4 us
    dot_general x6, matrix products, matmul(): return jnp.dot(left, right, preferred_element_type=jnp.float32)  32 us
    reduce_scatter x1, waiting for transfers between devices, local(): lax.psum_scatter(routed + shared_part, 'mp', scatter_dimension=1, tiled=T...  24.9 us
    reduce_scatter x1, waiting for transfers between devices, local(): lax.psum_scatter(partial_value, 'mp', scatter_dimension=1, tiled=True)  21.4 us
    all_gather x1, blocking collectives, local(): whole_rows = lax.all_gather(normed, 'mp', axis=1, tiled=True)  13.2 us
  transfers between devices with their start and end apart: 8, of which 6 were waited for; matrix products, arithmetic and copies ran while one was open for 5% of the time, Pallas kernels for 0%

profile of v1, /device:TPU:8, one launch (start us, length us, event | category | flops | bytes accessed | tf_op | source)
XLA Modules:
  0.0 476.1 jit_solution(9288351023330188056)
XLA Ops:
  7.2 0.0 copy-start
  7.2 0.0 all-gather.5.cloned.1.call-start
  7.3 0.7 all-gather.5.cloned.1.call-update
  8.0 0.0 reduce-scatter.3.cloned.1.call-start
  8.0 82.0 %all-gather.5.cloned.1.call-done = bf16[512,2048]{0,1:T(8,128)(2,1)} async-done(((bf16[512,32]{0,1:T(8,128)(2,1)}), bf16[512,2048]{0,1:T(8,128)(2,1)}) %all-gather.5.cloned.1.call-update) | async-done | bytes 2097168 | tf_op jit(solution)/shard_map/all_gather | solution.py:37
  90.0 3.5 fusion.32
  93.5 0.0 reduce-scatter.3.cloned.1.call-update
  93.5 0.1 copy.21
  93.6 0.1 eq.43
  93.8 0.1 eq.39
  93.9 1.8 reduce-window.6
  95.7 0.3 slice_reduce_fusion
  96.1 0.1 select_reduce_fusion.1
  96.2 0.1 add.43
  96.4 0.1 copy.24
  96.4 0.5 fusion
  96.9 21.4 %reduce-scatter.3.cloned.1.call-done = f32[128,512]{1,0:T(8,128)} async-done(((f32[128,2048]{1,0:T(8,128)}), f32[128,512]{1,0:T(8,128)}) %reduce-scatter.3.cloned.1.call-update) | async-done | bytes 262160 | tf_op jit(solution)/shard_map/reduce_scatter | solution.py:38
  118.4 1.1 fusion.20
  119.5 8.5 %psum.14 = f32[128]{0:T(128)S(1)} all-reduce(f32[128]{0:T(128)S(1)} %get-tuple-element.6), channel_id=1, replica_groups=mesh['dp'=64,'mp'=4] {'mp'}, use_global_device_ids=true, to_apply=%region_8.9 | all-reduce | flops 128 | bytes 1024 | tf_op jit(solution)/shard_map/psum | solution.py:41
  128.0 0.1 fusion.22
  128.1 13.2 %all_gather.16 = bf16[128,2048]{1,0:T(8,128)(2,1)S(1)} all-gather(bf16[128,512]{1,0:T(8,128)(2,1)S(1)} %fusion.22), channel_id=1, replica_groups=mesh['dp'=64,'mp'=4] {'mp'}, dimensions={1}, use_global_device_ids=true | all-gather | bytes 655360 | tf_op jit(solution)/shard_map/all_gather | solution.py:45
  141.3 3.2 convolution_convert_fusion.1
  144.6 10.6 %all-to-all-start = ((bf16[64,16,2048]{2,1,0:T(8,128)(2,1)}), bf16[64,16,2048]{2,1,0:T(8,128)(2,1)}, u32[]{:S(2)}, u32[]{:S(2)}) async-start(bf16[64,16,2048]{2,1,0:T(8,128)(2,1)} %bitcast.50), calls=%async_computation.1 | async-start | bytes 8388608 | tf_op jit(solution)/shard_map/all_to_all | solution.py:61
  155.2 0.0 all-gather.7.cloned.1.call-start
  155.2 0.7 all-gather.7.cloned.1.call-update
  155.9 0.0 all-gather.11.cloned.1.call-start
  156.0 0.5 all-gather.11.cloned.1.call-update
  156.5 104.0 %all-to-all-done = bf16[64,16,2048]{2,1,0:T(8,128)(2,1)} async-done(((bf16[64,16,2048]{2,1,0:T(8,128)(2,1)}), bf16[64,16,2048]{2,1,0:T(8,128)(2,1)}, u32[]{:S(2)}, u32[]{:S(2)}) %all-to-all-start) | async-done | bytes 4194336 | tf_op jit(solution)/shard_map/all_to_all | solution.py:61
  260.5 5.1 %fusion.3 = f32[1024,352]{0,1:T(8,128)} fusion(bf16[1024,2048]{1,0:T(8,128)(2,1)} %bitcast.2, bf16[1,2048,352]{1,2,0:T(8,128)(2,1)S(1)} %copy-done.10), kind=kOutput, calls=%fused_computation.9 | convolution fusion | flops 1476395008 | bytes 7077888 | tf_op jit(solution)/shard_map/dot_general | solution.py:13
  265.6 8.9 %convolution_convert_fusion = bf16[1024,2048]{1,0:T(8,128)(2,1)} fusion(bf16[1,352,2048]{2,1,0:T(8,128)(2,1)S(1)} %copy-done, bf16[1024,2048]{1,0:T(8,128)(2,1)} %bitcast.2, bf16[1,2048,352]{1,2,0:T(8,128)(2,1)} %param.22, f32[1024,352]{0,1:T(8,128)} %fusion.3), kind=kOutput, calls=%fused_computation | convolution fusion | flops 2957049856 | bytes 12713984 | tf_op jit(solution)/shard_map/dot_general | solution.py:13
  274.6 5.8 %all-to-all-start.1 = ((bf16[64,16,2048]{2,1,0:T(8,128)(2,1)}), bf16[64,16,2048]{2,1,0:T(8,128)(2,1)}, u32[]{:S(2)}, u32[]{:S(2)}) async-start(bf16[64,16,2048]{2,1,0:T(8,128)(2,1)} %bitcast.51), calls=%async_computation.2 | async-start | bytes 8388608 | tf_op jit(solution)/shard_map/all_to_all | solution.py:73
  280.4 0.0 all-gather.9.cloned.1.call-start
  280.4 0.5 all-gather.9.cloned.1.call-update
  281.0 0.2 reduce-scatter.5.cloned.1.call-start
  281.2 0.4 select_reduce_fusion
  281.6 0.0 all-gather.7.cloned.1.call-done
  281.7 3.9 fusion.34
  285.6 98.6 %all-to-all-done.1 = bf16[64,16,2048]{2,1,0:T(8,128)(2,1)} async-done(((bf16[64,16,2048]{2,1,0:T(8,128)(2,1)}), bf16[64,16,2048]{2,1,0:T(8,128)(2,1)}, u32[]{:S(2)}, u32[]{:S(2)}) %all-to-all-start.1) | async-done | bytes 4194336 | tf_op jit(solution)/shard_map/all_to_all | solution.py:73
  384.2 4.0 fusion.33
  388.2 0.0 copy-start.2
  388.3 0.0 all-gather.11.cloned.1.call-done
  388.3 38.4 %all-gather.9.cloned.1.call-done = bf16[2048,704]{1,0:T(8,128)(2,1)} async-done(((bf16[32,704]{1,0:T(8,128)(2,1)}), bf16[2048,704]{1,0:T(8,128)(2,1)}) %all-gather.9.cloned.1.call-update) | async-done | bytes 2883600 | tf_op jit(solution)/shard_map/all_gather | solution.py:89
  426.7 7.3 %convolution_add_fusion = f32[128,2048]{1,0:T(8,128)} fusion(f32[128,2048]{1,0:T(8,128)S(1)} %fusion.33, bf16[704,2048]{0,1:T(8,128)(2,1)} %all-gather.11.cloned.1.call-done, bf16[128,2048]{1,0:T(8,128)(2,1)S(1)} %all_gather.16, bf16[2048,704]{1,0:T(8,128)(2,1)} %all-gather.9.cloned.1.call-done, f32[128,704]{0,1:T(8,128)} %fusion.34), kind=kOutput, calls=%fused_computation.5 | convolution fusion | flops 739000320 | bytes 8749056 | tf_op jit(solution)/shard_map/dot_general | solution.py:13
  434.0 0.0 reduce-scatter.5.cloned.1.call-update
  434.0 24.9 %reduce-scatter.5.cloned.1.call-done = f32[128,512]{1,0:T(8,128)} async-done(((f32[128,2048]{1,0:T(8,128)}), f32[128,512]{1,0:T(8,128)}) %reduce-scatter.5.cloned.1.call-update) | async-done | bytes 262160 | tf_op jit(solution)/shard_map/reduce_scatter | solution.py:95
  458.9 1.1 fusion.17
  460.0 8.5 %psum.15 = f32[128]{0:T(128)S(1)} all-reduce(f32[128]{0:T(128)S(1)} %get-tuple-element.4), channel_id=1, replica_groups=mesh['dp'=64,'mp'=4] {'mp'}, use_global_device_ids=true, to_apply=%region_11.12 | all-reduce | flops 128 | bytes 1024 | tf_op jit(solution)/shard_map/psum | solution.py:98
  468.5 0.8 fusion.19
  (25 shorter events, 0.1 us)
Async XLA Ops:
  7.2 258.5 %copy-start = (bf16[1,352,2048]{2,1,0:T(8,128)(2,1)S(1)}, bf16[1,352,2048]{2,1,0:T(8,128)(2,1)}, u32[]{:S(2)}) copy-start(bf16[1,352,2048]{2,1,0:T(8,128)(2,1)} %param.23) | copy-start | bytes 4325380
  7.2 86.3 %copy-start.6 = (s32[128,6]{0,1:T(8,128)S(1)}, s32[128,6]{0,1:T(8,128)}, u32[]{:S(2)}) copy-start(s32[128,6]{0,1:T(8,128)} %param.24) | copy-start | bytes 9220
  7.2 88.9 %copy-start.9 = (s32[64]{0:T(128)S(1)}, s32[64]{0:T(128)}, u32[]{:S(2)}) copy-start(s32[64]{0:T(128)} %param.26) | copy-start | bytes 772
  7.2 111.2 %copy-start.4 = (bf16[128,512]{1,0:T(8,128)(2,1)S(1)}, bf16[128,512]{1,0:T(8,128)(2,1)}, u32[]{:S(2)}) copy-start(bf16[128,512]{1,0:T(8,128)(2,1)} %param.15) | copy-start | bytes 393220
  7.2 82.8 %all-gather.5.cloned.1.call-start = ((), (), s32[]{:S(2)}) async-start(), calls=%async_computation.4 | async-start | bytes 2129920 | tf_op jit(solution)/shard_map/all_gather | solution.py:37
  7.9 120.1 %copy-start.7 = (f32[512]{0:T(512)S(1)}, f32[512]{0:T(512)}, u32[]{:S(2)}) copy-start(f32[512]{0:T(512)} %param.17) | copy-start | bytes 6148
  8.0 110.4 %reduce-scatter.3.cloned.1.call-start = ((), (), s32[]{:S(2)}) async-start(), calls=%async_computation.5 | async-start | bytes 1310720 | tf_op jit(solution)/shard_map/reduce_scatter | solution.py:38
  119.5 8.6 %copy-start.1 = (bf16[128,512]{1,0:T(8,128)(2,1)}, bf16[128,512]{1,0:T(8,128)(2,1)S(1)}, u32[]{:S(2)}) copy-start(bf16[128,512]{1,0:T(8,128)(2,1)S(1)} %get-tuple-element.7) | copy-start | bytes 393220
  144.6 116.0 %copy-start.10 = (bf16[1,2048,352]{1,2,0:T(8,128)(2,1)S(1)}, bf16[1,2048,352]{1,2,0:T(8,128)(2,1)}, u32[]{:S(2)}) copy-start(bf16[1,2048,352]{1,2,0:T(8,128)(2,1)} %param.21) | copy-start | bytes 4325380
  144.6 116.0 %all-to-all-start = ((bf16[64,16,2048]{2,1,0:T(8,128)(2,1)}), bf16[64,16,2048]{2,1,0:T(8,128)(2,1)}, u32[]{:S(2)}, u32[]{:S(2)}) async-start(bf16[64,16,2048]{2,1,0:T(8,128)(2,1)} %bitcast.50), calls=%async_computation.1 | async-start | bytes 8388608 | tf_op jit(solution)/shard_map/all_to_all | solution.py:61
  155.2 126.5 %all-gather.7.cloned.1.call-start = ((), (), s32[]{:S(2)}) async-start(), calls=%async_computation.6 | async-start | bytes 3194880 | tf_op jit(solution)/shard_map/all_gather | solution.py:88
  155.9 232.4 %all-gather.11.cloned.1.call-start = ((), (), s32[]{:S(2)}) async-start(), calls=%async_computation.8 | async-start | bytes 3194880 | tf_op jit(solution)/shard_map/all_gather | solution.py:94
  274.6 6.6 %copy-start.5 = (f32[128,6]{0,1:T(8,128)S(1)}, f32[128,6]{0,1:T(8,128)}, u32[]{:S(2)}) copy-start(f32[128,6]{0,1:T(8,128)} %param.25) | copy-start | bytes 9220
  274.6 109.6 %all-to-all-start.1 = ((bf16[64,16,2048]{2,1,0:T(8,128)(2,1)}), bf16[64,16,2048]{2,1,0:T(8,128)(2,1)}, u32[]{:S(2)}, u32[]{:S(2)}) async-start(bf16[64,16,2048]{2,1,0:T(8,128)(2,1)} %bitcast.51), calls=%async_computation.2 | async-start | bytes 8388608 | tf_op jit(solution)/shard_map/all_to_all | solution.py:73
  280.4 146.3 %all-gather.9.cloned.1.call-start = ((), (), s32[]{:S(2)}) async-start(), calls=%async_computation.7 | async-start | bytes 3194880 | tf_op jit(solution)/shard_map/all_gather | solution.py:89
  281.0 177.9 %reduce-scatter.5.cloned.1.call-start = ((), (), s32[]{:S(2)}) async-start(), calls=%async_computation.9 | async-start | bytes 1310720 | tf_op jit(solution)/shard_map/reduce_scatter | solution.py:95
  388.2 70.7 %copy-start.2 = (bf16[128,512]{1,0:T(8,128)(2,1)S(1)}, bf16[128,512]{1,0:T(8,128)(2,1)}, u32[]{:S(2)}) copy-start(bf16[128,512]{1,0:T(8,128)(2,1)} %copy-done.1) | copy-start | bytes 393220
  388.2 80.3 %copy-start.8 = (f32[512]{0:T(512)S(1)}, f32[512]{0:T(512)}, u32[]{:S(2)}) copy-start(f32[512]{0:T(512)} %param.27) | copy-start | bytes 6148
  460.0 9.3 %copy-start.3 = (bf16[128,512]{1,0:T(8,128)(2,1)}, bf16[128,512]{1,0:T(8,128)(2,1)S(1)}, u32[]{:S(2)}) copy-start(bf16[128,512]{1,0:T(8,128)(2,1)S(1)} %get-tuple-element.5) | copy-start | bytes 393220
Sparse Core Ops, SparseCore 0:
  10.8 79.1 all-gather.4
  93.6 24.6 reduce-scatter.2
  159.2 92.0 all-gather.6
  254.3 88.4 all-gather.10
  345.8 80.8 all-gather.8
  434.2 24.7 reduce-scatter.4

commit v2 on v1

--- a/solution.py
+++ b/solution.py
@@ -11,6 +11,12 @@
 
 def matmul(left, right):
     return jnp.dot(left, right, preferred_element_type=jnp.float32)
+
+
+def matmul_t(left, right_t):
+    return lax.dot_general(
+        left, right_t, (((1,), (1,)), ((), ())), preferred_element_type=jnp.float32
+    )
 
 
 def local(
@@ -31,18 +37,23 @@
 ):
     tok_rows = attention.shape[0]
     top_count = route_ids.shape[1]
+    mp_count = lax.axis_size("mp")
     experts = lax.axis_size("dp")
     capacity = min(tok_rows, 8 * tok_rows // experts)
+    quarter = capacity // mp_count
     model_width = D
-    partial_value = matmul(attention, lax.all_gather(out_weight, "dp", axis=1, tiled=True))
+    block_width = model_width // mp_count
+    out_weight_t = lax.all_gather(out_weight.T, "dp", axis=0, tiled=True)
+    partial_value = matmul_t(attention, out_weight_t)
     projected = lax.psum_scatter(partial_value, "mp", scatter_dimension=1, tiled=True)
     hidden = (residual.astype(jnp.float32) + projected).astype(jnp.bfloat16)
     hidden_float = hidden.astype(jnp.float32)
-    squares = lax.psum(jnp.sum(hidden_float * hidden_float, axis=1), "mp")
-    normed = (hidden_float * lax.rsqrt(squares / model_width + EPSILON)[:, None] * ffn_gain).astype(
-        jnp.bfloat16
-    )
-    whole_rows = lax.all_gather(normed, "mp", axis=1, tiled=True)
+    whole_hidden = lax.all_gather(hidden, "mp", axis=1, tiled=True).astype(jnp.float32)
+    squares = jnp.sum(whole_hidden * whole_hidden, axis=1)
+    gain = lax.all_gather(ffn_gain, "mp", axis=0, tiled=True)
+    whole_rows = (
+        whole_hidden * lax.rsqrt(squares / model_width + EPSILON)[:, None] * gain
+    ).astype(jnp.bfloat16)
 
     flat_ids = route_ids.reshape(-1)
     expert_iota = jnp.arange(experts, dtype=jnp.int32)
@@ -57,26 +68,29 @@
     flat_scores = route_scores.reshape(tok_rows, top_count)
     combine = jnp.sum(jnp.where(hit, flat_scores[:, :, None], 0.0), axis=1)
     pick = jnp.any(hit, axis=1).astype(jnp.bfloat16)
-    outgoing = matmul(pick.T, whole_rows).astype(jnp.bfloat16)
+    mine = pick.reshape(tok_rows, experts, mp_count, quarter)[:, :, lax.axis_index("mp"), :]
+    outgoing = matmul(mine.reshape(tok_rows, experts * quarter).T, whole_rows).astype(jnp.bfloat16)
     arrived = lax.all_to_all(
-        outgoing.reshape(experts, capacity, model_width),
+        outgoing.reshape(experts, quarter, model_width),
         "dp",
         split_axis=0,
         concat_axis=0,
         tiled=True,
     )
-    in_rows = arrived.reshape(slots, model_width)
+    copies = jnp.broadcast_to(arrived[None], (mp_count, experts, quarter, model_width))
+    in_rows = lax.all_to_all(copies, "mp", split_axis=0, concat_axis=0, tiled=True)
+    in_rows = in_rows.reshape(mp_count * experts * quarter, model_width)
     gate_val = matmul(in_rows, expert_gate[0])
     up_val = matmul(in_rows, expert_up[0])
     activated = (jax.nn.silu(gate_val) * up_val).astype(jnp.bfloat16)
     partial_out = matmul(activated, expert_down[0]).astype(jnp.bfloat16)
+    by_block = partial_out.reshape(mp_count, experts, quarter, mp_count, block_width)
+    by_block = jnp.transpose(by_block, (3, 1, 0, 2, 4))
+    summed = lax.all_to_all(by_block, "mp", split_axis=0, concat_axis=0, tiled=True)
+    expert_out = jnp.sum(summed.astype(jnp.float32), axis=0).astype(jnp.bfloat16)
     returned = lax.all_to_all(
-        partial_out.reshape(experts, capacity, model_width),
-        "dp",
-        split_axis=0,
-        concat_axis=0,
-        tiled=True,
-    ).reshape(slots, model_width)
+        expert_out, "dp", split_axis=0, concat_axis=0, tiled=True
+    ).reshape(slots, block_width)
     routed = jnp.dot(
         combine,
         returned.astype(jnp.float32),
@@ -91,8 +105,9 @@
     shared_gval = matmul(whole_rows, pieces[0])
     shared_uval = matmul(whole_rows, pieces[1])
     shared_act = (jax.nn.silu(shared_gval) * shared_uval).astype(jnp.bfloat16)
-    shared_part = matmul(shared_act, lax.all_gather(shared_down, "dp", axis=1, tiled=True))
-    mixture = lax.psum_scatter(routed + shared_part, "mp", scatter_dimension=1, tiled=True)
+    shared_down_t = lax.all_gather(shared_down.T, "dp", axis=0, tiled=True)
+    shared_part = matmul_t(shared_act, shared_down_t)
+    mixture = lax.psum_scatter(shared_part, "mp", scatter_dimension=1, tiled=True) + routed
     final = (hidden_float + mixture).astype(jnp.bfloat16)
     final_float = final.astype(jnp.float32)
     final_squares = lax.psum(jnp.sum(final_float * final_float, axis=1), "mp")

time: 477 us -> 430 us (0.901)
  waiting for transfers between devices: 372 us -> 252 us
  blocking collectives: 30.3 us -> 74 us
  local copies, waits for them, and re-layouts: 0.9 us -> 29.9 us
  matrix products: 36 us -> 30.6 us
    all_to_all x2 -> x3, waiting for transfers between devices: 203 us -> 75.4 us  [the longest x1 47.8 us: local(): lax.all_to_all(copies, 'mp', split_axis=0, concat_axis=0, tiled=True)]
    all_gather x2, waiting for transfers between devices: 82 us -> 161 us  [the longest x1 82 us: local(): out_weight_t = lax.all_gather(out_weight.T, 'dp', axis=0, tiled=True)]
    all_to_all x0 -> x1, blocking collectives: none -> 39.8 us  [local(): lax.all_to_all(outgoing.reshape(experts, quarter, model_width), 'dp', spl...]
    all_gather x1, waiting for transfers between devices: 38.4 us -> 4.17 us  [local(): lax.all_gather(shared_up, 'dp', axis=0, tiled=True)]
    reduce_scatter x1, waiting for transfers between devices: 24.9 us -> 0.02 us  [local(): lax.psum_scatter(shared_part, 'mp', scatter_dimension=1, tiled=True)]
    reshape x0 -> x5, local copies, waits for them, and re-layouts: none -> 22.4 us  [the longest x2 14 us: local(): partial_out.reshape(mp_count, experts, quarter, mp_count, block_width)]
    dot_general x6 -> x4, matrix products: 32 us -> 18.1 us  [matmul(): return jnp.dot(left, right, preferred_element_type=jnp.float32)]
    reduce_scatter x1, waiting for transfers between devices: 21.4 us -> 8.84 us  [local(): lax.psum_scatter(partial_value, 'mp', scatter_dimension=1, tiled=True)]
  transfers between devices with their start and end apart: 8 -> 9, of which waited for: 6 -> 6; matrix products, arithmetic and copies ran while one was open for 5% -> 15% of each run, Pallas kernels for 0% -> 0%
where the time goes in v2:
time: 430 us; the launch traced here: 429 us
  waiting for transfers between devices  252 us (59%)
  blocking collectives  74 us (17%)
  matrix products  30.6 us (7%)
  local copies, waits for them, and re-layouts  29.9 us (7%)
  starting transfers between devices  18.4 us (4%)
  between operations  14.4 us (3%)
  other arithmetic  10.5 us (2%)
    all_gather x1, waiting for transfers between devices, local(): out_weight_t = lax.all_gather(out_weight.T, 'dp', axis=0, tiled=True)  82 us
    all_gather x1, waiting for transfers between devices, local(): shared_down_t = lax.all_gather(shared_down.T, 'dp', axis=0, tiled=True)  78.8 us
    all_to_all x1, waiting for transfers between devices, local(): lax.all_to_all(copies, 'mp', split_axis=0, concat_axis=0, tiled=True)  47.8 us
    all_to_all x1, blocking collectives, local(): lax.all_to_all(outgoing.reshape(experts, quarter, model_width), 'dp', spl...  39.8 us
    all_to_all x1, waiting for transfers between devices, local(): lax.all_to_all(expert_out, 'dp', split_axis=0, concat_axis=0, tiled=True)  27.5 us
    dot_general x4, matrix products, matmul(): return jnp.dot(left, right, preferred_element_type=jnp.float32)  18.1 us
    reshape x2, local copies, waits for them, and re-layouts, local(): partial_out.reshape(mp_count, experts, quarter, mp_count, block_width)  14 us
    all_gather x1, blocking collectives, local(): lax.all_gather(hidden, 'mp', axis=1, tiled=True).astype(jnp.float32)  12.8 us
  transfers between devices with their start and end apart: 9, of which 6 were waited for; matrix products, arithmetic and copies ran while one was open for 15% of the time, Pallas kernels for 0%

profile of v2, /device:TPU:8, one launch (start us, length us, event | category | flops | bytes accessed | tf_op | source)
XLA Modules:
  0.0 429.3 jit_solution(12252464773864155934)
XLA Ops:
  7.3 0.7 all-gather.6.cloned.1.call-update
  8.0 82.0 %all-gather.6.cloned.1.call-done = bf16[2048,512]{1,0:T(8,128)(2,1)} async-done(((bf16[32,512]{1,0:T(8,128)(2,1)}), bf16[2048,512]{1,0:T(8,128)(2,1)}) %all-gather.6.cloned.1.call-update) | async-done | bytes 2097168 | tf_op jit(solution)/shard_map/all_gather | solution.py:46
  90.0 3.5 fusion.38
  93.6 0.7 all-gather.8.cloned.1.call-update
  94.3 0.5 all-gather.10.cloned.1.call-update
  94.8 0.1 copy.41
  95.0 0.1 eq.43
  95.1 0.1 eq.39
  95.3 1.8 reduce-window.6
  97.1 0.3 slice_reduce_fusion
  97.4 0.1 select_reduce_fusion.1
  97.5 0.1 add.50
  97.7 0.5 fusion
  98.2 0.3 copy.45
  98.5 11.0 %all-gather = f32[4,1,512]{2,1,0:T(1,128)S(1)} all-gather(f32[1,1,512]{2,1,0:T(1,128)S(1)} %bitcast.61), channel_id=1, replica_groups=mesh['dp'=64,'mp'=4] {'mp'}, dimensions={0}, use_global_device_ids=true | all-gather | bytes 10240 | tf_op jit(solution)/shard_map/all_gather | solution.py:53
  109.6 8.8 %reduce-scatter.3.cloned.1.call-done = f32[128,512]{1,0:T(8,128)} async-done(((f32[128,2048]{1,0:T(8,128)}), f32[128,512]{1,0:T(8,128)}) %reduce-scatter.3.cloned.1.call-update) | async-done | bytes 262160 | tf_op jit(solution)/shard_map/reduce_scatter | solution.py:48
  118.4 1.0 add_convert_fusion
  119.4 0.6 copy-done.1
  120.1 12.8 %all_gather.19 = bf16[128,2048]{1,0:T(8,128)(2,1)S(1)} all-gather(bf16[128,512]{1,0:T(8,128)(2,1)S(1)} %add_convert_fusion), channel_id=1, replica_groups=mesh['dp'=64,'mp'=4] {'mp'}, dimensions={1}, use_global_device_ids=true | all-gather | bytes 655360 | tf_op jit(solution)/shard_map/all_gather | solution.py:51
  132.9 0.2 fusion.12
  133.0 0.5 convolution_convert_fusion.1
  133.6 1.2 reshape.69
  134.8 39.8 %all_to_all.20 = bf16[64,4,2048]{2,1,0:T(4,128)(2,1)S(1)} all-to-all(bf16[64,4,2048]{2,1,0:T(4,128)(2,1)} %reshape.69), channel_id=1, replica_groups=mesh['dp'=64,'mp'=4] {'dp'}, dimensions={0} | all-to-all | bytes 2097152 | tf_op jit(solution)/shard_map/all_to_all | solution.py:73
  174.6 4.1 broadcast_in_dim.16
  178.7 4.9 %all-to-all-start.1 = ((bf16[4,64,4,2048]{3,2,1,0:T(4,128)(2,1)}), bf16[4,64,4,2048]{3,2,1,0:T(4,128)(2,1)}, u32[]{:S(2)}, u32[]{:S(2)}) async-start(bf16[4,64,4,2048]{3,2,1,0:T(4,128)(2,1)} %broadcast_in_dim.16), calls=%async_computation.3 | async-start | bytes 8388608 | tf_op jit(solution)/shard_map/all_to_all | solution.py:81
  183.5 0.2 all-gather.12.cloned.1.call-start
  183.8 0.4 all-gather.12.cloned.1.call-update
  184.1 47.8 %all-to-all-done.1 = bf16[4,64,4,2048]{3,2,1,0:T(4,128)(2,1)} async-done(((bf16[4,64,4,2048]{3,2,1,0:T(4,128)(2,1)}), bf16[4,64,4,2048]{3,2,1,0:T(4,128)(2,1)}, u32[]{:S(2)}, u32[]{:S(2)}) %all-to-all-start.1) | async-done | bytes 4194336 | tf_op jit(solution)/shard_map/all_to_all | solution.py:81
  232.0 6.9 %reshape.70 = bf16[1024,2048]{1,0:T(8,128)(2,1)} reshape(bf16[4,64,4,2048]{3,2,1,0:T(4,128)(2,1)} %all-to-all-done.1) | data formatting | bytes 8388608 | tf_op jit(solution)/shard_map/reshape | solution.py:82
  238.9 5.4 %fusion.3 = f32[1024,352]{0,1:T(8,128)} fusion(bf16[1024,2048]{1,0:T(8,128)(2,1)} %reshape.70, bf16[1,2048,352]{1,2,0:T(8,128)(2,1)} %param.21), kind=kOutput, calls=%fused_computation.9 | convolution fusion | flops 1476395008 | bytes 7077888 | tf_op jit(solution)/shard_map/dot_general | solution.py:13
  244.3 8.9 %convolution_convert_fusion = bf16[1024,2048]{1,0:T(8,128)(2,1)} fusion(bf16[1,352,2048]{2,1,0:T(8,128)(2,1)S(1)} %copy-done, bf16[1024,2048]{1,0:T(8,128)(2,1)} %reshape.70, bf16[1,2048,352]{1,2,0:T(8,128)(2,1)} %param.22, f32[1024,352]{0,1:T(8,128)} %fusion.3), kind=kOutput, calls=%fused_computation.1 | convolution fusion | flops 2957049856 | bytes 12713984 | tf_op jit(solution)/shard_map/dot_general | solution.py:13
  253.2 7.9 %reshape.71 = bf16[4,64,4,4,512]{4,3,2,1,0:T(4,128)(2,1)} reshape(bf16[1024,2048]{1,0:T(8,128)(2,1)} %convolution_convert_fusion) | data formatting | bytes 8388608 | tf_op jit(solution)/shard_map/reshape | solution.py:87
  261.1 6.2 %copy.53 = bf16[4,64,4,4,512]{4,2,1,0,3:T(4,128)(2,1)} copy(bf16[4,64,4,4,512]{4,3,2,1,0:T(4,128)(2,1)} %reshape.71) | data formatting | bytes 8388608 | tf_op jit(solution)/shard_map/reshape | solution.py:87
  267.3 4.9 %all-to-all-start.2 = ((bf16[4,64,4,4,512]{4,3,1,2,0:T(4,128)(2,1)}), bf16[4,64,4,4,512]{4,3,1,2,0:T(4,128)(2,1)}, u32[]{:S(2)}, u32[]{:S(2)}) async-start(bf16[4,64,4,4,512]{4,3,1,2,0:T(4,128)(2,1)} %bitcast.52), calls=%async_computation.4 | async-start | bytes 8388608 | tf_op jit(solution)/shard_map/all_to_all | solution.py:89
  272.1 0.3 reduce-scatter.5.cloned.1.call-start
  272.4 3.2 fusion.36
  275.7 4.2 all-gather.10.cloned.1.call-done
  279.8 78.8 %all-gather.12.cloned.1.call-done = bf16[2048,704]{1,0:T(8,128)(2,1)} async-done(((bf16[32,704]{1,0:T(8,128)(2,1)}), bf16[2048,704]{1,0:T(8,128)(2,1)}) %all-gather.12.cloned.1.call-update) | async-done | bytes 2883600 | tf_op jit(solution)/shard_map/all_gather | solution.py:108
  358.6 7.2 %fusion.11 = f32[128,2048]{1,0:T(8,128)} fusion(bf16[2048,704]{1,0:T(8,128)(2,1)} %all-gather.12.cloned.1.call-done, bf16[2048,704]{1,0:T(8,128)(2,1)} %all-gather.10.cloned.1.call-done, f32[128,704]{0,1:T(8,128)S(1)} %fusion.36, bf16[128,2048]{1,0:T(8,128)(2,1)S(1)} %all_gather.19, f32[2048]{0:T(1024)S(1)} %bitcast.56, f32[128]{0:T(128)S(1)} %add_rsqrt_fusion.1), kind=kOutput, calls=%fused_computation.19 | convolution fusion | flops 739786752 | bytes 7709184 | tf_op jit(solution)/shard_map/dot_general | solution.py:17
  365.9 4.8 %reduce_sum.61 = bf16[64,4,4,512]{3,2,0,1:T(4,128)(2,1)S(1)} reduce(bf16[4,64,4,4,512]{4,3,1,2,0:T(4,128)(2,1)} %all-to-all-done.2, bf16[]{:T(256)} %constant.31.clone.1), dimensions={0}, to_apply=%region_9.10 | reduce | flops 1572864 | bytes 5242882 | tf_op jit(solution)/shard_map/reduce_sum | solution.py:90
  370.7 1.6 copy.48
  372.3 8.0 %all-to-all-start.3 = ((bf16[64,4,4,512]{3,2,1,0:T(4,128)(2,1)}), bf16[64,4,4,512]{3,2,1,0:T(4,128)(2,1)S(1)}, u32[]{:S(2)}, u32[]{:S(2)}) async-start(bf16[64,4,4,512]{3,2,1,0:T(4,128)(2,1)} %copy.48), calls=%async_computation.5 | async-start | bytes 2097152 | tf_op jit(solution)/shard_map/all_to_all | solution.py:91
  380.4 1.2 select_reduce_fusion
  381.6 27.5 %all-to-all-done.3 = bf16[64,4,4,512]{3,2,1,0:T(4,128)(2,1)S(1)} async-done(((bf16[64,4,4,512]{3,2,1,0:T(4,128)(2,1)}), bf16[64,4,4,512]{3,2,1,0:T(4,128)(2,1)S(1)}, u32[]{:S(2)}, u32[]{:S(2)}) %all-to-all-start.3) | async-done | bytes 1048608 | tf_op jit(solution)/shard_map/all_to_all | solution.py:91
  409.1 0.3 reshape.72
  409.4 1.8 fusion.23
  411.3 10.4 %psum.7 = f32[128]{0:T(128)S(1)} all-reduce(f32[128]{0:T(128)S(1)} %get-tuple-element.4), channel_id=1, replica_groups=mesh['dp'=64,'mp'=4] {'mp'}, use_global_device_ids=true, to_apply=%region_11.12 | all-reduce | flops 128 | bytes 1024 | tf_op jit(solution)/shard_map/psum | solution.py:113
  421.7 0.8 fusion.25
  (33 shorter events, 0.4 us)
Async XLA Ops:
  7.2 237.1 %copy-start = (bf16[1,352,2048]{2,1,0:T(8,128)(2,1)S(1)}, bf16[1,352,2048]{2,1,0:T(8,128)(2,1)}, u32[]{:S(2)}) copy-start(bf16[1,352,2048]{2,1,0:T(8,128)(2,1)} %param.23) | copy-start | bytes 4325380
  7.2 87.7 %copy-start.5 = (s32[128,6]{0,1:T(8,128)S(1)}, s32[128,6]{0,1:T(8,128)}, u32[]{:S(2)}) copy-start(s32[128,6]{0,1:T(8,128)} %param.24) | copy-start | bytes 9220
  7.2 90.2 %copy-start.8 = (s32[64]{0:T(128)S(1)}, s32[64]{0:T(128)}, u32[]{:S(2)}) copy-start(s32[64]{0:T(128)} %param.26) | copy-start | bytes 772
  7.2 91.3 %copy-start.7 = (f32[512]{0:T(512)S(1)}, f32[512]{0:T(512)}, u32[]{:S(2)}) copy-start(f32[512]{0:T(512)} %param.17) | copy-start | bytes 6148
  7.2 82.8 %all-gather.6.cloned.1.call-start = ((), (), s32[]{:S(2)}) async-start(), calls=%async_computation.6 | async-start | bytes 2129920 | tf_op jit(solution)/shard_map/all_gather | solution.py:46
  7.9 110.5 %copy-start.3 = (bf16[128,512]{1,0:T(8,128)(2,1)S(1)}, bf16[128,512]{1,0:T(8,128)(2,1)}, u32[]{:S(2)}) copy-start(bf16[128,512]{1,0:T(8,128)(2,1)} %param.15) | copy-start | bytes 393220
  8.0 110.5 %reduce-scatter.3.cloned.1.call-start = ((), (), s32[]{:S(2)}) async-start(), calls=%async_computation.7 | async-start | bytes 1310720 | tf_op jit(solution)/shard_map/reduce_scatter | solution.py:48
  93.5 178.9 %all-gather.8.cloned.1.call-start = ((), (), s32[]{:S(2)}) async-start(), calls=%async_computation.8 | async-start | bytes 3194880 | tf_op jit(solution)/shard_map/all_gather | solution.py:102
  94.3 185.6 %all-gather.10.cloned.1.call-start = ((), (), s32[]{:S(2)}) async-start(), calls=%async_computation.9 | async-start | bytes 3194880 | tf_op jit(solution)/shard_map/all_gather | solution.py:103
  119.4 0.7 copy-start.1
  178.7 53.3 %all-to-all-start.1 = ((bf16[4,64,4,2048]{3,2,1,0:T(4,128)(2,1)}), bf16[4,64,4,2048]{3,2,1,0:T(4,128)(2,1)}, u32[]{:S(2)}, u32[]{:S(2)}) async-start(bf16[4,64,4,2048]{3,2,1,0:T(4,128)(2,1)} %broadcast_in_dim.16), calls=%async_computation.3 | async-start | bytes 8388608 | tf_op jit(solution)/shard_map/all_to_all | solution.py:81
  183.5 175.1 %all-gather.12.cloned.1.call-start = ((), (), s32[]{:S(2)}) async-start(), calls=%async_computation.10 | async-start | bytes 3194880 | tf_op jit(solution)/shard_map/all_gather | solution.py:108
  267.3 98.6 %all-to-all-start.2 = ((bf16[4,64,4,4,512]{4,3,1,2,0:T(4,128)(2,1)}), bf16[4,64,4,4,512]{4,3,1,2,0:T(4,128)(2,1)}, u32[]{:S(2)}, u32[]{:S(2)}) async-start(bf16[4,64,4,4,512]{4,3,1,2,0:T(4,128)(2,1)} %bitcast.52), calls=%async_computation.4 | async-start | bytes 8388608 | tf_op jit(solution)/shard_map/all_to_all | solution.py:89
  272.1 137.3 %reduce-scatter.5.cloned.1.call-start = ((), (), s32[]{:S(2)}) async-start(), calls=%async_computation.11 | async-start | bytes 1310720 | tf_op jit(solution)/shard_map/reduce_scatter | solution.py:110
  370.7 9.6 %copy-start.4 = (f32[128,6]{0,1:T(8,128)S(1)}, f32[128,6]{0,1:T(8,128)}, u32[]{:S(2)}) copy-start(f32[128,6]{0,1:T(8,128)} %param.25) | copy-start | bytes 9220
  372.3 49.4 %copy-start.6 = (f32[512]{0:T(512)S(1)}, f32[512]{0:T(512)}, u32[]{:S(2)}) copy-start(f32[512]{0:T(512)} %param.27) | copy-start | bytes 6148
  372.3 36.9 %all-to-all-start.3 = ((bf16[64,4,4,512]{3,2,1,0:T(4,128)(2,1)}), bf16[64,4,4,512]{3,2,1,0:T(4,128)(2,1)S(1)}, u32[]{:S(2)}, u32[]{:S(2)}) async-start(bf16[64,4,4,512]{3,2,1,0:T(4,128)(2,1)} %copy.48), calls=%async_computation.5 | async-start | bytes 2097152 | tf_op jit(solution)/shard_map/all_to_all | solution.py:91
  411.3 11.2 %copy-start.2 = (bf16[128,512]{1,0:T(8,128)(2,1)}, bf16[128,512]{1,0:T(8,128)(2,1)S(1)}, u32[]{:S(2)}) copy-start(bf16[128,512]{1,0:T(8,128)(2,1)S(1)} %get-tuple-element.5) | copy-start | bytes 393220
Sparse Core Ops, SparseCore 0:
  10.8 79.1 all-gather.5
  93.6 24.7 reduce-scatter.2
  121.6 79.4 all-gather.7
  204.0 75.7 all-gather.9
  282.8 75.7 all-gather.11
  366.0 24.7 reduce-scatter.4

commit v3 on v2

--- a/solution.py
+++ b/solution.py
@@ -1,7 +1,13 @@
+import functools
+
 import jax
 import jax.numpy as jnp
 from jax import lax
+from jax.experimental import pallas as pl
+from jax.experimental.pallas import tpu as pltpu
 from jax.sharding import PartitionSpec as P
+
+MESH = pl.DeviceIdType.MESH
 
 D = 2048
 
@@ -17,6 +23,60 @@
     return lax.dot_general(
         left, right_t, (((1,), (1,)), ((), ())), preferred_element_type=jnp.float32
     )
+
+
+def _gather_kernel(n, x_ref, o_ref, send_sem, recv_sem):
+    me = lax.axis_index("dp")
+    col = lax.axis_index("mp")
+    rows = x_ref.shape[0]
+    barrier = pltpu.get_barrier_semaphore()
+
+    def greet(p, carry):
+        peer = lax.rem(me + p, n)
+        pl.semaphore_signal(barrier, inc=1, device_id=(peer, col), device_id_type=MESH)
+        return carry
+
+    lax.fori_loop(1, n, greet, 0)
+    pl.semaphore_wait(barrier, n - 1)
+    own = o_ref.at[pl.ds(me * rows, rows)]
+    pltpu.make_async_copy(x_ref, own, recv_sem).start()
+
+    def send(p, carry):
+        peer = lax.rem(me + p, n)
+        pltpu.make_async_remote_copy(
+            src_ref=x_ref,
+            dst_ref=own,
+            send_sem=send_sem,
+            recv_sem=recv_sem,
+            device_id=(peer, col),
+            device_id_type=MESH,
+        ).start()
+        return carry
+
+    lax.fori_loop(1, n, send, 0)
+    sent = o_ref.at[pl.ds(0, (n - 1) * rows)]
+    pltpu.make_async_copy(sent, sent, send_sem).wait()
+    pltpu.make_async_copy(o_ref, o_ref, recv_sem).wait()
+
+
+def gather_dp(x, collective_id):
+    n = lax.axis_size("dp")
+    rows, cols = x.shape
+    return pl.pallas_call(
+        functools.partial(_gather_kernel, n),
+        out_shape=jax.ShapeDtypeStruct((n * rows, cols), x.dtype),
+        in_specs=[pl.BlockSpec(memory_space=pl.ANY)],
+        out_specs=pl.BlockSpec(memory_space=pl.ANY),
+        scratch_shapes=[pltpu.SemaphoreType.DMA(()), pltpu.SemaphoreType.DMA(())],
+        compiler_params=pltpu.CompilerParams(collective_id=collective_id, has_side_effects=True),
+    )(x)
+
+
+def reduce_scatter_mp(value):
+    mp_count = lax.axis_size("mp")
+    rows, width = value.shape
+    blocks = jnp.transpose(value.reshape(rows, mp_count, width // mp_count), (1, 0, 2))
+    return jnp.sum(lax.all_to_all(blocks, "mp", split_axis=0, concat_axis=0, tiled=True), axis=0)
 
 
 def local(
@@ -43,9 +103,9 @@
     quarter = capacity // mp_count
     model_width = D
     block_width = model_width // mp_count
-    out_weight_t = lax.all_gather(out_weight.T, "dp", axis=0, tiled=True)
+    out_weight_t = gather_dp(out_weight.T, 0)
     partial_value = matmul_t(attention, out_weight_t)
-    projected = lax.psum_scatter(partial_value, "mp", scatter_dimension=1, tiled=True)
+    projected = reduce_scatter_mp(partial_value)
     hidden = (residual.astype(jnp.float32) + projected).astype(jnp.bfloat16)
     hidden_float = hidden.astype(jnp.float32)
     whole_hidden = lax.all_gather(hidden, "mp", axis=1, tiled=True).astype(jnp.float32)
@@ -107,7 +167,7 @@
     shared_act = (jax.nn.silu(shared_gval) * shared_uval).astype(jnp.bfloat16)
     shared_down_t = lax.all_gather(shared_down.T, "dp", axis=0, tiled=True)
     shared_part = matmul_t(shared_act, shared_down_t)
-    mixture = lax.psum_scatter(shared_part, "mp", scatter_dimension=1, tiled=True) + routed
+    mixture = reduce_scatter_mp(shared_part) + routed
     final = (hidden_float + mixture).astype(jnp.bfloat16)
     final_float = final.astype(jnp.float32)
     final_squares = lax.psum(jnp.sum(final_float * final_float, axis=1), "mp")

time: 430 us -> 372 us (0.87)
  waiting for transfers between devices: 252 us -> 120 us
  Pallas kernels: 0 us -> 58.4 us
  starting transfers between devices: 18.4 us -> 27.4 us
  blocking collectives: 74 us -> 80 us
    all_gather x1 -> x0, waiting for transfers between devices: 82 us -> none  [local(): out_weight_t = lax.all_gather(out_weight.T, 'dp', axis=0, tiled=True)]
    all_gather x1, waiting for transfers between devices: 78.8 us -> 11.3 us  [local(): shared_down_t = lax.all_gather(shared_down.T, 'dp', axis=0, tiled=True)]
    pallas_call x0 -> x1, Pallas kernels: none -> 58.4 us  [gather_dp(): pl.pallas_call(functools.partial(_gather_kernel, n), out_shape=jax.ShapeD...]
    all_to_all x1, waiting for transfers between devices: 0.01 us -> 25.6 us  [local(): lax.all_to_all(by_block, 'mp', split_axis=0, concat_axis=0, tiled=True)]
    reduce_scatter x2 -> x0, waiting for transfers between devices: 8.86 us -> none  [the longest x1 8.84 us: local(): lax.psum_scatter(partial_value, 'mp', scatter_dimension=1, tiled=True)]
    all_to_all x0 -> x2, starting transfers between devices: none -> 8.15 us  [reduce_scatter_mp(): lax.all_to_all(blocks, 'mp', split_axis=0, concat_axis=0, tiled=True)]
    all_to_all x0 -> x2, waiting for transfers between devices: none -> 6.26 us  [reduce_scatter_mp(): lax.all_to_all(blocks, 'mp', split_axis=0, concat_axis=0, tiled=True)]
    all_gather x1, blocking collectives: 11 us -> 15.9 us  [local(): gain = lax.all_gather(ffn_gain, 'mp', axis=0, tiled=True)]
  transfers between devices with their start and end apart: 9 -> 8, of which waited for: 6 -> 5; matrix products, arithmetic and copies ran while one was open for 15% -> 18% of each run, Pallas kernels for 0% -> 16%
where the time goes in v3:
time: 372 us; the launch traced here: 371 us
  waiting for transfers between devices  120 us (32%)
  blocking collectives  80 us (22%)
  Pallas kernels  58.4 us (16%)
  local copies, waits for them, and re-layouts  32.1 us (9%)
  matrix products  28.7 us (8%)
  starting transfers between devices  27.4 us (7%)
  between operations  14 us (4%)
  other arithmetic  10.4 us (3%)
    pallas_call x1, Pallas kernels, gather_dp(): pl.pallas_call(functools.partial(_gather_kernel, n), out_shape=jax.ShapeD...  58.4 us
    all_to_all x1, waiting for transfers between devices, local(): lax.all_to_all(copies, 'mp', split_axis=0, concat_axis=0, tiled=True)  47.8 us
    all_to_all x1, blocking collectives, local(): lax.all_to_all(outgoing.reshape(experts, quarter, model_width), 'dp', spl...  42.3 us
    all_to_all x1, waiting for transfers between devices, local(): lax.all_to_all(expert_out, 'dp', split_axis=0, concat_axis=0, tiled=True)  26.8 us
    all_to_all x1, waiting for transfers between devices, local(): lax.all_to_all(by_block, 'mp', split_axis=0, concat_axis=0, tiled=True)  25.6 us
    dot_general x4, matrix products, matmul(): return jnp.dot(left, right, preferred_element_type=jnp.float32)  18.1 us
    all_gather x1, blocking collectives, local(): gain = lax.all_gather(ffn_gain, 'mp', axis=0, tiled=True)  15.9 us
    reshape x2, local copies, waits for them, and re-layouts, local(): partial_out.reshape(mp_count, experts, quarter, mp_count, block_width)  14 us
  transfers between devices with their start and end apart: 8, of which 5 were waited for; matrix products, arithmetic and copies ran while one was open for 18% of the time, Pallas kernels for 16%

profile of v3, /device:TPU:8, one launch (start us, length us, event | category | flops | bytes accessed | tf_op | source)
XLA Modules:
  0.0 370.7 jit_solution(18232724362432621349)
XLA Ops:
  7.2 0.7 all-gather.5.cloned.1.call-update
  8.0 0.7 all-gather.7.cloned.1.call-update
  8.7 58.4 %shard_map.149 = bf16[2048,512]{1,0:T(8,128)(2,1)} custom-call(bf16[32,512]{1,0:T(8,128)(2,1)} %bitcast.76), custom_call_target="tpu_custom_call" | custom-call | tf_op jit(solution)/shard_map/pallas_call | solution.py:65
  67.1 2.5 fusion.38
  69.6 1.1 copy.67
  70.7 4.4 %all-to-all-start = ((f32[4,128,512]{2,1,0:T(8,128)}), f32[4,128,512]{2,1,0:T(8,128)S(1)}, u32[]{:S(2)}, u32[]{:S(2)}) async-start(f32[4,128,512]{2,1,0:T(8,128)} %bitcast.64), calls=%async_computation | async-start | bytes 2097152 | tf_op jit(solution)/shard_map/all_to_all | solution.py:79
  75.3 0.1 eq.43
  75.4 0.1 eq.39
  75.6 1.8 reduce-window.6
  77.4 0.3 slice_reduce_fusion
  77.7 0.1 select_reduce_fusion.1
  78.0 0.5 fusion
  78.5 0.3 copy.53
  78.8 15.9 %all-gather = f32[4,1,512]{2,1,0:T(1,128)S(1)} all-gather(f32[1,1,512]{2,1,0:T(1,128)S(1)} %bitcast.78), channel_id=1, replica_groups=mesh['dp'=64,'mp'=4] {'mp'}, dimensions={0}, use_global_device_ids=true | all-gather | bytes 10240 | tf_op jit(solution)/shard_map/all_gather | solution.py:113
  94.9 0.6 copy-done.1
  95.5 12.9 %all_gather.15 = bf16[128,2048]{1,0:T(8,128)(2,1)S(1)} all-gather(bf16[128,512]{1,0:T(8,128)(2,1)S(1)} %add_convert_fusion), channel_id=1, replica_groups=mesh['dp'=64,'mp'=4] {'mp'}, dimensions={1}, use_global_device_ids=true | all-gather | bytes 655360 | tf_op jit(solution)/shard_map/all_gather | solution.py:111
  108.4 0.2 fusion.12
  108.6 0.5 convolution_convert_fusion.1
  109.2 1.2 reshape.77
  110.4 42.3 %all_to_all.30 = bf16[64,4,2048]{2,1,0:T(4,128)(2,1)S(1)} all-to-all(bf16[64,4,2048]{2,1,0:T(4,128)(2,1)} %reshape.77), channel_id=1, replica_groups=mesh['dp'=64,'mp'=4] {'dp'}, dimensions={0} | all-to-all | bytes 2097152 | tf_op jit(solution)/shard_map/all_to_all | solution.py:133
  152.7 4.1 %broadcast_in_dim.16 = bf16[4,64,4,2048]{3,2,1,0:T(4,128)(2,1)} broadcast(bf16[64,4,2048]{2,1,0:T(4,128)(2,1)S(1)} %all_to_all.30), dimensions={1,2,3} | broadcast | bytes 5242880 | tf_op jit(solution)/shard_map/broadcast_in_dim | solution.py:140
  156.8 4.9 %all-to-all-start.3 = ((bf16[4,64,4,2048]{3,2,1,0:T(4,128)(2,1)}), bf16[4,64,4,2048]{3,2,1,0:T(4,128)(2,1)}, u32[]{:S(2)}, u32[]{:S(2)}) async-start(bf16[4,64,4,2048]{3,2,1,0:T(4,128)(2,1)} %broadcast_in_dim.16), calls=%async_computation.3 | async-start | bytes 8388608 | tf_op jit(solution)/shard_map/all_to_all | solution.py:141
  161.7 0.2 all-gather.9.cloned.1.call-start
  161.9 0.5 all-gather.9.cloned.1.call-update
  162.4 47.8 %all-to-all-done.3 = bf16[4,64,4,2048]{3,2,1,0:T(4,128)(2,1)} async-done(((bf16[4,64,4,2048]{3,2,1,0:T(4,128)(2,1)}), bf16[4,64,4,2048]{3,2,1,0:T(4,128)(2,1)}, u32[]{:S(2)}, u32[]{:S(2)}) %all-to-all-start.3) | async-done | bytes 4194336 | tf_op jit(solution)/shard_map/all_to_all | solution.py:141
  210.2 6.9 %reshape.78 = bf16[1024,2048]{1,0:T(8,128)(2,1)} reshape(bf16[4,64,4,2048]{3,2,1,0:T(4,128)(2,1)} %all-to-all-done.3) | data formatting | bytes 8388608 | tf_op jit(solution)/shard_map/reshape | solution.py:142
  217.1 5.4 %fusion.3 = f32[1024,352]{0,1:T(8,128)} fusion(bf16[1024,2048]{1,0:T(8,128)(2,1)} %reshape.78, bf16[1,2048,352]{1,2,0:T(8,128)(2,1)} %param.21), kind=kOutput, calls=%fused_computation.9 | convolution fusion | flops 1476395008 | bytes 7077888 | tf_op jit(solution)/shard_map/dot_general | solution.py:19
  222.6 8.9 %convolution_convert_fusion = bf16[1024,2048]{1,0:T(8,128)(2,1)} fusion(bf16[1,352,2048]{2,1,0:T(8,128)(2,1)S(1)} %copy-done, bf16[1024,2048]{1,0:T(8,128)(2,1)} %reshape.78, bf16[1,2048,352]{1,2,0:T(8,128)(2,1)} %param.22, f32[1024,352]{0,1:T(8,128)} %fusion.3), kind=kOutput, calls=%fused_computation.1 | convolution fusion | flops 2957049856 | bytes 12713984 | tf_op jit(solution)/shard_map/dot_general | solution.py:19
  231.5 7.8 %reshape.79 = bf16[4,64,4,4,512]{4,3,2,1,0:T(4,128)(2,1)} reshape(bf16[1024,2048]{1,0:T(8,128)(2,1)} %convolution_convert_fusion) | data formatting | bytes 8388608 | tf_op jit(solution)/shard_map/reshape | solution.py:147
  239.3 6.1 %copy.65 = bf16[4,64,4,4,512]{4,2,1,0,3:T(4,128)(2,1)} copy(bf16[4,64,4,4,512]{4,3,2,1,0:T(4,128)(2,1)} %reshape.79) | data formatting | bytes 8388608 | tf_op jit(solution)/shard_map/reshape | solution.py:147
  245.5 4.8 %all-to-all-start.4 = ((bf16[4,64,4,4,512]{4,3,1,2,0:T(4,128)(2,1)}), bf16[4,64,4,4,512]{4,3,1,2,0:T(4,128)(2,1)}, u32[]{:S(2)}, u32[]{:S(2)}) async-start(bf16[4,64,4,4,512]{4,3,1,2,0:T(4,128)(2,1)} %bitcast.66), calls=%async_computation.4 | async-start | bytes 8388608 | tf_op jit(solution)/shard_map/all_to_all | solution.py:149
  250.3 3.2 fusion.36
  253.6 11.3 %all-gather.9.cloned.1.call-done = bf16[2048,704]{1,0:T(8,128)(2,1)} async-done(((bf16[32,704]{1,0:T(8,128)(2,1)}), bf16[2048,704]{1,0:T(8,128)(2,1)}) %all-gather.9.cloned.1.call-update) | async-done | bytes 2883600 | tf_op jit(solution)/shard_map/all_gather | solution.py:168
  264.9 6.2 %fusion.11 = f32[128,2048]{1,0:T(8,128)S(1)} fusion(bf16[2048,704]{1,0:T(8,128)(2,1)} %all-gather.9.cloned.1.call-done, bf16[2048,704]{1,0:T(8,128)(2,1)} %all-gather.7.cloned.1.call-done, f32[128,704]{0,1:T(8,128)S(1)} %fusion.36, bf16[128,2048]{1,0:T(8,128)(2,1)S(1)} %all_gather.15, f32[2048]{0:T(1024)S(1)} %bitcast.73, f32[128]{0:T(128)S(1)} %add_rsqrt_fusion.1), kind=kOutput, calls=%fused_computation.19 | convolution fusion | flops 739786752 | bytes 7709184 | tf_op jit(solution)/shard_map/dot_general | solution.py:23
  271.1 1.2 copy.66
  272.3 25.6 %all-to-all-done.4 = bf16[4,64,4,4,512]{4,3,1,2,0:T(4,128)(2,1)} async-done(((bf16[4,64,4,4,512]{4,3,1,2,0:T(4,128)(2,1)}), bf16[4,64,4,4,512]{4,3,1,2,0:T(4,128)(2,1)}, u32[]{:S(2)}, u32[]{:S(2)}) %all-to-all-start.4) | async-done | bytes 4194336 | tf_op jit(solution)/shard_map/all_to_all | solution.py:149
  297.9 3.7 %all-to-all-start.1 = ((f32[4,128,512]{2,1,0:T(8,128)}), f32[4,128,512]{2,1,0:T(8,128)S(1)}, u32[]{:S(2)}, u32[]{:S(2)}) async-start(f32[4,128,512]{2,1,0:T(8,128)} %bitcast.69), calls=%async_computation.1 | async-start | bytes 2097152 | tf_op jit(solution)/shard_map/all_to_all | solution.py:79
  301.7 4.8 %reduce_sum.81 = bf16[64,4,4,512]{3,2,0,1:T(4,128)(2,1)S(1)} reduce(bf16[4,64,4,4,512]{4,3,1,2,0:T(4,128)(2,1)} %all-to-all-done.4, bf16[]{:T(256)} %constant.31.clone.1), dimensions={0}, to_apply=%region_9.10 | reduce | flops 1572864 | bytes 5242882 | tf_op jit(solution)/shard_map/reduce_sum | solution.py:150
  306.5 1.6 copy.56
  308.1 6.3 %all-to-all-done.1 = f32[4,128,512]{2,1,0:T(8,128)S(1)} async-done(((f32[4,128,512]{2,1,0:T(8,128)}), f32[4,128,512]{2,1,0:T(8,128)S(1)}, u32[]{:S(2)}, u32[]{:S(2)}) %all-to-all-start.1) | async-done | bytes 1048608 | tf_op jit(solution)/shard_map/all_to_all | solution.py:79
  314.3 9.3 %all-to-all-start.5 = ((bf16[64,4,4,512]{3,2,1,0:T(4,128)(2,1)}), bf16[64,4,4,512]{3,2,1,0:T(4,128)(2,1)S(1)}, u32[]{:S(2)}, u32[]{:S(2)}) async-start(bf16[64,4,4,512]{3,2,1,0:T(4,128)(2,1)} %copy.56), calls=%async_computation.5 | async-start | bytes 2097152 | tf_op jit(solution)/shard_map/all_to_all | solution.py:151
  323.6 1.2 select_reduce_fusion
  324.9 0.8 reduce_sum.77
  325.7 26.8 %all-to-all-done.5 = bf16[64,4,4,512]{3,2,1,0:T(4,128)(2,1)S(1)} async-done(((bf16[64,4,4,512]{3,2,1,0:T(4,128)(2,1)}), bf16[64,4,4,512]{3,2,1,0:T(4,128)(2,1)S(1)}, u32[]{:S(2)}, u32[]{:S(2)}) %all-to-all-start.5) | async-done | bytes 1048608 | tf_op jit(solution)/shard_map/all_to_all | solution.py:151
  352.4 0.3 reshape.80
  352.7 1.8 fusion.23
  354.5 8.9 %psum.7 = f32[128]{0:T(128)S(1)} all-reduce(f32[128]{0:T(128)S(1)} %get-tuple-element.4), channel_id=1, replica_groups=mesh['dp'=64,'mp'=4] {'mp'}, use_global_device_ids=true, to_apply=%region_11.12 | all-reduce | flops 128 | bytes 1024 | tf_op jit(solution)/shard_map/psum | solution.py:173
  363.5 0.8 fusion.25
  (33 shorter events, 0.7 us)
Async XLA Ops:
  7.2 215.4 %copy-start = (bf16[1,352,2048]{2,1,0:T(8,128)(2,1)S(1)}, bf16[1,352,2048]{2,1,0:T(8,128)(2,1)}, u32[]{:S(2)}) copy-start(bf16[1,352,2048]{2,1,0:T(8,128)(2,1)} %param.23) | copy-start | bytes 4325380
  7.2 243.2 %all-gather.5.cloned.1.call-start = ((), (), s32[]{:S(2)}) async-start(), calls=%async_computation.6 | async-start | bytes 3194880 | tf_op jit(solution)/shard_map/all_gather | solution.py:162
  7.9 245.7 %all-gather.7.cloned.1.call-start = ((), (), s32[]{:S(2)}) async-start(), calls=%async_computation.7 | async-start | bytes 3194880 | tf_op jit(solution)/shard_map/all_gather | solution.py:163
  67.1 8.0 %copy-start.5 = (s32[128,6]{0,1:T(8,128)S(1)}, s32[128,6]{0,1:T(8,128)}, u32[]{:S(2)}) copy-start(s32[128,6]{0,1:T(8,128)} %param.24) | copy-start | bytes 9220
  69.6 8.1 %copy-start.8 = (s32[64]{0:T(128)S(1)}, s32[64]{0:T(128)}, u32[]{:S(2)}) copy-start(s32[64]{0:T(128)} %param.26) | copy-start | bytes 772
  69.6 9.2 %copy-start.7 = (f32[512]{0:T(512)S(1)}, f32[512]{0:T(512)}, u32[]{:S(2)}) copy-start(f32[512]{0:T(512)} %param.17) | copy-start | bytes 6148
  70.7 24.1 %copy-start.3 = (bf16[128,512]{1,0:T(8,128)(2,1)S(1)}, bf16[128,512]{1,0:T(8,128)(2,1)}, u32[]{:S(2)}) copy-start(bf16[128,512]{1,0:T(8,128)(2,1)} %param.15) | copy-start | bytes 393220
  70.7 24.0 %all-to-all-start = ((f32[4,128,512]{2,1,0:T(8,128)}), f32[4,128,512]{2,1,0:T(8,128)S(1)}, u32[]{:S(2)}, u32[]{:S(2)}) async-start(f32[4,128,512]{2,1,0:T(8,128)} %bitcast.64), calls=%async_computation | async-start | bytes 2097152 | tf_op jit(solution)/shard_map/all_to_all | solution.py:79
  94.9 0.7 copy-start.1
  156.8 53.4 %all-to-all-start.3 = ((bf16[4,64,4,2048]{3,2,1,0:T(4,128)(2,1)}), bf16[4,64,4,2048]{3,2,1,0:T(4,128)(2,1)}, u32[]{:S(2)}, u32[]{:S(2)}) async-start(bf16[4,64,4,2048]{3,2,1,0:T(4,128)(2,1)} %broadcast_in_dim.16), calls=%async_computation.3 | async-start | bytes 8388608 | tf_op jit(solution)/shard_map/all_to_all | solution.py:141
  161.7 103.2 %all-gather.9.cloned.1.call-start = ((), (), s32[]{:S(2)}) async-start(), calls=%async_computation.8 | async-start | bytes 3194880 | tf_op jit(solution)/shard_map/all_gather | solution.py:168
  245.5 52.5 %all-to-all-start.4 = ((bf16[4,64,4,4,512]{4,3,1,2,0:T(4,128)(2,1)}), bf16[4,64,4,4,512]{4,3,1,2,0:T(4,128)(2,1)}, u32[]{:S(2)}, u32[]{:S(2)}) async-start(bf16[4,64,4,4,512]{4,3,1,2,0:T(4,128)(2,1)} %bitcast.66), calls=%async_computation.4 | async-start | bytes 8388608 | tf_op jit(solution)/shard_map/all_to_all | solution.py:149
  297.9 16.4 %all-to-all-start.1 = ((f32[4,128,512]{2,1,0:T(8,128)}), f32[4,128,512]{2,1,0:T(8,128)S(1)}, u32[]{:S(2)}, u32[]{:S(2)}) async-start(f32[4,128,512]{2,1,0:T(8,128)} %bitcast.69), calls=%async_computation.1 | async-start | bytes 2097152 | tf_op jit(solution)/shard_map/all_to_all | solution.py:79
  306.5 17.1 %copy-start.4 = (f32[128,6]{0,1:T(8,128)S(1)}, f32[128,6]{0,1:T(8,128)}, u32[]{:S(2)}) copy-start(f32[128,6]{0,1:T(8,128)} %param.25) | copy-start | bytes 9220
  314.3 38.1 %all-to-all-start.5 = ((bf16[64,4,4,512]{3,2,1,0:T(4,128)(2,1)}), bf16[64,4,4,512]{3,2,1,0:T(4,128)(2,1)S(1)}, u32[]{:S(2)}, u32[]{:S(2)}) async-start(bf16[64,4,4,512]{3,2,1,0:T(4,128)(2,1)} %copy.56), calls=%async_computation.5 | async-start | bytes 2097152 | tf_op jit(solution)/shard_map/all_to_all | solution.py:151
  323.6 39.8 %copy-start.6 = (f32[512]{0:T(512)S(1)}, f32[512]{0:T(512)}, u32[]{:S(2)}) copy-start(f32[512]{0:T(512)} %param.27) | copy-start | bytes 6148
  354.5 9.7 %copy-start.2 = (bf16[128,512]{1,0:T(8,128)(2,1)}, bf16[128,512]{1,0:T(8,128)(2,1)S(1)}, u32[]{:S(2)}) copy-start(bf16[128,512]{1,0:T(8,128)(2,1)S(1)} %get-tuple-element.5) | copy-start | bytes 393220
Sparse Core Ops, SparseCore 0:
  10.8 94.1 all-gather.4
  107.8 78.6 all-gather.6
  189.2 75.6 all-gather.8

commit v4 on v3

--- a/solution.py
+++ b/solution.py
@@ -72,10 +72,7 @@
     )(x)
 
 
-def reduce_scatter_mp(value):
-    mp_count = lax.axis_size("mp")
-    rows, width = value.shape
-    blocks = jnp.transpose(value.reshape(rows, mp_count, width // mp_count), (1, 0, 2))
+def reduce_scatter_mp(blocks):
     return jnp.sum(lax.all_to_all(blocks, "mp", split_axis=0, concat_axis=0, tiled=True), axis=0)
 
 
@@ -100,20 +97,29 @@
     mp_count = lax.axis_size("mp")
     experts = lax.axis_size("dp")
     capacity = min(tok_rows, 8 * tok_rows // experts)
-    quarter = capacity // mp_count
     model_width = D
     block_width = model_width // mp_count
-    out_weight_t = gather_dp(out_weight.T, 0)
-    partial_value = matmul_t(attention, out_weight_t)
-    projected = reduce_scatter_mp(partial_value)
+    out_weight_t = gather_dp(out_weight.T, 0).reshape(mp_count, block_width, -1)
+    partial_value = jnp.einsum(
+        "tk,qfk->qtf", attention, out_weight_t, preferred_element_type=jnp.float32
+    )
+    gain_row = jnp.broadcast_to(ffn_gain[None, None, :], (mp_count, 1, block_width))
+    exchanged = lax.all_to_all(
+        jnp.concatenate([partial_value, gain_row], axis=1),
+        "mp",
+        split_axis=0,
+        concat_axis=0,
+        tiled=True,
+    )
+    projected = jnp.sum(exchanged[:, :tok_rows, :], axis=0)
+    gain = exchanged[:, tok_rows, :].reshape(model_width)
     hidden = (residual.astype(jnp.float32) + projected).astype(jnp.bfloat16)
     hidden_float = hidden.astype(jnp.float32)
     whole_hidden = lax.all_gather(hidden, "mp", axis=1, tiled=True).astype(jnp.float32)
     squares = jnp.sum(whole_hidden * whole_hidden, axis=1)
-    gain = lax.all_gather(ffn_gain, "mp", axis=0, tiled=True)
-    whole_rows = (
-        whole_hidden * lax.rsqrt(squares / model_width + EPSILON)[:, None] * gain
-    ).astype(jnp.bfloat16)
+    scale = lax.rsqrt(squares / model_width + EPSILON)[:, None]
+    whole_rows = (whole_hidden * scale * gain).astype(jnp.bfloat16)
+    normed = (hidden_float * scale * ffn_gain).astype(jnp.bfloat16)
 
     flat_ids = route_ids.reshape(-1)
     expert_iota = jnp.arange(experts, dtype=jnp.int32)
@@ -128,28 +134,33 @@
     flat_scores = route_scores.reshape(tok_rows, top_count)
     combine = jnp.sum(jnp.where(hit, flat_scores[:, :, None], 0.0), axis=1)
     pick = jnp.any(hit, axis=1).astype(jnp.bfloat16)
-    mine = pick.reshape(tok_rows, experts, mp_count, quarter)[:, :, lax.axis_index("mp"), :]
-    outgoing = matmul(mine.reshape(tok_rows, experts * quarter).T, whole_rows).astype(jnp.bfloat16)
+    outgoing = matmul(pick.T, normed).astype(jnp.bfloat16)
     arrived = lax.all_to_all(
-        outgoing.reshape(experts, quarter, model_width),
+        outgoing.reshape(experts, capacity, block_width),
         "dp",
         split_axis=0,
         concat_axis=0,
         tiled=True,
-    )
-    copies = jnp.broadcast_to(arrived[None], (mp_count, experts, quarter, model_width))
+    ).reshape(slots, block_width)
+    copies = jnp.broadcast_to(arrived[None], (mp_count, slots, block_width))
     in_rows = lax.all_to_all(copies, "mp", split_axis=0, concat_axis=0, tiled=True)
-    in_rows = in_rows.reshape(mp_count * experts * quarter, model_width)
-    gate_val = matmul(in_rows, expert_gate[0])
-    up_val = matmul(in_rows, expert_up[0])
+    gate_block = expert_gate[0].reshape(mp_count, block_width, -1)
+    up_block = expert_up[0].reshape(mp_count, block_width, -1)
+    gate_val = jnp.einsum("qsf,qfh->sh", in_rows, gate_block, preferred_element_type=jnp.float32)
+    up_val = jnp.einsum("qsf,qfh->sh", in_rows, up_block, preferred_element_type=jnp.float32)
     activated = (jax.nn.silu(gate_val) * up_val).astype(jnp.bfloat16)
-    partial_out = matmul(activated, expert_down[0]).astype(jnp.bfloat16)
-    by_block = partial_out.reshape(mp_count, experts, quarter, mp_count, block_width)
-    by_block = jnp.transpose(by_block, (3, 1, 0, 2, 4))
-    summed = lax.all_to_all(by_block, "mp", split_axis=0, concat_axis=0, tiled=True)
+    down_block = expert_down[0].reshape(-1, mp_count, block_width)
+    partial_out = jnp.einsum(
+        "sh,hqf->qsf", activated, down_block, preferred_element_type=jnp.float32
+    ).astype(jnp.bfloat16)
+    summed = lax.all_to_all(partial_out, "mp", split_axis=0, concat_axis=0, tiled=True)
     expert_out = jnp.sum(summed.astype(jnp.float32), axis=0).astype(jnp.bfloat16)
     returned = lax.all_to_all(
-        expert_out, "dp", split_axis=0, concat_axis=0, tiled=True
+        expert_out.reshape(experts, capacity, block_width),
+        "dp",
+        split_axis=0,
+        concat_axis=0,
+        tiled=True,
     ).reshape(slots, block_width)
     routed = jnp.dot(
         combine,
@@ -166,7 +177,12 @@
     shared_uval = matmul(whole_rows, pieces[1])
     shared_act = (jax.nn.silu(shared_gval) * shared_uval).astype(jnp.bfloat16)
     shared_down_t = lax.all_gather(shared_down.T, "dp", axis=0, tiled=True)
-    shared_part = matmul_t(shared_act, shared_down_t)
+    shared_part = jnp.einsum(
+        "th,qfh->qtf",
+        shared_act,
+        shared_down_t.reshape(mp_count, block_width, -1),
+        preferred_element_type=jnp.float32,
+    )
     mixture = reduce_scatter_mp(shared_part) + routed
     final = (hidden_float + mixture).astype(jnp.bfloat16)
     final_float = final.astype(jnp.float32)

time: 372 us -> 345 us (0.927)
  local copies, waits for them, and re-layouts: 32.1 us -> 16.3 us
  blocking collectives: 80 us -> 64.8 us
  waiting for transfers between devices: 120 us -> 125 us
    all_gather x1, waiting for transfers between devices: 0.02 us -> 37.2 us  [local(): lax.all_gather(shared_up, 'dp', axis=0, tiled=True)]
    reshape x7 -> x0, local copies, waits for them, and re-layouts: 24.6 us -> none  [the longest x2 14 us: local(): partial_out.reshape(mp_count, experts, quarter, mp_count, block_width)]
    all_gather x1 -> x0, blocking collectives: 15.9 us -> none  [local(): gain = lax.all_gather(ffn_gain, 'mp', axis=0, tiled=True)]
    dot_general x2 -> x4, matrix products: 8.72 us -> 24.4 us  [the longest x1 9.4 us: local(): jnp.einsum('sh,hqf->qsf', activated, down_block, preferred_element_type=j...]
    dot_general x4 -> x2, matrix products: 18.1 us -> 3.75 us  [matmul(): return jnp.dot(left, right, preferred_element_type=jnp.float32)]
    all_to_all x1, waiting for transfers between devices: 47.8 us -> 34.1 us  [local(): lax.all_to_all(copies, 'mp', split_axis=0, concat_axis=0, tiled=True)]
    another operation x0 -> x3, local copies, waits for them, and re-layouts: none -> 13.2 us  [the longest x1 4.4 us: local(): up_block = expert_up[0].reshape(mp_count, block_width, -1)]
    all_to_all x2 -> x3, waiting for transfers between devices: 52.4 us -> 40.7 us  [the longest x1 28.3 us: local(): lax.all_to_all(expert_out.reshape(experts, capacity, block_width), 'dp',...]
  transfers between devices with their start and end apart: 8 -> 8, of which waited for: 5 -> 5; matrix products, arithmetic and copies ran while one was open for 18% -> 15% of each run, Pallas kernels for 16% -> 17%
where the time goes in v4:
time: 345 us; the launch traced here: 344 us
  waiting for transfers between devices  125 us (36%)
  blocking collectives  64.8 us (19%)
  Pallas kernels  58.4 us (17%)
  matrix products  28.9 us (8%)
  starting transfers between devices  27 us (8%)
  local copies, waits for them, and re-layouts  16.3 us (5%)
  between operations  14 us (4%)
  other arithmetic  9.39 us (3%)
    pallas_call x1, Pallas kernels, gather_dp(): pl.pallas_call(functools.partial(_gather_kernel, n), out_shape=jax.ShapeD...  58.4 us
    all_to_all x1, blocking collectives, local(): lax.all_to_all(outgoing.reshape(experts, capacity, block_width), 'dp', sp...  42.7 us
    all_gather x1, waiting for transfers between devices, local(): lax.all_gather(shared_up, 'dp', axis=0, tiled=True)  37.2 us
    all_to_all x1, waiting for transfers between devices, local(): lax.all_to_all(copies, 'mp', split_axis=0, concat_axis=0, tiled=True)  34.1 us
    all_to_all x1, waiting for transfers between devices, local(): lax.all_to_all(expert_out.reshape(experts, capacity, block_width), 'dp',...  28.3 us
    all_gather x1, blocking collectives, local(): lax.all_gather(hidden, 'mp', axis=1, tiled=True).astype(jnp.float32)  13.3 us
    all_to_all x1, waiting for transfers between devices, local(): lax.all_to_all(jnp.concatenate([partial_value, gain_row], axis=1), 'mp',...  12.4 us
    all_to_all x1, waiting for transfers between devices, reduce_scatter_mp(): lax.all_to_all(blocks, 'mp', split_axis=0, concat_axis=0, tiled=True)  11.3 us
  transfers between devices with their start and end apart: 8, of which 5 were waited for; matrix products, arithmetic and copies ran while one was open for 15% of the time, Pallas kernels for 17%

profile of v4, /device:TPU:8, one launch (start us, length us, event | category | flops | bytes accessed | tf_op | source)
XLA Modules:
  0.0 344.1 jit_solution(1325244139276227856)
XLA Ops:
  7.2 0.0 all-gather.4.cloned.1.call-start
  7.2 0.7 all-gather.4.cloned.1.call-update
  7.9 0.0 all-gather.8.cloned.1.call-start
  8.0 0.7 all-gather.8.cloned.1.call-update
  8.7 58.4 %shard_map.149 = bf16[2048,512]{1,0:T(8,128)(2,1)} custom-call(bf16[32,512]{1,0:T(8,128)(2,1)} %bitcast.79), custom_call_target="tpu_custom_call" | custom-call | tf_op jit(solution)/shard_map/pallas_call | solution.py:65
  67.1 2.4 convolution_bitcast_fusion.3
  69.6 1.1 pad_maximum_fusion
  70.7 4.4 %all-to-all-start = ((f32[4,129,512]{2,1,0:T(8,128)}), f32[4,129,512]{2,1,0:T(8,128)S(1)}, u32[]{:S(2)}, u32[]{:S(2)}) async-start(f32[4,129,512]{2,1,0:T(8,128)} %pad_maximum_fusion), calls=%async_computation | async-start | bytes 2228224 | tf_op jit(solution)/shard_map/all_to_all | solution.py:107
  75.1 0.1 copy.29
  75.2 0.1 eq.39
  75.4 0.1 eq.43
  75.5 1.8 reduce-window.6
  77.3 0.3 slice_reduce_fusion.1
  77.6 0.1 select_reduce_fusion.1
  77.8 0.1 add.43
  77.9 0.1 copy.32
  78.0 0.5 fusion
  78.5 12.4 %all-to-all-done = f32[4,129,512]{2,1,0:T(8,128)S(1)} async-done(((f32[4,129,512]{2,1,0:T(8,128)}), f32[4,129,512]{2,1,0:T(8,128)S(1)}, u32[]{:S(2)}, u32[]{:S(2)}) %all-to-all-start) | async-done | bytes 1056800 | tf_op jit(solution)/shard_map/all_to_all | solution.py:107
  90.9 0.1 slice_reduce_fusion
  91.1 13.3 %all_gather.12 = bf16[128,2048]{1,0:T(8,128)(2,1)S(1)} all-gather(bf16[128,512]{1,0:T(8,128)(2,1)S(1)} %add_convert_fusion), channel_id=1, replica_groups=mesh['dp'=64,'mp'=4] {'mp'}, dimensions={1}, use_global_device_ids=true | all-gather | bytes 655360 | tf_op jit(solution)/shard_map/all_gather | solution.py:118
  104.4 0.2 fusion.15
  104.6 0.5 convolution_convert_fusion
  105.1 42.7 %all_to_all.30 = bf16[64,16,512]{2,1,0:T(8,128)(2,1)S(1)} all-to-all(bf16[64,16,512]{2,1,0:T(8,128)(2,1)S(1)} %bitcast.74), channel_id=1, replica_groups=mesh['dp'=64,'mp'=4] {'dp'}, dimensions={0} | all-to-all | bytes 2097152 | tf_op jit(solution)/shard_map/all_to_all | solution.py:138
  147.7 2.2 broadcast_in_dim.22
  150.0 4.8 %all-to-all-start.3 = ((bf16[4,1024,512]{2,1,0:T(8,128)(2,1)}), bf16[4,1024,512]{2,1,0:T(8,128)(2,1)}, u32[]{:S(2)}, u32[]{:S(2)}) async-start(bf16[4,1024,512]{2,1,0:T(8,128)(2,1)} %broadcast_in_dim.22), calls=%async_computation.3 | async-start | bytes 8388608 | tf_op jit(solution)/shard_map/all_to_all | solution.py:146
  154.8 0.2 all-gather.6.cloned.1.call-start
  155.1 0.5 all-gather.6.cloned.1.call-update
  155.6 4.4 %reshape_squeeze.11 = bf16[352,4,512]{2,1,0:T(4,128)(2,1)} reshape(bf16[1,352,2048]{2,1,0:T(8,128)(2,1)} %param.23) | data formatting | bytes 2883584 | tf_op jit(solution)/shard_map/reshape;squeeze | solution.py:152
  160.0 4.4 %reshape_squeeze.10 = bf16[4,512,352]{1,0,2:T(4,128)(2,1)} reshape(bf16[1,2048,352]{1,2,0:T(8,128)(2,1)} %param.22) | data formatting | bytes 2883584 | tf_op jit(solution)/shard_map/reshape;squeeze | solution.py:148
  164.4 4.4 %reshape_squeeze.9 = bf16[4,512,352]{1,0,2:T(4,128)(2,1)} reshape(bf16[1,2048,352]{1,2,0:T(8,128)(2,1)} %param.21) | data formatting | bytes 2883584 | tf_op jit(solution)/shard_map/reshape;squeeze | solution.py:147
  168.8 34.1 %all-to-all-done.3 = bf16[4,1024,512]{2,1,0:T(8,128)(2,1)} async-done(((bf16[4,1024,512]{2,1,0:T(8,128)(2,1)}), bf16[4,1024,512]{2,1,0:T(8,128)(2,1)}, u32[]{:S(2)}, u32[]{:S(2)}) %all-to-all-start.3) | async-done | bytes 4194336 | tf_op jit(solution)/shard_map/all_to_all | solution.py:146
  202.9 5.4 %convolution_bitcast_fusion.1 = f32[1024,352]{0,1:T(8,128)} fusion(bf16[4,1024,512]{2,1,0:T(8,128)(2,1)} %all-to-all-done.3, bf16[4,512,352]{1,0,2:T(4,128)(2,1)} %reshape_squeeze.9), kind=kOutput, calls=%fused_computation.7 | convolution fusion | flops 1476395008 | bytes 7077888 | tf_op jit(solution)/shard_map/qsf,qfh->sh/dot_general | solution.py:149
  208.4 9.4 %convert_bitcast_fusion = bf16[4,1024,512]{2,1,0:T(8,128)(2,1)} fusion(bf16[352,4,512]{2,1,0:T(4,128)(2,1)} %reshape_squeeze.11, bf16[4,1024,512]{2,1,0:T(8,128)(2,1)} %all-to-all-done.3, bf16[4,512,352]{1,0,2:T(4,128)(2,1)} %reshape_squeeze.10, f32[1024,352]{0,1:T(8,128)} %convolution_bitcast_fusion.1), kind=kOutput, calls=%fused_computation | convolution fusion | flops 2957049856 | bytes 12713984 | tf_op jit(solution)/shard_map/sh,hqf->qsf/dot_general | solution.py:153
  217.7 5.1 %all-to-all-start.4 = ((bf16[4,1024,512]{2,1,0:T(8,128)(2,1)}), bf16[4,1024,512]{2,1,0:T(8,128)(2,1)}, u32[]{:S(2)}, u32[]{:S(2)}) async-start(bf16[4,1024,512]{2,1,0:T(8,128)(2,1)} %convert_bitcast_fusion), calls=%async_computation.4 | async-start | bytes 8388608 | tf_op jit(solution)/shard_map/all_to_all | solution.py:156
  222.8 0.0 all-gather.4.cloned.1.call-done
  222.9 3.2 fusion.38
  226.1 37.2 %all-gather.6.cloned.1.call-done = bf16[2048,704]{1,0:T(8,128)(2,1)} async-done(((bf16[32,704]{1,0:T(8,128)(2,1)}), bf16[2048,704]{1,0:T(8,128)(2,1)}) %all-gather.6.cloned.1.call-update) | async-done | bytes 2883600 | tf_op jit(solution)/shard_map/all_gather | solution.py:174
  263.3 7.2 %convolution_bitcast_fusion.2 = f32[4,128,512]{2,1,0:T(8,128)} fusion(bf16[4,512,704]{2,1,0:T(8,128)(2,1)} %bitcast.75, bf16[2048,704]{1,0:T(8,128)(2,1)} %all-gather.6.cloned.1.call-done, f32[128,704]{0,1:T(8,128)S(1)} %fusion.38, bf16[128,2048]{1,0:T(8,128)(2,1)S(1)} %all_gather.12, f32[2048]{0:T(1024)S(1)} %bitcast.77, f32[128]{0:T(128)S(1)} %add_rsqrt_fusion.1), kind=kOutput, calls=%fused_computation.12 | convolution fusion | flops 739786752 | bytes 7709184 | tf_op jit(solution)/shard_map/th,qfh->qtf/dot_general | solution.py:180
  270.5 4.3 %all-to-all-start.1 = ((f32[4,128,512]{2,1,0:T(8,128)}), f32[4,128,512]{2,1,0:T(8,128)S(1)}, u32[]{:S(2)}, u32[]{:S(2)}) async-start(f32[4,128,512]{2,1,0:T(8,128)} %convolution_bitcast_fusion.2), calls=%async_computation.1 | async-start | bytes 2097152 | tf_op jit(solution)/shard_map/all_to_all | solution.py:76
  274.8 4.2 %reduce_sum.81 = bf16[1024,512]{1,0:T(8,128)(2,1)} reduce(bf16[4,1024,512]{2,1,0:T(8,128)(2,1)} %all-to-all-done.4, bf16[]{:T(256)} %constant.25.clone.1), dimensions={0}, to_apply=%region_9.10 | reduce | flops 1572864 | bytes 5242882 | tf_op jit(solution)/shard_map/reduce_sum | solution.py:157
  279.1 11.3 %all-to-all-done.1 = f32[4,128,512]{2,1,0:T(8,128)S(1)} async-done(((f32[4,128,512]{2,1,0:T(8,128)}), f32[4,128,512]{2,1,0:T(8,128)S(1)}, u32[]{:S(2)}, u32[]{:S(2)}) %all-to-all-start.1) | async-done | bytes 1048608 | tf_op jit(solution)/shard_map/all_to_all | solution.py:76
  290.4 8.0 %all-to-all-start.5 = ((bf16[64,16,512]{2,1,0:T(8,128)(2,1)}), bf16[64,16,512]{2,1,0:T(8,128)(2,1)S(1)}, u32[]{:S(2)}, u32[]{:S(2)}) async-start(bf16[64,16,512]{2,1,0:T(8,128)(2,1)} %bitcast.16), calls=%async_computation.5 | async-start | bytes 2097152 | tf_op jit(solution)/shard_map/all_to_all | solution.py:158
  298.4 0.4 select_reduce_fusion
  298.8 0.1 reduce_sum.77
  298.9 28.3 %all-to-all-done.5 = bf16[64,16,512]{2,1,0:T(8,128)(2,1)S(1)} async-done(((bf16[64,16,512]{2,1,0:T(8,128)(2,1)}), bf16[64,16,512]{2,1,0:T(8,128)(2,1)S(1)}, u32[]{:S(2)}, u32[]{:S(2)}) %all-to-all-start.5) | async-done | bytes 1048608 | tf_op jit(solution)/shard_map/all_to_all | solution.py:158
  327.2 0.7 fusion.28
  327.9 8.9 %psum.7 = f32[128]{0:T(128)S(1)} all-reduce(f32[128]{0:T(128)S(1)} %get-tuple-element.4), channel_id=1, replica_groups=mesh['dp'=64,'mp'=4] {'mp'}, use_global_device_ids=true, to_apply=%region_11.12 | all-reduce | flops 128 | bytes 1024 | tf_op jit(solution)/shard_map/psum | solution.py:189
  336.8 0.8 fusion.30
  (26 shorter events, 0.2 us)
Async XLA Ops:
  7.2 60.0 %copy-start = (bf16[128,512]{1,0:T(8,128)(2,1)S(1)}, bf16[128,512]{1,0:T(8,128)(2,1)}, u32[]{:S(2)}) copy-start(bf16[128,512]{1,0:T(8,128)(2,1)} %param.14) | copy-start | bytes 393220
  7.2 215.7 %all-gather.4.cloned.1.call-start = ((), (), s32[]{:S(2)}) async-start(), calls=%async_computation.6 | async-start | bytes 3194880 | tf_op jit(solution)/shard_map/all_gather | solution.py:173
  7.9 218.2 %all-gather.8.cloned.1.call-start = ((), (), s32[]{:S(2)}) async-start(), calls=%async_computation.8 | async-start | bytes 3194880 | tf_op jit(solution)/shard_map/all_gather | solution.py:179
  67.1 2.4 copy-start.3
  69.6 5.6 %copy-start.5 = (s32[128,6]{0,1:T(8,128)S(1)}, s32[128,6]{0,1:T(8,128)}, u32[]{:S(2)}) copy-start(s32[128,6]{0,1:T(8,128)} %param.24) | copy-start | bytes 9220
  70.7 7.0 %copy-start.7 = (s32[64]{0:T(128)S(1)}, s32[64]{0:T(128)}, u32[]{:S(2)}) copy-start(s32[64]{0:T(128)} %param.26) | copy-start | bytes 772
  70.7 20.4 %copy-start.2 = (bf16[128,512]{1,0:T(8,128)(2,1)S(1)}, bf16[128,512]{1,0:T(8,128)(2,1)}, u32[]{:S(2)}) copy-start(bf16[128,512]{1,0:T(8,128)(2,1)} %param.15) | copy-start | bytes 393220
  70.7 20.3 %all-to-all-start = ((f32[4,129,512]{2,1,0:T(8,128)}), f32[4,129,512]{2,1,0:T(8,128)S(1)}, u32[]{:S(2)}, u32[]{:S(2)}) async-start(f32[4,129,512]{2,1,0:T(8,128)} %pad_maximum_fusion), calls=%async_computation | async-start | bytes 2228224 | tf_op jit(solution)/shard_map/all_to_all | solution.py:107
  150.0 52.9 %all-to-all-start.3 = ((bf16[4,1024,512]{2,1,0:T(8,128)(2,1)}), bf16[4,1024,512]{2,1,0:T(8,128)(2,1)}, u32[]{:S(2)}, u32[]{:S(2)}) async-start(bf16[4,1024,512]{2,1,0:T(8,128)(2,1)} %broadcast_in_dim.22), calls=%async_computation.3 | async-start | bytes 8388608 | tf_op jit(solution)/shard_map/all_to_all | solution.py:146
  154.8 108.5 %all-gather.6.cloned.1.call-start = ((), (), s32[]{:S(2)}) async-start(), calls=%async_computation.7 | async-start | bytes 3194880 | tf_op jit(solution)/shard_map/all_gather | solution.py:174
  217.7 52.8 %all-to-all-start.4 = ((bf16[4,1024,512]{2,1,0:T(8,128)(2,1)}), bf16[4,1024,512]{2,1,0:T(8,128)(2,1)}, u32[]{:S(2)}, u32[]{:S(2)}) async-start(bf16[4,1024,512]{2,1,0:T(8,128)(2,1)} %convert_bitcast_fusion), calls=%async_computation.4 | async-start | bytes 8388608 | tf_op jit(solution)/shard_map/all_to_all | solution.py:156
  270.5 19.8 %all-to-all-start.1 = ((f32[4,128,512]{2,1,0:T(8,128)}), f32[4,128,512]{2,1,0:T(8,128)S(1)}, u32[]{:S(2)}, u32[]{:S(2)}) async-start(f32[4,128,512]{2,1,0:T(8,128)} %convolution_bitcast_fusion.2), calls=%async_computation.1 | async-start | bytes 2097152 | tf_op jit(solution)/shard_map/all_to_all | solution.py:76
  279.1 19.3 %copy-start.4 = (f32[128,6]{0,1:T(8,128)S(1)}, f32[128,6]{0,1:T(8,128)}, u32[]{:S(2)}) copy-start(f32[128,6]{0,1:T(8,128)} %param.25) | copy-start | bytes 9220
  290.4 36.8 %all-to-all-start.5 = ((bf16[64,16,512]{2,1,0:T(8,128)(2,1)}), bf16[64,16,512]{2,1,0:T(8,128)(2,1)S(1)}, u32[]{:S(2)}, u32[]{:S(2)}) async-start(bf16[64,16,512]{2,1,0:T(8,128)(2,1)} %bitcast.16), calls=%async_computation.5 | async-start | bytes 2097152 | tf_op jit(solution)/shard_map/all_to_all | solution.py:158
  298.4 38.4 %copy-start.6 = (f32[512]{0:T(512)S(1)}, f32[512]{0:T(512)}, u32[]{:S(2)}) copy-start(f32[512]{0:T(512)} %param.27) | copy-start | bytes 6148
  327.9 9.7 %copy-start.1 = (bf16[128,512]{1,0:T(8,128)(2,1)}, bf16[128,512]{1,0:T(8,128)(2,1)S(1)}, u32[]{:S(2)}) copy-start(bf16[128,512]{1,0:T(8,128)(2,1)S(1)} %get-tuple-element.5) | copy-start | bytes 393220
Sparse Core Ops, SparseCore 0:
  10.8 94.1 all-gather.3
  107.7 77.0 all-gather.7
  187.6 75.6 all-gather.5

commit v5 on v4

--- a/solution.py
+++ b/solution.py
@@ -144,6 +144,9 @@
     ).reshape(slots, block_width)
     copies = jnp.broadcast_to(arrived[None], (mp_count, slots, block_width))
     in_rows = lax.all_to_all(copies, "mp", split_axis=0, concat_axis=0, tiled=True)
+    down_shard, _ = lax.optimization_barrier((shared_down.T, copies))
+    shared_down_t = gather_dp(down_shard, 1)
+    in_rows, shared_down_t = lax.optimization_barrier((in_rows, shared_down_t))
     gate_block = expert_gate[0].reshape(mp_count, block_width, -1)
     up_block = expert_up[0].reshape(mp_count, block_width, -1)
     gate_val = jnp.einsum("qsf,qfh->sh", in_rows, gate_block, preferred_element_type=jnp.float32)
@@ -176,7 +179,6 @@
     shared_gval = matmul(whole_rows, pieces[0])
     shared_uval = matmul(whole_rows, pieces[1])
     shared_act = (jax.nn.silu(shared_gval) * shared_uval).astype(jnp.bfloat16)
-    shared_down_t = lax.all_gather(shared_down.T, "dp", axis=0, tiled=True)
     shared_part = jnp.einsum(
         "th,qfh->qtf",
         shared_act,

time: 345 us -> 394 us (1.14)
  Pallas kernels: 58.4 us -> 135 us
  waiting for transfers between devices: 125 us -> 92.4 us
  starting transfers between devices: 27 us -> 33 us
    pallas_call x1 -> x2, Pallas kernels: 58.4 us -> 135 us  [gather_dp(): pl.pallas_call(functools.partial(_gather_kernel, n), out_shape=jax.ShapeD...]
    all_to_all x1, waiting for transfers between devices: 0.01 us -> 39.3 us  [local(): lax.all_to_all(partial_out, 'mp', split_axis=0, concat_axis=0, tiled=True)]
    all_gather x1, waiting for transfers between devices: 37.2 us -> 0.02 us  [local(): lax.all_gather(shared_up, 'dp', axis=0, tiled=True)]
    all_to_all x1, waiting for transfers between devices: 34.1 us -> 0.01 us  [local(): lax.all_to_all(copies, 'mp', split_axis=0, concat_axis=0, tiled=True)]
    all_to_all x1, starting transfers between devices: 8 us -> 14.9 us  [local(): lax.all_to_all(expert_out.reshape(experts, capacity, block_width), 'dp',...]
  transfers between devices with their start and end apart: 8 -> 7, of which waited for: 5 -> 4; matrix products, arithmetic and copies ran while one was open for 15% -> 14% of each run, Pallas kernels for 17% -> 34%
where the time goes in v5:
time: 394 us; the launch traced here: 393 us
  Pallas kernels  135 us (34%)
  waiting for transfers between devices  92.4 us (23%)
  blocking collectives  63.1 us (16%)
  starting transfers between devices  33 us (8%)
  matrix products  29 us (7%)
  local copies, waits for them, and re-layouts  16.5 us (4%)
  between operations  14.3 us (4%)
  other arithmetic  9.28 us (2%)
    pallas_call x2, Pallas kernels, gather_dp(): pl.pallas_call(functools.partial(_gather_kernel, n), out_shape=jax.ShapeD...  135 us
    all_to_all x1, blocking collectives, local(): lax.all_to_all(outgoing.reshape(experts, capacity, block_width), 'dp', sp...  40.8 us
    all_to_all x1, waiting for transfers between devices, local(): lax.all_to_all(partial_out, 'mp', split_axis=0, concat_axis=0, tiled=True)  39.3 us
    all_to_all x1, waiting for transfers between devices, local(): lax.all_to_all(expert_out.reshape(experts, capacity, block_width), 'dp',...  28.1 us
    all_to_all x1, starting transfers between devices, local(): lax.all_to_all(expert_out.reshape(experts, capacity, block_width), 'dp',...  14.9 us
    all_gather x1, blocking collectives, local(): lax.all_gather(hidden, 'mp', axis=1, tiled=True).astype(jnp.float32)  13.4 us
    all_to_all x1, waiting for transfers between devices, local(): lax.all_to_all(jnp.concatenate([partial_value, gain_row], axis=1), 'mp',...  12.4 us
    all_to_all x1, waiting for transfers between devices, reduce_scatter_mp(): lax.all_to_all(blocks, 'mp', split_axis=0, concat_axis=0, tiled=True)  11.3 us
  transfers between devices with their start and end apart: 7, of which 4 were waited for; matrix products, arithmetic and copies ran while one was open for 14% of the time, Pallas kernels for 34%

profile of v5, /device:TPU:8, one launch (start us, length us, event | category | flops | bytes accessed | tf_op | source)
XLA Modules:
  0.0 393.0 jit_solution(3304502946321604743)
XLA Ops:
  7.2 0.0 all-gather.3.cloned.1.call-start
  7.2 0.7 all-gather.3.cloned.1.call-update
  7.9 58.4 %shard_map.149 = bf16[2048,512]{1,0:T(8,128)(2,1)} custom-call(bf16[32,512]{1,0:T(8,128)(2,1)} %bitcast.77), custom_call_target="tpu_custom_call" | custom-call | tf_op jit(solution)/shard_map/pallas_call | solution.py:65
  66.4 2.4 convolution_bitcast_fusion.3
  68.8 1.1 pad_maximum_fusion
  69.9 4.4 %all-to-all-start = ((f32[4,129,512]{2,1,0:T(8,128)}), f32[4,129,512]{2,1,0:T(8,128)S(1)}, u32[]{:S(2)}, u32[]{:S(2)}) async-start(f32[4,129,512]{2,1,0:T(8,128)} %pad_maximum_fusion), calls=%async_computation | async-start | bytes 2228224 | tf_op jit(solution)/shard_map/all_to_all | solution.py:107
  74.4 0.1 copy.36
  74.5 0.1 eq.39
  74.6 0.1 eq.43
  74.8 1.8 reduce-window.6
  76.6 0.3 slice_reduce_fusion.1
  76.9 0.1 select_reduce_fusion.1
  77.1 0.1 add.41
  77.2 0.1 copy.39
  77.2 0.5 fusion
  77.8 12.4 %all-to-all-done = f32[4,129,512]{2,1,0:T(8,128)S(1)} async-done(((f32[4,129,512]{2,1,0:T(8,128)}), f32[4,129,512]{2,1,0:T(8,128)S(1)}, u32[]{:S(2)}, u32[]{:S(2)}) %all-to-all-start) | async-done | bytes 1056800 | tf_op jit(solution)/shard_map/all_to_all | solution.py:107
  90.2 0.1 slice_reduce_fusion
  90.3 13.4 %all_gather.9 = bf16[128,2048]{1,0:T(8,128)(2,1)S(1)} all-gather(bf16[128,512]{1,0:T(8,128)(2,1)S(1)} %add_convert_fusion), channel_id=1, replica_groups=mesh['dp'=64,'mp'=4] {'mp'}, dimensions={1}, use_global_device_ids=true | all-gather | bytes 655360 | tf_op jit(solution)/shard_map/all_gather | solution.py:118
  103.7 0.2 fusion.15
  103.9 0.5 convolution_convert_fusion
  104.4 40.8 %all_to_all.30 = bf16[64,16,512]{2,1,0:T(8,128)(2,1)S(1)} all-to-all(bf16[64,16,512]{2,1,0:T(8,128)(2,1)S(1)} %bitcast.74), channel_id=1, replica_groups=mesh['dp'=64,'mp'=4] {'dp'}, dimensions={0} | all-to-all | bytes 2097152 | tf_op jit(solution)/shard_map/all_to_all | solution.py:138
  145.2 2.3 broadcast_in_dim.20
  147.5 4.9 %all-to-all-start.2 = ((bf16[4,1024,512]{2,1,0:T(8,128)(2,1)}), bf16[4,1024,512]{2,1,0:T(8,128)(2,1)}, u32[]{:S(2)}, u32[]{:S(2)}) async-start(bf16[4,1024,512]{2,1,0:T(8,128)(2,1)} %broadcast_in_dim.20), calls=%async_computation.2 | async-start | bytes 8388608 | tf_op jit(solution)/shard_map/all_to_all | solution.py:146
  152.4 0.2 all-gather.5.cloned.1.call-start
  152.6 0.5 all-gather.5.cloned.1.call-update
  153.1 4.4 %reshape_squeeze.11 = bf16[352,4,512]{2,1,0:T(4,128)(2,1)} reshape(bf16[1,352,2048]{2,1,0:T(8,128)(2,1)} %param.23) | data formatting | bytes 2883584 | tf_op jit(solution)/shard_map/reshape;squeeze | solution.py:155
  157.5 4.4 %reshape_squeeze.10 = bf16[4,512,352]{1,0,2:T(4,128)(2,1)} reshape(bf16[1,2048,352]{1,2,0:T(8,128)(2,1)} %param.22) | data formatting | bytes 2883584 | tf_op jit(solution)/shard_map/reshape;squeeze | solution.py:151
  161.9 4.4 %reshape_squeeze.9 = bf16[4,512,352]{1,0,2:T(4,128)(2,1)} reshape(bf16[1,2048,352]{1,2,0:T(8,128)(2,1)} %param.21) | data formatting | bytes 2883584 | tf_op jit(solution)/shard_map/reshape;squeeze | solution.py:150
  166.3 76.9 %shard_map.150 = bf16[2048,704]{1,0:T(8,128)(2,1)} custom-call(bf16[32,704]{1,0:T(8,128)(2,1)} %bitcast.76), custom_call_target="tpu_custom_call" | custom-call | tf_op jit(solution)/shard_map/pallas_call | solution.py:65
  243.3 5.5 %convolution_bitcast_fusion.1 = f32[1024,352]{0,1:T(8,128)} fusion(bf16[4,1024,512]{2,1,0:T(8,128)(2,1)} %all-to-all-done.2, bf16[4,512,352]{1,0,2:T(4,128)(2,1)} %reshape_squeeze.9), kind=kOutput, calls=%fused_computation.7 | convolution fusion | flops 1476395008 | bytes 7077888 | tf_op jit(solution)/shard_map/qsf,qfh->sh/dot_general | solution.py:152
  248.7 9.5 %convert_bitcast_fusion = bf16[4,1024,512]{2,1,0:T(8,128)(2,1)} fusion(bf16[352,4,512]{2,1,0:T(4,128)(2,1)} %reshape_squeeze.11, bf16[4,1024,512]{2,1,0:T(8,128)(2,1)} %all-to-all-done.2, bf16[4,512,352]{1,0,2:T(4,128)(2,1)} %reshape_squeeze.10, f32[1024,352]{0,1:T(8,128)} %convolution_bitcast_fusion.1), kind=kOutput, calls=%fused_computation | convolution fusion | flops 2957049856 | bytes 12713984 | tf_op jit(solution)/shard_map/sh,hqf->qsf/dot_general | solution.py:156
  258.2 5.1 %all-to-all-start.4 = ((bf16[4,1024,512]{2,1,0:T(8,128)(2,1)}), bf16[4,1024,512]{2,1,0:T(8,128)(2,1)}, u32[]{:S(2)}, u32[]{:S(2)}) async-start(bf16[4,1024,512]{2,1,0:T(8,128)(2,1)} %convert_bitcast_fusion), calls=%async_computation.4 | async-start | bytes 8388608 | tf_op jit(solution)/shard_map/all_to_all | solution.py:159
  263.3 0.0 all-gather.3.cloned.1.call-done
  263.4 3.2 fusion.38
  266.6 0.0 all-gather.5.cloned.1.call-done
  266.6 7.2 %convolution_bitcast_fusion.2 = f32[4,128,512]{1,2,0:T(8,128)} fusion(bf16[4,512,704]{2,1,0:T(8,128)(2,1)} %bitcast.75, bf16[2048,704]{1,0:T(8,128)(2,1)} %all-gather.5.cloned.1.call-done, f32[128,704]{0,1:T(8,128)S(1)} %fusion.38, bf16[128,2048]{1,0:T(8,128)(2,1)S(1)} %all_gather.9, f32[2048]{0:T(1024)S(1)} %bitcast.79, f32[128]{0:T(128)S(1)} %add_rsqrt_fusion.1), kind=kOutput, calls=%fused_computation.12 | convolution fusion | flops 739786752 | bytes 7709184 | tf_op jit(solution)/shard_map/th,qfh->qtf/dot_general | solution.py:182
  273.8 39.3 %all-to-all-done.4 = bf16[4,1024,512]{2,1,0:T(8,128)(2,1)} async-done(((bf16[4,1024,512]{2,1,0:T(8,128)(2,1)}), bf16[4,1024,512]{2,1,0:T(8,128)(2,1)}, u32[]{:S(2)}, u32[]{:S(2)}) %all-to-all-start.4) | async-done | bytes 4194336 | tf_op jit(solution)/shard_map/all_to_all | solution.py:159
  313.1 3.5 all-to-all-start.3
  316.7 4.1 %reduce_sum.81 = bf16[1024,512]{1,0:T(8,128)(2,1)} reduce(bf16[4,1024,512]{2,1,0:T(8,128)(2,1)} %all-to-all-done.4, bf16[]{:T(256)} %constant.25.clone.1), dimensions={0}, to_apply=%region_9.10 | reduce | flops 1572864 | bytes 5242882 | tf_op jit(solution)/shard_map/reduce_sum | solution.py:160
  320.8 11.3 %all-to-all-done.3 = f32[4,128,512]{1,2,0:T(8,128)S(1)} async-done(((f32[4,128,512]{1,2,0:T(8,128)}), f32[4,128,512]{1,2,0:T(8,128)S(1)}, u32[]{:S(2)}, u32[]{:S(2)}) %all-to-all-start.3) | async-done | bytes 1048608 | tf_op jit(solution)/shard_map/all_to_all | solution.py:76
  332.1 14.9 %all-to-all-start.5 = ((bf16[64,16,512]{2,1,0:T(8,128)(2,1)}), bf16[64,16,512]{2,1,0:T(8,128)(2,1)S(1)}, u32[]{:S(2)}, u32[]{:S(2)}) async-start(bf16[64,16,512]{2,1,0:T(8,128)(2,1)} %bitcast.16), calls=%async_computation.5 | async-start | bytes 2097152 | tf_op jit(solution)/shard_map/all_to_all | solution.py:161
  347.0 0.4 select_reduce_fusion
  347.4 0.1 reduce_sum.79
  347.5 0.1 copy.44
  347.6 28.1 %all-to-all-done.5 = bf16[64,16,512]{2,1,0:T(8,128)(2,1)S(1)} async-done(((bf16[64,16,512]{2,1,0:T(8,128)(2,1)}), bf16[64,16,512]{2,1,0:T(8,128)(2,1)S(1)}, u32[]{:S(2)}, u32[]{:S(2)}) %all-to-all-start.5) | async-done | bytes 1048608 | tf_op jit(solution)/shard_map/all_to_all | solution.py:161
  375.7 0.7 fusion.28
  376.4 8.9 %psum.7 = f32[128]{0:T(128)S(1)} all-reduce(f32[128]{0:T(128)S(1)} %get-tuple-element.10), channel_id=1, replica_groups=mesh['dp'=64,'mp'=4] {'mp'}, use_global_device_ids=true, to_apply=%region_11.12 | all-reduce | flops 128 | bytes 1024 | tf_op jit(solution)/shard_map/psum | solution.py:191
  385.4 0.8 fusion.30
  (25 shorter events, 0.2 us)
Async XLA Ops:
  7.2 59.2 %copy-start = (bf16[128,512]{1,0:T(8,128)(2,1)S(1)}, bf16[128,512]{1,0:T(8,128)(2,1)}, u32[]{:S(2)}) copy-start(bf16[128,512]{1,0:T(8,128)(2,1)} %param.14) | copy-start | bytes 393220
  7.2 256.2 %all-gather.3.cloned.1.call-start = ((), (), s32[]{:S(2)}) async-start(), calls=%async_computation.6 | async-start | bytes 3194880 | tf_op jit(solution)/shard_map/all_gather | solution.py:176
  66.4 2.4 copy-start.3
  68.8 5.6 %copy-start.5 = (s32[128,6]{0,1:T(8,128)S(1)}, s32[128,6]{0,1:T(8,128)}, u32[]{:S(2)}) copy-start(s32[128,6]{0,1:T(8,128)} %param.24) | copy-start | bytes 9220
  69.9 7.0 %copy-start.7 = (s32[64]{0:T(128)S(1)}, s32[64]{0:T(128)}, u32[]{:S(2)}) copy-start(s32[64]{0:T(128)} %param.26) | copy-start | bytes 772
  69.9 20.3 %copy-start.2 = (bf16[128,512]{1,0:T(8,128)(2,1)S(1)}, bf16[128,512]{1,0:T(8,128)(2,1)}, u32[]{:S(2)}) copy-start(bf16[128,512]{1,0:T(8,128)(2,1)} %param.15) | copy-start | bytes 393220
  69.9 20.2 %all-to-all-start = ((f32[4,129,512]{2,1,0:T(8,128)}), f32[4,129,512]{2,1,0:T(8,128)S(1)}, u32[]{:S(2)}, u32[]{:S(2)}) async-start(f32[4,129,512]{2,1,0:T(8,128)} %pad_maximum_fusion), calls=%async_computation | async-start | bytes 2228224 | tf_op jit(solution)/shard_map/all_to_all | solution.py:107
  147.5 95.7 %all-to-all-start.2 = ((bf16[4,1024,512]{2,1,0:T(8,128)(2,1)}), bf16[4,1024,512]{2,1,0:T(8,128)(2,1)}, u32[]{:S(2)}, u32[]{:S(2)}) async-start(bf16[4,1024,512]{2,1,0:T(8,128)(2,1)} %broadcast_in_dim.20), calls=%async_computation.2 | async-start | bytes 8388608 | tf_op jit(solution)/shard_map/all_to_all | solution.py:146
  152.4 114.2 %all-gather.5.cloned.1.call-start = ((), (), s32[]{:S(2)}) async-start(), calls=%async_computation.7 | async-start | bytes 3194880 | tf_op jit(solution)/shard_map/all_gather | solution.py:177
  258.2 54.9 %all-to-all-start.4 = ((bf16[4,1024,512]{2,1,0:T(8,128)(2,1)}), bf16[4,1024,512]{2,1,0:T(8,128)(2,1)}, u32[]{:S(2)}, u32[]{:S(2)}) async-start(bf16[4,1024,512]{2,1,0:T(8,128)(2,1)} %convert_bitcast_fusion), calls=%async_computation.4 | async-start | bytes 8388608 | tf_op jit(solution)/shard_map/all_to_all | solution.py:159
  313.1 18.9 %all-to-all-start.3 = ((f32[4,128,512]{1,2,0:T(8,128)}), f32[4,128,512]{1,2,0:T(8,128)S(1)}, u32[]{:S(2)}, u32[]{:S(2)}) async-start(f32[4,128,512]{1,2,0:T(8,128)} %convolution_bitcast_fusion.2), calls=%async_computation.3 | async-start | bytes 2097152 | tf_op jit(solution)/shard_map/all_to_all | solution.py:76
  320.8 26.2 %copy-start.4 = (f32[128,6]{0,1:T(8,128)S(1)}, f32[128,6]{0,1:T(8,128)}, u32[]{:S(2)}) copy-start(f32[128,6]{0,1:T(8,128)} %param.25) | copy-start | bytes 9220
  332.1 43.7 %all-to-all-start.5 = ((bf16[64,16,512]{2,1,0:T(8,128)(2,1)}), bf16[64,16,512]{2,1,0:T(8,128)(2,1)S(1)}, u32[]{:S(2)}, u32[]{:S(2)}) async-start(bf16[64,16,512]{2,1,0:T(8,128)(2,1)} %bitcast.16), calls=%async_computation.5 | async-start | bytes 2097152 | tf_op jit(solution)/shard_map/all_to_all | solution.py:161
  347.4 38.0 %copy-start.6 = (f32[512]{0:T(512)S(1)}, f32[512]{0:T(512)}, u32[]{:S(2)}) copy-start(f32[512]{0:T(512)} %param.27) | copy-start | bytes 6148
  376.4 9.7 %copy-start.1 = (bf16[128,512]{1,0:T(8,128)(2,1)}, bf16[128,512]{1,0:T(8,128)(2,1)S(1)}, u32[]{:S(2)}) copy-start(bf16[128,512]{1,0:T(8,128)(2,1)S(1)} %get-tuple-element.11) | copy-start | bytes 393220
Sparse Core Ops, SparseCore 0:
  10.8 93.5 all-gather.2
  156.0 106.0 all-gather.4

commit v6 on v4

--- a/solution.py
+++ b/solution.py
@@ -5,7 +5,7 @@
 from jax import lax
 from jax.experimental import pallas as pl
 from jax.experimental.pallas import tpu as pltpu
-from jax.sharding import PartitionSpec as P
+from jax.sharding import Mesh, PartitionSpec as P
 
 MESH = pl.DeviceIdType.MESH
 
@@ -26,14 +26,15 @@
 
 
 def _gather_kernel(n, x_ref, o_ref, send_sem, recv_sem):
-    me = lax.axis_index("dp")
+    me = lax.axis_index("g")
+    core = lax.axis_index("c")
     col = lax.axis_index("mp")
     rows = x_ref.shape[0]
     barrier = pltpu.get_barrier_semaphore()
 
     def greet(p, carry):
         peer = lax.rem(me + p, n)
-        pl.semaphore_signal(barrier, inc=1, device_id=(peer, col), device_id_type=MESH)
+        pl.semaphore_signal(barrier, inc=1, device_id=(peer, core, col), device_id_type=MESH)
         return carry
 
     lax.fori_loop(1, n, greet, 0)
@@ -48,7 +49,7 @@
             dst_ref=own,
             send_sem=send_sem,
             recv_sem=recv_sem,
-            device_id=(peer, col),
+            device_id=(peer, core, col),
             device_id_type=MESH,
         ).start()
         return carry
@@ -59,8 +60,8 @@
     pltpu.make_async_copy(o_ref, o_ref, recv_sem).wait()
 
 
-def gather_dp(x, collective_id):
-    n = lax.axis_size("dp")
+def gather_g(x, collective_id):
+    n = lax.axis_size("g")
     rows, cols = x.shape
     return pl.pallas_call(
         functools.partial(_gather_kernel, n),
@@ -74,6 +75,20 @@
 
 def reduce_scatter_mp(blocks):
     return jnp.sum(lax.all_to_all(blocks, "mp", split_axis=0, concat_axis=0, tiled=True), axis=0)
+
+
+def swap_halves(value, tok_rows):
+    return lax.all_to_all(
+        value.reshape(2, tok_rows, value.shape[1]), "c", split_axis=0, concat_axis=0, tiled=True
+    )
+
+
+def natural_blocks(halves, mp_count):
+    _, rows, cols = halves.shape
+    pairs = lax.axis_size("g")
+    width = cols // pairs
+    ordered = jnp.transpose(halves.reshape(2, rows, pairs, width), (1, 2, 0, 3))
+    return jnp.transpose(ordered.reshape(rows, mp_count, -1), (1, 0, 2))
 
 
 def local(
@@ -92,17 +107,21 @@
     placement,
     next_gain,
 ):
+    dp = ("g", "c")
     tok_rows = attention.shape[0]
     top_count = route_ids.shape[1]
     mp_count = lax.axis_size("mp")
-    experts = lax.axis_size("dp")
+    pairs = lax.axis_size("g")
+    experts = pairs * lax.axis_size("c")
+    core = lax.axis_index("c")
     capacity = min(tok_rows, 8 * tok_rows // experts)
     model_width = D
     block_width = model_width // mp_count
-    out_weight_t = gather_dp(out_weight.T, 0).reshape(mp_count, block_width, -1)
-    partial_value = jnp.einsum(
-        "tk,qfk->qtf", attention, out_weight_t, preferred_element_type=jnp.float32
-    )
+
+    w_half = gather_g(out_weight.T, 0)
+    att_pair = lax.all_gather(attention, "c", axis=0, tiled=True)
+    part_half = matmul_t(att_pair, w_half)
+    partial_value = natural_blocks(swap_halves(part_half, tok_rows), mp_count)
     gain_row = jnp.broadcast_to(ffn_gain[None, None, :], (mp_count, 1, block_width))
     exchanged = lax.all_to_all(
         jnp.concatenate([partial_value, gain_row], axis=1),
@@ -137,7 +156,7 @@
     outgoing = matmul(pick.T, normed).astype(jnp.bfloat16)
     arrived = lax.all_to_all(
         outgoing.reshape(experts, capacity, block_width),
-        "dp",
+        dp,
         split_axis=0,
         concat_axis=0,
         tiled=True,
@@ -157,7 +176,7 @@
     expert_out = jnp.sum(summed.astype(jnp.float32), axis=0).astype(jnp.bfloat16)
     returned = lax.all_to_all(
         expert_out.reshape(experts, capacity, block_width),
-        "dp",
+        dp,
         split_axis=0,
         concat_axis=0,
         tiled=True,
@@ -169,20 +188,22 @@
         preferred_element_type=jnp.float32,
     )
 
-    pieces = (
-        lax.all_gather(shared_gate, "dp", axis=0, tiled=True),
-        lax.all_gather(shared_up, "dp", axis=0, tiled=True),
-    )
-    shared_gval = matmul(whole_rows, pieces[0])
-    shared_uval = matmul(whole_rows, pieces[1])
-    shared_act = (jax.nn.silu(shared_gval) * shared_uval).astype(jnp.bfloat16)
-    shared_down_t = lax.all_gather(shared_down.T, "dp", axis=0, tiled=True)
-    shared_part = jnp.einsum(
-        "th,qfh->qtf",
-        shared_act,
-        shared_down_t.reshape(mp_count, block_width, -1),
-        preferred_element_type=jnp.float32,
-    )
+    k_block = shared_gate.shape[0]
+    hidden_units = shared_gate.shape[1]
+    rows_pair = lax.all_gather(whole_rows, "c", axis=0, tiled=True)
+    rows_half = lax.dynamic_index_in_dim(
+        rows_pair.reshape(2 * tok_rows, pairs, 2, k_block), core, axis=2, keepdims=False
+    ).reshape(2 * tok_rows, pairs * k_block)
+    gate_half = lax.all_gather(shared_gate, "g", axis=0, tiled=True)
+    up_half = lax.all_gather(shared_up, "g", axis=0, tiled=True)
+    gate_up = jnp.concatenate([matmul(rows_half, gate_half), matmul(rows_half, up_half)], axis=1)
+    gate_up = jnp.sum(swap_halves(gate_up, tok_rows), axis=0)
+    shared_act = (
+        jax.nn.silu(gate_up[:, :hidden_units]) * gate_up[:, hidden_units:]
+    ).astype(jnp.bfloat16)
+    act_pair = lax.all_gather(shared_act, "c", axis=0, tiled=True)
+    down_half = lax.all_gather(shared_down.T, "g", axis=0, tiled=True)
+    shared_part = natural_blocks(swap_halves(matmul_t(act_pair, down_half), tok_rows), mp_count)
     mixture = reduce_scatter_mp(shared_part) + routed
     final = (hidden_float + mixture).astype(jnp.bfloat16)
     final_float = final.astype(jnp.float32)
@@ -194,21 +215,24 @@
 
 
 def solution(mesh):
+    dp_count, mp_count = mesh.devices.shape
+    paired = Mesh(mesh.devices.reshape(dp_count // 2, 2, mp_count), ("g", "c", "mp"))
+    dp = ("g", "c")
     in_specs = (
-        P("dp", "mp"),
-        P("dp", "mp"),
-        P("mp", "dp"),
+        P(dp, "mp"),
+        P(dp, "mp"),
+        P("mp", dp),
         P("mp"),
-        P("dp", "mp"),
-        P("dp", "mp"),
-        P("mp", "dp"),
-        P("dp", None, "mp"),
-        P("dp", None, "mp"),
-        P("dp", "mp", None),
-        P("dp", None),
-        P("dp", None),
+        P(dp, "mp"),
+        P(dp, "mp"),
+        P("mp", dp),
+        P(dp, None, "mp"),
+        P(dp, None, "mp"),
+        P(dp, "mp", None),
+        P(dp, None),
+        P(dp, None),
         P(),
         P("mp"),
     )
-    out_specs = (P("dp", "mp"), P("dp", "mp"))
-    return jax.shard_map(local, mesh=mesh, in_specs=in_specs, out_specs=out_specs, check_vma=False)
+    out_specs = (P(dp, "mp"), P(dp, "mp"))
+    return jax.shard_map(local, mesh=paired, in_specs=in_specs, out_specs=out_specs, check_vma=False)

time: 345 us -> 534 us (1.55)
  waiting for transfers between devices: 125 us -> 316 us
  blocking collectives: 64.8 us -> 93 us
  Pallas kernels: 58.4 us -> 34.2 us
    all_gather x3 -> x4, waiting for transfers between devices: 37.2 us -> 226 us  [the longest x1 78.4 us: local(): up_half = lax.all_gather(shared_up, 'g', axis=0, tiled=True)]
    all_to_all x1, waiting for transfers between devices: 0.01 us -> 48.4 us  [local(): lax.all_to_all(partial_out, 'mp', split_axis=0, concat_axis=0, tiled=True)]
    all_to_all x1, waiting for transfers between devices: 34.1 us -> 0.01 us  [local(): lax.all_to_all(copies, 'mp', split_axis=0, concat_axis=0, tiled=True)]
    pallas_call x1, Pallas kernels: 58.4 us -> 34.2 us  [gather_g(): pl.pallas_call(functools.partial(_gather_kernel, n), out_shape=jax.ShapeD...]
    all_to_all x1 -> x4, blocking collectives: 42.7 us -> 66.2 us  [the longest x1 36.5 us: local(): lax.all_to_all(outgoing.reshape(experts, capacity, block_width), dp, spli...]
    all_to_all x2, waiting for transfers between devices: 40.7 us -> 28.1 us  [the longest x1 28.1 us: local(): lax.all_to_all(expert_out.reshape(experts, capacity, block_width), dp, sp...]
    dot_general x2, matrix products: 9.61 us -> 3.71 us  [matmul_t(): lax.dot_general(left, right_t, (((1,), (1,)), ((), ())), preferred_elemen...]
  transfers between devices with their start and end apart: 8 -> 9, of which waited for: 5 -> 7; matrix products, arithmetic and copies ran while one was open for 15% -> 8% of each run, Pallas kernels for 17% -> 0%
where the time goes in v6:
time: 534 us; the launch traced here: 533 us
  waiting for transfers between devices  316 us (59%)
  blocking collectives  93 us (17%)
  Pallas kernels  34.2 us (6%)
  starting transfers between devices  25.2 us (5%)
  matrix products  23.8 us (4%)
  local copies, waits for them, and re-layouts  17.7 us (3%)
  between operations  14.1 us (3%)
  other arithmetic  9.65 us (2%)
    all_gather x1, waiting for transfers between devices, local(): up_half = lax.all_gather(shared_up, 'g', axis=0, tiled=True)  78.4 us
    all_gather x1, waiting for transfers between devices, local(): gate_half = lax.all_gather(shared_gate, 'g', axis=0, tiled=True)  75.1 us
    all_gather x1, waiting for transfers between devices, local(): down_half = lax.all_gather(shared_down.T, 'g', axis=0, tiled=True)  64.7 us
    all_to_all x1, waiting for transfers between devices, local(): lax.all_to_all(partial_out, 'mp', split_axis=0, concat_axis=0, tiled=True)  48.4 us
    all_to_all x1, blocking collectives, local(): lax.all_to_all(outgoing.reshape(experts, capacity, block_width), dp, spli...  36.5 us
    pallas_call x1, Pallas kernels, gather_g(): pl.pallas_call(functools.partial(_gather_kernel, n), out_shape=jax.ShapeD...  34.2 us
    all_to_all x1, waiting for transfers between devices, local(): lax.all_to_all(expert_out.reshape(experts, capacity, block_width), dp, sp...  28.1 us
    all_to_all x1, blocking collectives, local(): lax.all_to_all(jnp.concatenate([partial_value, gain_row], axis=1), 'mp',...  20.3 us
  transfers between devices with their start and end apart: 9, of which 7 were waited for; matrix products, arithmetic and copies ran while one was open for 8% of the time, Pallas kernels for 0%

profile of v6, /device:TPU:8, one launch (start us, length us, event | category | flops | bytes accessed | tf_op | source)
XLA Modules:
  0.0 533.3 jit_solution(1522442356685785508)
XLA Ops:
  7.2 2.2 all_gather.21
  9.4 34.2 %shard_map.149 = bf16[1024,512]{1,0:T(8,128)(2,1)} custom-call(bf16[32,512]{1,0:T(8,128)(2,1)} %bitcast.96), custom_call_target="tpu_custom_call" | custom-call | tf_op jit(solution)/shard_map/pallas_call | solution.py:66
  43.6 1.7 fusion.33
  45.3 0.3 copy.60
  45.7 4.6 all_to_all.45
  50.3 0.6 copy-done.7
  51.2 0.8 copy.62
  52.0 20.3 %all_to_all.46 = f32[4,129,512]{2,1,0:T(8,128)S(1)} all-to-all(f32[4,129,512]{2,1,0:T(8,128)S(1)} %copy.62), channel_id=1, replica_groups=mesh['g'=32,'c'=2,'mp'=4] {'mp'}, dimensions={0} | all-to-all | bytes 2113536 | tf_op jit(solution)/shard_map/all_to_all | solution.py:126
  72.5 13.6 %all_gather.22 = bf16[128,2048]{1,0:T(8,128)(2,1)S(1)} all-gather(bf16[128,512]{1,0:T(8,128)(2,1)S(1)} %add_convert_fusion), channel_id=1, replica_groups=mesh['g'=32,'c'=2,'mp'=4] {'mp'}, dimensions={1}, use_global_device_ids=true | all-gather | bytes 655360 | tf_op jit(solution)/shard_map/all_gather | solution.py:137
  86.3 1.0 fusion.15
  87.3 0.7 all-gather.9.cloned.1.call-update
  88.1 0.7 all-gather.7.cloned.1.call-update
  89.2 1.8 reduce-window.6
  91.7 0.5 fusion
  92.2 0.5 convolution_convert_fusion
  92.7 8.0 %all-gather.5.cloned.1.call-done = bf16[256,2048]{1,0:T(8,128)(2,1)} async-done(((bf16[128,2048]{1,0:T(8,128)(2,1)}), bf16[256,2048]{1,0:T(8,128)(2,1)}) %all-gather.5.cloned.1.call-update) | async-done | bytes 1048592 | tf_op jit(solution)/shard_map/all_gather | solution.py:193
  100.8 1.5 copy.65
  102.3 78.4 %all-gather.9.cloned.1.call-done = bf16[1024,704]{1,0:T(8,128)(2,1)} async-done(((bf16[32,704]{1,0:T(8,128)(2,1)}), bf16[1024,704]{1,0:T(8,128)(2,1)}) %all-gather.9.cloned.1.call-update) | async-done | bytes 1441808 | tf_op jit(solution)/shard_map/all_gather | solution.py:198
  180.7 2.1 fusion.35
  182.8 75.1 %all-gather.7.cloned.1.call-done = bf16[1024,704]{1,0:T(8,128)(2,1)} async-done(((bf16[32,704]{1,0:T(8,128)(2,1)}), bf16[1024,704]{1,0:T(8,128)(2,1)}) %all-gather.7.cloned.1.call-update) | async-done | bytes 1441808 | tf_op jit(solution)/shard_map/all_gather | solution.py:197
  258.0 2.1 fusion.34
  260.2 4.9 all_to_all.47
  265.1 36.5 %all_to_all.48 = bf16[64,16,512]{2,1,0:T(8,128)(2,1)S(1)} all-to-all(bf16[64,16,512]{2,1,0:T(8,128)(2,1)S(1)} %bitcast.88), channel_id=1, replica_groups=mesh['g'=32,'c'=2,'mp'=4] {'g','c'}, dimensions={0} | all-to-all | bytes 2097152 | tf_op jit(solution)/shard_map/all_to_all | solution.py:157
  301.6 2.3 broadcast_in_dim.22
  303.9 5.0 all-to-all-start.6
  308.9 0.5 all-gather.11.cloned.1.call-update
  309.4 2.0 reshape_squeeze.11
  311.4 4.5 reshape_squeeze.10
  315.9 2.0 reshape_squeeze.9
  318.2 2.1 all_gather.26
  320.2 64.7 %all-gather.11.cloned.1.call-done = bf16[1024,704]{1,0:T(8,128)(2,1)} async-done(((bf16[32,704]{1,0:T(8,128)(2,1)}), bf16[1024,704]{1,0:T(8,128)(2,1)}) %all-gather.11.cloned.1.call-update) | async-done | bytes 1441808 | tf_op jit(solution)/shard_map/all_gather | solution.py:205
  384.9 2.0 fusion.36
  386.9 1.3 copy.68
  388.3 3.8 all-to-all-start.3
  392.1 5.6 %convolution_bitcast_fusion.1 = f32[1024,352]{0,1:T(8,128)} fusion(bf16[4,1024,512]{2,1,0:T(8,128)(2,1)} %all-to-all-done.6, bf16[4,512,352]{1,0,2:T(4,128)(2,1)} %reshape_squeeze.9), kind=kOutput, calls=%fused_computation.8 | convolution fusion | flops 1476395008 | bytes 7077888 | tf_op jit(solution)/shard_map/qsf,qfh->sh/dot_general | solution.py:168
  397.7 9.0 %convert_bitcast_fusion = bf16[4,1024,512]{2,1,0:T(8,128)(2,1)} fusion(bf16[352,4,512]{2,1,0:T(4,128)(2,1)S(1)} %copy-done.4, bf16[4,1024,512]{2,1,0:T(8,128)(2,1)} %all-to-all-done.6, bf16[4,512,352]{1,0,2:T(4,128)(2,1)} %reshape_squeeze.10, f32[1024,352]{0,1:T(8,128)} %convolution_bitcast_fusion.1), kind=kOutput, calls=%fused_computation | convolution fusion | flops 2957049856 | bytes 12713984 | tf_op jit(solution)/shard_map/sh,hqf->qsf/dot_general | solution.py:172
  406.7 4.9 all-to-all-start.7
  411.6 1.2 copy.69
  412.7 48.4 %all-to-all-done.7 = bf16[4,1024,512]{2,1,0:T(8,128)(2,1)} async-done(((bf16[4,1024,512]{2,1,0:T(8,128)(2,1)}), bf16[4,1024,512]{2,1,0:T(8,128)(2,1)}, u32[]{:S(2)}, u32[]{:S(2)}) %all-to-all-start.7) | async-done | bytes 4194336 | tf_op jit(solution)/shard_map/all_to_all | solution.py:175
  461.2 3.5 all-to-all-start.4
  464.7 4.1 reduce_sum.91
  468.8 10.9 %all-to-all-done.4 = f32[4,128,512]{1,2,0:T(8,128)S(1)} async-done(((f32[4,128,512]{1,2,0:T(8,128)}), f32[4,128,512]{1,2,0:T(8,128)S(1)}, u32[]{:S(2)}, u32[]{:S(2)}) %all-to-all-start.4) | async-done | bytes 1048608 | tf_op jit(solution)/shard_map/all_to_all | solution.py:77
  479.7 7.9 %all-to-all-start.8 = ((bf16[64,16,512]{2,1,0:T(8,128)(2,1)}), bf16[64,16,512]{2,1,0:T(8,128)(2,1)S(1)}, u32[]{:S(2)}, u32[]{:S(2)}) async-start(bf16[64,16,512]{2,1,0:T(8,128)(2,1)} %bitcast.22), calls=%async_computation.8 | async-start | bytes 2097152 | tf_op jit(solution)/shard_map/all_to_all | solution.py:177
  487.6 0.4 select_reduce_fusion
  488.2 28.1 %all-to-all-done.8 = bf16[64,16,512]{2,1,0:T(8,128)(2,1)S(1)} async-done(((bf16[64,16,512]{2,1,0:T(8,128)(2,1)}), bf16[64,16,512]{2,1,0:T(8,128)(2,1)S(1)}, u32[]{:S(2)}, u32[]{:S(2)}) %all-to-all-start.8) | async-done | bytes 1048608 | tf_op jit(solution)/shard_map/all_to_all | solution.py:177
  516.4 0.7 fusion.22
  517.1 8.9 %psum.7 = f32[128]{0:T(128)S(1)} all-reduce(f32[128]{0:T(128)S(1)} %get-tuple-element.4), channel_id=1, replica_groups=mesh['g'=32,'c'=2,'mp'=4] {'mp'}, use_global_device_ids=true, to_apply=%region_12.13 | all-reduce | flops 128 | bytes 1024 | tf_op jit(solution)/shard_map/psum | solution.py:210
  526.0 0.8 fusion.24
  (55 shorter events, 2.5 us)
Async XLA Ops:
  7.2 93.6 %all-gather.5.cloned.1.call-start = ((), (), s32[]{:S(2)}) async-start(), calls=%async_computation.9 | async-start | bytes 1572864 | tf_op jit(solution)/shard_map/all_gather | solution.py:193
  50.2 0.7 copy-start.7
  52.0 20.4 %copy-start.6 = (bf16[128,512]{1,0:T(8,128)(2,1)S(1)}, bf16[128,512]{1,0:T(8,128)(2,1)}, u32[]{:S(2)}) copy-start(bf16[128,512]{1,0:T(8,128)(2,1)} %param.15) | copy-start | bytes 393220
  72.4 19.8 %copy-start = (bf16[128,512]{1,0:T(8,128)(2,1)}, bf16[128,512]{1,0:T(8,128)(2,1)S(1)}, u32[]{:S(2)}) copy-start(bf16[128,512]{1,0:T(8,128)(2,1)S(1)} %add_convert_fusion) | copy-start | bytes 393220
  72.4 16.3 %copy-start.9 = (s32[128,6]{0,1:T(8,128)S(1)}, s32[128,6]{0,1:T(8,128)}, u32[]{:S(2)}) copy-start(s32[128,6]{0,1:T(8,128)} %param.24) | copy-start | bytes 9220
  86.2 5.1 copy-start.11
  87.3 93.4 %all-gather.9.cloned.1.call-start = ((), (), s32[]{:S(2)}) async-start(), calls=%async_computation.11 | async-start | bytes 1622016 | tf_op jit(solution)/shard_map/all_gather | solution.py:198
  88.0 170.0 %all-gather.7.cloned.1.call-start = ((), (), s32[]{:S(2)}) async-start(), calls=%async_computation.10 | async-start | bytes 1622016 | tf_op jit(solution)/shard_map/all_gather | solution.py:197
  303.9 5.6 %copy-start.2 = (bf16[1,352,2048]{2,1,0:T(8,128)(2,1)S(1)}, bf16[1,352,2048]{2,1,0:T(8,128)(2,1)}, u32[]{:S(2)}) copy-start(bf16[1,352,2048]{2,1,0:T(8,128)(2,1)} %param.23) | copy-start | bytes 4325380
  303.9 84.4 %all-to-all-start.6 = ((bf16[4,1024,512]{2,1,0:T(8,128)(2,1)}), bf16[4,1024,512]{2,1,0:T(8,128)(2,1)}, u32[]{:S(2)}, u32[]{:S(2)}) async-start(bf16[4,1024,512]{2,1,0:T(8,128)(2,1)} %broadcast_in_dim.22), calls=%async_computation.6 | async-start | bytes 8388608 | tf_op jit(solution)/shard_map/all_to_all | solution.py:165
  308.9 76.1 %all-gather.11.cloned.1.call-start = ((), (), s32[]{:S(2)}) async-start(), calls=%async_computation.12 | async-start | bytes 1622016 | tf_op jit(solution)/shard_map/all_gather | solution.py:205
  311.4 4.5 copy-start.3
  388.3 18.4 %all-to-all-start.3 = ((f32[2,128,1024]{1,2,0:T(8,128)}), f32[2,128,1024]{1,2,0:T(8,128)S(1)}, u32[]{:S(2)}, u32[]{:S(2)}) async-start(f32[2,128,1024]{1,2,0:T(8,128)} %copy.68), calls=%async_computation.3 | async-start | bytes 2097152 | tf_op jit(solution)/shard_map/all_to_all | solution.py:81
  392.0 5.6 %copy-start.4 = (bf16[352,4,512]{2,1,0:T(4,128)(2,1)S(1)}, bf16[352,4,512]{2,1,0:T(4,128)(2,1)}, u32[]{:S(2)}) copy-start(bf16[352,4,512]{2,1,0:T(4,128)(2,1)} %reshape_squeeze.11) | copy-start | bytes 4325380
  406.7 54.5 %all-to-all-start.7 = ((bf16[4,1024,512]{2,1,0:T(8,128)(2,1)}), bf16[4,1024,512]{2,1,0:T(8,128)(2,1)}, u32[]{:S(2)}, u32[]{:S(2)}) async-start(bf16[4,1024,512]{2,1,0:T(8,128)(2,1)} %convert_bitcast_fusion), calls=%async_computation.7 | async-start | bytes 8388608 | tf_op jit(solution)/shard_map/all_to_all | solution.py:175
  461.2 18.5 %all-to-all-start.4 = ((f32[4,128,512]{1,2,0:T(8,128)}), f32[4,128,512]{1,2,0:T(8,128)S(1)}, u32[]{:S(2)}, u32[]{:S(2)}) async-start(f32[4,128,512]{1,2,0:T(8,128)} %bitcast.14), calls=%async_computation.4 | async-start | bytes 2097152 | tf_op jit(solution)/shard_map/all_to_all | solution.py:77
  468.8 18.8 %copy-start.8 = (f32[128,6]{0,1:T(8,128)S(1)}, f32[128,6]{0,1:T(8,128)}, u32[]{:S(2)}) copy-start(f32[128,6]{0,1:T(8,128)} %param.25) | copy-start | bytes 9220
  479.7 36.7 %all-to-all-start.8 = ((bf16[64,16,512]{2,1,0:T(8,128)(2,1)}), bf16[64,16,512]{2,1,0:T(8,128)(2,1)S(1)}, u32[]{:S(2)}, u32[]{:S(2)}) async-start(bf16[64,16,512]{2,1,0:T(8,128)(2,1)} %bitcast.22), calls=%async_computation.8 | async-start | bytes 2097152 | tf_op jit(solution)/shard_map/all_to_all | solution.py:177
  487.6 28.8 %copy-start.1 = (bf16[128,512]{1,0:T(8,128)(2,1)S(1)}, bf16[128,512]{1,0:T(8,128)(2,1)}, u32[]{:S(2)}) copy-start(bf16[128,512]{1,0:T(8,128)(2,1)} %copy-done) | copy-start | bytes 393220
  488.1 37.9 %copy-start.10 = (f32[512]{0:T(512)S(1)}, f32[512]{0:T(512)}, u32[]{:S(2)}) copy-start(f32[512]{0:T(512)} %param.27) | copy-start | bytes 6148
  517.1 9.7 %copy-start.5 = (bf16[128,512]{1,0:T(8,128)(2,1)}, bf16[128,512]{1,0:T(8,128)(2,1)S(1)}, u32[]{:S(2)}) copy-start(bf16[128,512]{1,0:T(8,128)(2,1)S(1)} %get-tuple-element.5) | copy-start | bytes 393220
Sparse Core Ops, SparseCore 0:
  87.4 13.3 all-gather.4
  103.3 77.3 all-gather.8
  183.3 74.6 all-gather.6
  312.0 72.9 all-gather.10

commit v7 on v6

--- a/solution.py
+++ b/solution.py
@@ -194,15 +194,18 @@
     rows_half = lax.dynamic_index_in_dim(
         rows_pair.reshape(2 * tok_rows, pairs, 2, k_block), core, axis=2, keepdims=False
     ).reshape(2 * tok_rows, pairs * k_block)
-    gate_half = lax.all_gather(shared_gate, "g", axis=0, tiled=True)
-    up_half = lax.all_gather(shared_up, "g", axis=0, tiled=True)
+    shared_half = lax.all_gather(
+        jnp.concatenate([shared_gate, shared_up, shared_down.T], axis=1), "g", axis=0, tiled=True
+    )
+    gate_half = shared_half[:, :hidden_units]
+    up_half = shared_half[:, hidden_units : 2 * hidden_units]
+    down_half = shared_half[:, 2 * hidden_units :]
     gate_up = jnp.concatenate([matmul(rows_half, gate_half), matmul(rows_half, up_half)], axis=1)
     gate_up = jnp.sum(swap_halves(gate_up, tok_rows), axis=0)
     shared_act = (
         jax.nn.silu(gate_up[:, :hidden_units]) * gate_up[:, hidden_units:]
     ).astype(jnp.bfloat16)
     act_pair = lax.all_gather(shared_act, "c", axis=0, tiled=True)
-    down_half = lax.all_gather(shared_down.T, "g", axis=0, tiled=True)
     shared_part = natural_blocks(swap_halves(matmul_t(act_pair, down_half), tok_rows), mp_count)
     mixture = reduce_scatter_mp(shared_part) + routed
     final = (hidden_float + mixture).astype(jnp.bfloat16)

time: 534 us -> 347 us (0.65)
  waiting for transfers between devices: 316 us -> 127 us
  blocking collectives: 93 us -> 101 us
    all_gather x3 -> x1, waiting for transfers between devices: 218 us -> 0.01 us  [local(): lax.all_gather(jnp.concatenate([shared_gate, shared_up, shared_down.T], a...]
    all_to_all x1, waiting for transfers between devices: 0.01 us -> 40.4 us  [local(): lax.all_to_all(copies, 'mp', split_axis=0, concat_axis=0, tiled=True)]
    all_gather x1, waiting for transfers between devices: 8.05 us -> 0.01 us  [local(): rows_pair = lax.all_gather(whole_rows, 'c', axis=0, tiled=True)]
    all_to_all x2 -> x3, blocking collectives: 9.47 us -> 14 us  [swap_halves(): lax.all_to_all(value.reshape(2, tok_rows, value.shape[1]), 'c', split_axi...]
  transfers between devices with their start and end apart: 9 -> 6, of which waited for: 7 -> 4; matrix products, arithmetic and copies ran while one was open for 8% -> 10% of each run, Pallas kernels for 0% -> 0%
where the time goes in v7:
time: 347 us; the launch traced here: 346 us
  waiting for transfers between devices  127 us (37%)
  blocking collectives  101 us (29%)
  Pallas kernels  34.2 us (10%)
  matrix products  24.1 us (7%)
  starting transfers between devices  20.3 us (6%)
  local copies, waits for them, and re-layouts  14.8 us (4%)
  between operations  14.4 us (4%)
  other arithmetic  9.7 us (3%)
    all_to_all x1, waiting for transfers between devices, local(): lax.all_to_all(partial_out, 'mp', split_axis=0, concat_axis=0, tiled=True)  48.4 us
    all_to_all x1, waiting for transfers between devices, local(): lax.all_to_all(copies, 'mp', split_axis=0, concat_axis=0, tiled=True)  40.4 us
    all_to_all x1, blocking collectives, local(): lax.all_to_all(outgoing.reshape(experts, capacity, block_width), dp, spli...  40.2 us
    pallas_call x1, Pallas kernels, gather_g(): pl.pallas_call(functools.partial(_gather_kernel, n), out_shape=jax.ShapeD...  34.2 us
    all_to_all x1, waiting for transfers between devices, local(): lax.all_to_all(expert_out.reshape(experts, capacity, block_width), dp, sp...  28.1 us
    all_to_all x1, blocking collectives, local(): lax.all_to_all(jnp.concatenate([partial_value, gain_row], axis=1), 'mp',...  20.3 us
    all_to_all x3, blocking collectives, swap_halves(): lax.all_to_all(value.reshape(2, tok_rows, value.shape[1]), 'c', split_axi...  14 us
    all_gather x1, blocking collectives, local(): lax.all_gather(hidden, 'mp', axis=1, tiled=True).astype(jnp.float32)  13.6 us
  transfers between devices with their start and end apart: 6, of which 4 were waited for; matrix products, arithmetic and copies ran while one was open for 10% of the time, Pallas kernels for 0%

profile of v7, /device:TPU:8, one launch (start us, length us, event | category | flops | bytes accessed | tf_op | source)
XLA Modules:
  0.0 346.3 jit_solution(12926957355102290933)
XLA Ops:
  7.2 2.2 all_gather.15
  9.4 34.2 %shard_map.149 = bf16[1024,512]{1,0:T(8,128)(2,1)} custom-call(bf16[32,512]{1,0:T(8,128)(2,1)} %bitcast.93), custom_call_target="tpu_custom_call" | custom-call | tf_op jit(solution)/shard_map/pallas_call | solution.py:66
  43.6 1.7 fusion.39
  45.3 0.3 copy.60
  45.7 4.6 %all_to_all.45 = f32[2,128,1024]{1,2,0:T(8,128)S(1)} all-to-all(f32[2,128,1024]{1,2,0:T(8,128)S(1)} %copy.60), channel_id=1, replica_groups=mesh['g'=32,'c'=2,'mp'=4] {'c'}, dimensions={0} | all-to-all | bytes 2097152 | tf_op jit(solution)/shard_map/all_to_all | solution.py:81
  50.3 0.6 copy-done.10
  51.1 0.1 pad_maximum_fusion
  51.2 0.8 copy.62
  52.0 20.3 %all_to_all.46 = f32[4,129,512]{2,1,0:T(8,128)S(1)} all-to-all(f32[4,129,512]{2,1,0:T(8,128)S(1)} %copy.62), channel_id=1, replica_groups=mesh['g'=32,'c'=2,'mp'=4] {'mp'}, dimensions={0} | all-to-all | bytes 2113536 | tf_op jit(solution)/shard_map/all_to_all | solution.py:126
  72.5 13.6 %all_gather.16 = bf16[128,2048]{1,0:T(8,128)(2,1)S(1)} all-gather(bf16[128,512]{1,0:T(8,128)(2,1)S(1)} %add_convert_fusion), channel_id=1, replica_groups=mesh['g'=32,'c'=2,'mp'=4] {'mp'}, dimensions={1}, use_global_device_ids=true | all-gather | bytes 655360 | tf_op jit(solution)/shard_map/all_gather | solution.py:137
  86.1 0.2 fusion.19
  86.3 1.0 fusion.21
  87.4 0.8 concatenate.10
  88.6 1.8 reduce-window.6
  90.4 0.3 slice_reduce_fusion.1
  90.7 0.1 select_reduce_fusion.1
  91.0 0.5 fusion
  91.6 0.5 convolution_convert_fusion
  92.1 40.2 %all_to_all.47 = bf16[64,16,512]{2,1,0:T(8,128)(2,1)S(1)} all-to-all(bf16[64,16,512]{2,1,0:T(8,128)(2,1)S(1)} %bitcast.84), channel_id=1, replica_groups=mesh['g'=32,'c'=2,'mp'=4] {'g','c'}, dimensions={0} | all-to-all | bytes 2097152 | tf_op jit(solution)/shard_map/all_to_all | solution.py:157
  132.3 2.3 broadcast_in_dim.22
  134.6 5.2 %all-to-all-start.6 = ((bf16[4,1024,512]{2,1,0:T(8,128)(2,1)}), bf16[4,1024,512]{2,1,0:T(8,128)(2,1)}, u32[]{:S(2)}, u32[]{:S(2)}) async-start(bf16[4,1024,512]{2,1,0:T(8,128)(2,1)} %broadcast_in_dim.22), calls=%async_computation.6 | async-start | bytes 8388608 | tf_op jit(solution)/shard_map/all_to_all | solution.py:165
  139.8 2.0 reshape_squeeze.11
  141.8 2.0 reshape_squeeze.10
  143.8 2.0 reshape_squeeze.9
  145.8 1.5 copy.65
  147.3 40.4 %all-to-all-done.6 = bf16[4,1024,512]{2,1,0:T(8,128)(2,1)} async-done(((bf16[4,1024,512]{2,1,0:T(8,128)(2,1)}), bf16[4,1024,512]{2,1,0:T(8,128)(2,1)}, u32[]{:S(2)}, u32[]{:S(2)}) %all-to-all-start.6) | async-done | bytes 4194336 | tf_op jit(solution)/shard_map/all_to_all | solution.py:165
  187.7 5.4 %convolution_bitcast_fusion.1 = f32[1024,352]{0,1:T(8,128)} fusion(bf16[4,1024,512]{2,1,0:T(8,128)(2,1)} %all-to-all-done.6, bf16[4,512,352]{1,0,2:T(4,128)(2,1)} %reshape_squeeze.9), kind=kOutput, calls=%fused_computation.14 | convolution fusion | flops 1476395008 | bytes 7077888 | tf_op jit(solution)/shard_map/qsf,qfh->sh/dot_general | solution.py:168
  193.2 8.6 %convert_bitcast_fusion = bf16[4,1024,512]{2,1,0:T(8,128)(2,1)} fusion(bf16[352,4,512]{2,1,0:T(4,128)(2,1)S(1)} %copy-done.3, bf16[4,1024,512]{2,1,0:T(8,128)(2,1)} %all-to-all-done.6, bf16[4,512,352]{1,0,2:T(4,128)(2,1)S(1)} %copy-done.4, f32[1024,352]{0,1:T(8,128)} %convolution_bitcast_fusion.1), kind=kOutput, calls=%fused_computation | convolution fusion | flops 2957049856 | bytes 12713984 | tf_op jit(solution)/shard_map/sh,hqf->qsf/dot_general | solution.py:172
  201.8 3.0 fusion.3
  204.8 2.1 fusion.5
  207.0 4.9 %all_to_all.48 = f32[2,128,1408]{1,2,0:T(8,128)S(1)} all-to-all(f32[2,128,1408]{1,2,0:T(8,128)S(1)} %copy_bitcast_fusion), channel_id=1, replica_groups=mesh['g'=32,'c'=2,'mp'=4] {'c'}, dimensions={0} | all-to-all | bytes 2883584 | tf_op jit(solution)/shard_map/all_to_all | solution.py:81
  211.9 0.1 reduce_sum.86
  212.2 2.1 all_gather.19
  214.2 2.0 fusion.1
  216.3 0.3 copy.68
  216.6 4.6 %all_to_all.49 = f32[2,128,1024]{1,2,0:T(8,128)S(1)} all-to-all(f32[2,128,1024]{1,2,0:T(8,128)S(1)} %copy.68), channel_id=1, replica_groups=mesh['g'=32,'c'=2,'mp'=4] {'c'}, dimensions={0} | all-to-all | bytes 2097152 | tf_op jit(solution)/shard_map/all_to_all | solution.py:81
  221.2 4.9 %all-to-all-start.7 = ((bf16[4,1024,512]{2,1,0:T(8,128)(2,1)}), bf16[4,1024,512]{2,1,0:T(8,128)(2,1)}, u32[]{:S(2)}, u32[]{:S(2)}) async-start(bf16[4,1024,512]{2,1,0:T(8,128)(2,1)} %convert_bitcast_fusion), calls=%async_computation.7 | async-start | bytes 8388608 | tf_op jit(solution)/shard_map/all_to_all | solution.py:175
  226.1 1.1 copy.69
  227.1 48.4 %all-to-all-done.7 = bf16[4,1024,512]{2,1,0:T(8,128)(2,1)} async-done(((bf16[4,1024,512]{2,1,0:T(8,128)(2,1)}), bf16[4,1024,512]{2,1,0:T(8,128)(2,1)}, u32[]{:S(2)}, u32[]{:S(2)}) %all-to-all-start.7) | async-done | bytes 4194336 | tf_op jit(solution)/shard_map/all_to_all | solution.py:175
  275.5 3.7 %all-to-all-start.4 = ((f32[4,128,512]{1,2,0:T(8,128)}), f32[4,128,512]{1,2,0:T(8,128)S(1)}, u32[]{:S(2)}, u32[]{:S(2)}) async-start(f32[4,128,512]{1,2,0:T(8,128)} %bitcast.14), calls=%async_computation.4 | async-start | bytes 2097152 | tf_op jit(solution)/shard_map/all_to_all | solution.py:77
  279.2 4.2 %reduce_sum.91 = bf16[1024,512]{1,0:T(8,128)(2,1)} reduce(bf16[4,1024,512]{2,1,0:T(8,128)(2,1)} %all-to-all-done.7, bf16[]{:T(256)} %constant.36.clone.1), dimensions={0}, to_apply=%region_10.11 | reduce | flops 1572864 | bytes 5242882 | tf_op jit(solution)/shard_map/reduce_sum | solution.py:176
  283.4 10.4 %all-to-all-done.4 = f32[4,128,512]{1,2,0:T(8,128)S(1)} async-done(((f32[4,128,512]{1,2,0:T(8,128)}), f32[4,128,512]{1,2,0:T(8,128)S(1)}, u32[]{:S(2)}, u32[]{:S(2)}) %all-to-all-start.4) | async-done | bytes 1048608 | tf_op jit(solution)/shard_map/all_to_all | solution.py:77
  293.8 6.5 %all-to-all-start.8 = ((bf16[64,16,512]{2,1,0:T(8,128)(2,1)}), bf16[64,16,512]{2,1,0:T(8,128)(2,1)S(1)}, u32[]{:S(2)}, u32[]{:S(2)}) async-start(bf16[64,16,512]{2,1,0:T(8,128)(2,1)} %bitcast.22), calls=%async_computation.8 | async-start | bytes 2097152 | tf_op jit(solution)/shard_map/all_to_all | solution.py:177
  300.3 0.4 select_reduce_fusion
  301.0 28.1 %all-to-all-done.8 = bf16[64,16,512]{2,1,0:T(8,128)(2,1)S(1)} async-done(((bf16[64,16,512]{2,1,0:T(8,128)(2,1)}), bf16[64,16,512]{2,1,0:T(8,128)(2,1)S(1)}, u32[]{:S(2)}, u32[]{:S(2)}) %all-to-all-start.8) | async-done | bytes 1048608 | tf_op jit(solution)/shard_map/all_to_all | solution.py:177
  329.1 0.7 fusion.28
  329.8 8.9 %psum.7 = f32[128]{0:T(128)S(1)} all-reduce(f32[128]{0:T(128)S(1)} %get-tuple-element.4), channel_id=1, replica_groups=mesh['g'=32,'c'=2,'mp'=4] {'mp'}, use_global_device_ids=true, to_apply=%region_12.13 | all-reduce | flops 128 | bytes 1024 | tf_op jit(solution)/shard_map/psum | solution.py:213
  338.7 0.8 fusion.30
  (55 shorter events, 1.6 us)
Async XLA Ops:
  7.2 138.6 %all-gather.3.cloned.1.call-start = ((), (), s32[]{:S(2)}) async-start(), calls=%async_computation.9 | async-start | bytes 1572864 | tf_op jit(solution)/shard_map/all_gather | solution.py:193
  50.2 0.7 copy-start.10
  52.0 20.4 %copy-start.6 = (bf16[128,512]{1,0:T(8,128)(2,1)S(1)}, bf16[128,512]{1,0:T(8,128)(2,1)}, u32[]{:S(2)}) copy-start(bf16[128,512]{1,0:T(8,128)(2,1)} %param.15) | copy-start | bytes 393220
  72.4 14.9 %copy-start.7 = (bf16[32,704]{1,0:T(8,128)(2,1)S(1)}, bf16[32,704]{1,0:T(8,128)(2,1)}, u32[]{:S(2)}) copy-start(bf16[32,704]{1,0:T(8,128)(2,1)} %param.18) | copy-start | bytes 135172
  72.4 14.9 %copy-start.8 = (bf16[32,704]{1,0:T(8,128)(2,1)S(1)}, bf16[32,704]{1,0:T(8,128)(2,1)}, u32[]{:S(2)}) copy-start(bf16[32,704]{1,0:T(8,128)(2,1)} %param.19) | copy-start | bytes 135172
  72.5 14.9 %copy-start.9 = (bf16[704,32]{0,1:T(8,128)(2,1)S(1)}, bf16[704,32]{0,1:T(8,128)(2,1)}, u32[]{:S(2)}) copy-start(bf16[704,32]{0,1:T(8,128)(2,1)} %param.20) | copy-start | bytes 135172
  86.1 2.1 copy-start.12
  86.3 4.4 %copy-start.14 = (s32[64]{0:T(128)S(1)}, s32[64]{0:T(128)}, u32[]{:S(2)}) copy-start(s32[64]{0:T(128)} %param.26) | copy-start | bytes 772
  87.3 114.5 %all-gather.5.cloned.1.call-start = ((), (), s32[]{:S(2)}) async-start(), calls=%async_computation.10 | async-start | bytes 4595712 | tf_op jit(solution)/shard_map/all_gather | solution.py:197
  134.6 5.2 %copy-start = (bf16[1,352,2048]{2,1,0:T(8,128)(2,1)S(1)}, bf16[1,352,2048]{2,1,0:T(8,128)(2,1)}, u32[]{:S(2)}) copy-start(bf16[1,352,2048]{2,1,0:T(8,128)(2,1)} %param.23) | copy-start | bytes 4325380
  134.6 53.2 %all-to-all-start.6 = ((bf16[4,1024,512]{2,1,0:T(8,128)(2,1)}), bf16[4,1024,512]{2,1,0:T(8,128)(2,1)}, u32[]{:S(2)}, u32[]{:S(2)}) async-start(bf16[4,1024,512]{2,1,0:T(8,128)(2,1)} %broadcast_in_dim.22), calls=%async_computation.6 | async-start | bytes 8388608 | tf_op jit(solution)/shard_map/all_to_all | solution.py:165
  139.8 2.0 copy-start.1
  141.8 2.0 copy-start.2
  147.3 45.9 %copy-start.3 = (bf16[352,4,512]{2,1,0:T(4,128)(2,1)S(1)}, bf16[352,4,512]{2,1,0:T(4,128)(2,1)}, u32[]{:S(2)}) copy-start(bf16[352,4,512]{2,1,0:T(4,128)(2,1)} %reshape_squeeze.11) | copy-start | bytes 4325380
  147.3 45.8 %copy-start.4 = (bf16[4,512,352]{1,0,2:T(4,128)(2,1)S(1)}, bf16[4,512,352]{1,0,2:T(4,128)(2,1)}, u32[]{:S(2)}) copy-start(bf16[4,512,352]{1,0,2:T(4,128)(2,1)} %reshape_squeeze.10) | copy-start | bytes 4325380
  221.2 54.3 %all-to-all-start.7 = ((bf16[4,1024,512]{2,1,0:T(8,128)(2,1)}), bf16[4,1024,512]{2,1,0:T(8,128)(2,1)}, u32[]{:S(2)}, u32[]{:S(2)}) async-start(bf16[4,1024,512]{2,1,0:T(8,128)(2,1)} %convert_bitcast_fusion), calls=%async_computation.7 | async-start | bytes 8388608 | tf_op jit(solution)/shard_map/all_to_all | solution.py:175
  275.5 18.3 %all-to-all-start.4 = ((f32[4,128,512]{1,2,0:T(8,128)}), f32[4,128,512]{1,2,0:T(8,128)S(1)}, u32[]{:S(2)}, u32[]{:S(2)}) async-start(f32[4,128,512]{1,2,0:T(8,128)} %bitcast.14), calls=%async_computation.4 | async-start | bytes 2097152 | tf_op jit(solution)/shard_map/all_to_all | solution.py:77
  283.4 16.9 %copy-start.11 = (f32[128,6]{0,1:T(8,128)S(1)}, f32[128,6]{0,1:T(8,128)}, u32[]{:S(2)}) copy-start(f32[128,6]{0,1:T(8,128)} %param.25) | copy-start | bytes 9220
  293.8 35.3 %all-to-all-start.8 = ((bf16[64,16,512]{2,1,0:T(8,128)(2,1)}), bf16[64,16,512]{2,1,0:T(8,128)(2,1)S(1)}, u32[]{:S(2)}, u32[]{:S(2)}) async-start(bf16[64,16,512]{2,1,0:T(8,128)(2,1)} %bitcast.22), calls=%async_computation.8 | async-start | bytes 2097152 | tf_op jit(solution)/shard_map/all_to_all | solution.py:177
  300.8 37.9 %copy-start.13 = (f32[512]{0:T(512)S(1)}, f32[512]{0:T(512)}, u32[]{:S(2)}) copy-start(f32[512]{0:T(512)} %param.27) | copy-start | bytes 6148
  329.8 9.7 %copy-start.5 = (bf16[128,512]{1,0:T(8,128)(2,1)}, bf16[128,512]{1,0:T(8,128)(2,1)S(1)}, u32[]{:S(2)}) copy-start(bf16[128,512]{1,0:T(8,128)(2,1)S(1)} %get-tuple-element.5) | copy-start | bytes 393220
Sparse Core Ops, SparseCore 0:
  87.4 13.3 all-gather.2
  103.4 83.5 all-gather.4

commit v8 on v6

--- a/solution.py
+++ b/solution.py
@@ -188,22 +188,19 @@
         preferred_element_type=jnp.float32,
     )
 
-    k_block = shared_gate.shape[0]
     hidden_units = shared_gate.shape[1]
-    rows_pair = lax.all_gather(whole_rows, "c", axis=0, tiled=True)
-    rows_half = lax.dynamic_index_in_dim(
-        rows_pair.reshape(2 * tok_rows, pairs, 2, k_block), core, axis=2, keepdims=False
-    ).reshape(2 * tok_rows, pairs * k_block)
-    gate_half = lax.all_gather(shared_gate, "g", axis=0, tiled=True)
-    up_half = lax.all_gather(shared_up, "g", axis=0, tiled=True)
-    gate_up = jnp.concatenate([matmul(rows_half, gate_half), matmul(rows_half, up_half)], axis=1)
-    gate_up = jnp.sum(swap_halves(gate_up, tok_rows), axis=0)
-    shared_act = (
-        jax.nn.silu(gate_up[:, :hidden_units]) * gate_up[:, hidden_units:]
-    ).astype(jnp.bfloat16)
-    act_pair = lax.all_gather(shared_act, "c", axis=0, tiled=True)
-    down_half = lax.all_gather(shared_down.T, "g", axis=0, tiled=True)
-    shared_part = natural_blocks(swap_halves(matmul_t(act_pair, down_half), tok_rows), mp_count)
+    shared_all = lax.all_gather(
+        jnp.concatenate([shared_gate, shared_up, shared_down.T], axis=1), dp, axis=0, tiled=True
+    )
+    shared_gval = matmul(whole_rows, shared_all[:, :hidden_units])
+    shared_uval = matmul(whole_rows, shared_all[:, hidden_units : 2 * hidden_units])
+    shared_act = (jax.nn.silu(shared_gval) * shared_uval).astype(jnp.bfloat16)
+    shared_part = jnp.einsum(
+        "th,qfh->qtf",
+        shared_act,
+        shared_all[:, 2 * hidden_units :].reshape(mp_count, block_width, hidden_units),
+        preferred_element_type=jnp.float32,
+    )
     mixture = reduce_scatter_mp(shared_part) + routed
     final = (hidden_float + mixture).astype(jnp.bfloat16)
     final_float = final.astype(jnp.float32)

time: 534 us -> 325 us (0.61)
  waiting for transfers between devices: 316 us -> 123 us
  blocking collectives: 93 us -> 67.2 us
    all_gather x4 -> x1, waiting for transfers between devices: 226 us -> 0.02 us  [local(): lax.all_gather(jnp.concatenate([shared_gate, shared_up, shared_down.T], a...]
    all_to_all x1, waiting for transfers between devices: 0.01 us -> 39.4 us  [local(): lax.all_to_all(copies, 'mp', split_axis=0, concat_axis=0, tiled=True)]
    all_to_all x1 -> x0, blocking collectives: 20.3 us -> none  [local(): lax.all_to_all(jnp.concatenate([partial_value, gain_row], axis=1), 'mp',...]
    all_to_all x1, waiting for transfers between devices: 48.4 us -> 34.6 us  [local(): lax.all_to_all(partial_out, 'mp', split_axis=0, concat_axis=0, tiled=True)]
    all_to_all x1, waiting for transfers between devices: 0.01 us -> 12.7 us  [local(): lax.all_to_all(jnp.concatenate([partial_value, gain_row], axis=1), 'mp',...]
    dot_general x0 -> x1, matrix products: none -> 7.23 us  [local(): jnp.einsum('th,qfh->qtf', shared_act, shared_all[:, 2 * hidden_units:].re...]
  transfers between devices with their start and end apart: 9 -> 6, of which waited for: 7 -> 5; matrix products, arithmetic and copies ran while one was open for 8% -> 15% of each run, Pallas kernels for 0% -> 11%
where the time goes in v8:
time: 325 us; the launch traced here: 324 us
  waiting for transfers between devices  123 us (38%)
  blocking collectives  67.2 us (21%)
  Pallas kernels  37.1 us (11%)
  matrix products  28.7 us (9%)
  starting transfers between devices  28 us (9%)
  local copies, waits for them, and re-layouts  17.2 us (5%)
  between operations  14.3 us (4%)
  other arithmetic  8.33 us (3%)
    all_to_all x1, waiting for transfers between devices, local(): lax.all_to_all(copies, 'mp', split_axis=0, concat_axis=0, tiled=True)  39.4 us
    all_to_all x1, blocking collectives, local(): lax.all_to_all(outgoing.reshape(experts, capacity, block_width), dp, spli...  38.1 us
    pallas_call x1, Pallas kernels, gather_g(): pl.pallas_call(functools.partial(_gather_kernel, n), out_shape=jax.ShapeD...  37.1 us
    all_to_all x1, waiting for transfers between devices, local(): lax.all_to_all(partial_out, 'mp', split_axis=0, concat_axis=0, tiled=True)  34.6 us
    all_to_all x1, waiting for transfers between devices, local(): lax.all_to_all(expert_out.reshape(experts, capacity, block_width), dp, sp...  28.1 us
    all_gather x1, blocking collectives, local(): lax.all_gather(hidden, 'mp', axis=1, tiled=True).astype(jnp.float32)  13.4 us
    all_to_all x1, waiting for transfers between devices, local(): lax.all_to_all(jnp.concatenate([partial_value, gain_row], axis=1), 'mp',...  12.7 us
    all_to_all x1, starting transfers between devices, local(): lax.all_to_all(expert_out.reshape(experts, capacity, block_width), dp, sp...  9.77 us
  transfers between devices with their start and end apart: 6, of which 5 were waited for; matrix products, arithmetic and copies ran while one was open for 15% of the time, Pallas kernels for 11%

profile of v8, /device:TPU:8, one launch (start us, length us, event | category | flops | bytes accessed | tf_op | source)
XLA Modules:
  0.0 324.1 jit_solution(16200832378835494206)
XLA Ops:
  7.2 1.6 concatenate.7
  8.8 37.1 %shard_map.149 = bf16[1024,512]{1,0:T(8,128)(2,1)} custom-call(bf16[32,512]{1,0:T(8,128)(2,1)} %bitcast.79), custom_call_target="tpu_custom_call" | custom-call | tf_op jit(solution)/shard_map/pallas_call | solution.py:66
  45.9 2.2 all_gather.9
  48.1 1.7 fusion.57
  49.8 0.3 copy.55
  50.2 4.6 %all_to_all.35 = f32[2,128,1024]{1,2,0:T(8,128)S(1)} all-to-all(f32[2,128,1024]{1,2,0:T(8,128)S(1)} %copy.55), channel_id=1, replica_groups=mesh['g'=32,'c'=2,'mp'=4] {'c'}, dimensions={0} | all-to-all | bytes 2097152 | tf_op jit(solution)/shard_map/all_to_all | solution.py:81
  54.7 0.1 copy.56
  54.8 0.1 broadcast_in_dim.14
  55.0 0.1 pad_maximum_fusion
  55.1 1.6 copy.57
  56.7 4.4 %all-to-all-start.1 = ((f32[4,129,512]{2,1,0:T(8,128)}), f32[4,129,512]{2,1,0:T(8,128)S(1)}, u32[]{:S(2)}, u32[]{:S(2)}) async-start(f32[4,129,512]{2,1,0:T(8,128)} %copy.57), calls=%async_computation.1 | async-start | bytes 2228224 | tf_op jit(solution)/shard_map/all_to_all | solution.py:126
  61.1 0.1 copy.62
  61.3 0.1 eq.43
  61.4 0.1 eq.39
  61.6 1.8 reduce-window.6
  63.4 0.3 slice_reduce_fusion.1
  63.7 0.1 select_reduce_fusion.1
  63.8 0.1 add.43
  64.0 0.5 fusion.4
  64.5 12.7 %all-to-all-done.1 = f32[4,129,512]{2,1,0:T(8,128)S(1)} async-done(((f32[4,129,512]{2,1,0:T(8,128)}), f32[4,129,512]{2,1,0:T(8,128)S(1)}, u32[]{:S(2)}, u32[]{:S(2)}) %all-to-all-start.1) | async-done | bytes 1056800 | tf_op jit(solution)/shard_map/all_to_all | solution.py:126
  77.4 13.4 %all_gather.11 = bf16[128,2048]{1,0:T(8,128)(2,1)S(1)} all-gather(bf16[128,512]{1,0:T(8,128)(2,1)S(1)} %add_convert_fusion), channel_id=1, replica_groups=mesh['g'=32,'c'=2,'mp'=4] {'mp'}, dimensions={1}, use_global_device_ids=true | all-gather | bytes 655360 | tf_op jit(solution)/shard_map/all_gather | solution.py:137
  90.8 0.2 fusion.28
  91.0 0.6 copy-done
  91.6 0.5 convolution_convert_fusion
  92.2 38.1 %all_to_all.36 = bf16[64,16,512]{2,1,0:T(8,128)(2,1)S(1)} all-to-all(bf16[64,16,512]{2,1,0:T(8,128)(2,1)S(1)} %bitcast.75), channel_id=1, replica_groups=mesh['g'=32,'c'=2,'mp'=4] {'g','c'}, dimensions={0} | all-to-all | bytes 2097152 | tf_op jit(solution)/shard_map/all_to_all | solution.py:157
  130.2 2.3 broadcast_in_dim.22
  132.6 5.2 %all-to-all-start.4 = ((bf16[4,1024,512]{2,1,0:T(8,128)(2,1)}), bf16[4,1024,512]{2,1,0:T(8,128)(2,1)}, u32[]{:S(2)}, u32[]{:S(2)}) async-start(bf16[4,1024,512]{2,1,0:T(8,128)(2,1)} %broadcast_in_dim.22), calls=%async_computation.4 | async-start | bytes 8388608 | tf_op jit(solution)/shard_map/all_to_all | solution.py:165
  137.8 2.0 reshape_squeeze.9
  139.8 4.5 %reshape_squeeze.10 = bf16[4,512,352]{1,0,2:T(4,128)(2,1)} reshape(bf16[1,2048,352]{1,2,0:T(8,128)(2,1)} %param.22) | data formatting | bytes 2883584 | tf_op jit(solution)/shard_map/reshape;squeeze | solution.py:167
  144.3 2.0 reshape_squeeze.11
  146.3 39.4 %all-to-all-done.4 = bf16[4,1024,512]{2,1,0:T(8,128)(2,1)} async-done(((bf16[4,1024,512]{2,1,0:T(8,128)(2,1)}), bf16[4,1024,512]{2,1,0:T(8,128)(2,1)}, u32[]{:S(2)}, u32[]{:S(2)}) %all-to-all-start.4) | async-done | bytes 4194336 | tf_op jit(solution)/shard_map/all_to_all | solution.py:165
  185.7 5.4 %convolution_bitcast_fusion.1 = f32[1024,352]{0,1:T(8,128)} fusion(bf16[4,1024,512]{2,1,0:T(8,128)(2,1)} %all-to-all-done.4, bf16[4,512,352]{1,0,2:T(4,128)(2,1)} %reshape_squeeze.9), kind=kOutput, calls=%fused_computation.12 | convolution fusion | flops 1476395008 | bytes 7077888 | tf_op jit(solution)/shard_map/qsf,qfh->sh/dot_general | solution.py:168
  191.1 9.0 %convert_bitcast_fusion = bf16[4,1024,512]{2,1,0:T(8,128)(2,1)} fusion(bf16[352,4,512]{2,1,0:T(4,128)(2,1)} %reshape_squeeze.11, bf16[4,1024,512]{2,1,0:T(8,128)(2,1)} %all-to-all-done.4, bf16[4,512,352]{1,0,2:T(4,128)(2,1)S(1)} %copy-done.4, f32[1024,352]{0,1:T(8,128)} %convolution_bitcast_fusion.1), kind=kOutput, calls=%fused_computation | convolution fusion | flops 2957049856 | bytes 12713984 | tf_op jit(solution)/shard_map/sh,hqf->qsf/dot_general | solution.py:172
  200.2 5.1 %all-to-all-start.5 = ((bf16[4,1024,512]{2,1,0:T(8,128)(2,1)}), bf16[4,1024,512]{2,1,0:T(8,128)(2,1)}, u32[]{:S(2)}, u32[]{:S(2)}) async-start(bf16[4,1024,512]{2,1,0:T(8,128)(2,1)} %convert_bitcast_fusion), calls=%async_computation.5 | async-start | bytes 8388608 | tf_op jit(solution)/shard_map/all_to_all | solution.py:175
  205.3 1.0 copy-done.1
  206.4 4.1 %fusion.2 = f32[128,704]{0,1:T(8,128)} fusion(bf16[2048,2112]{1,0:T(8,128)(2,1)} %all-gather.2.cloned.1.call-done, bf16[128,2048]{1,0:T(8,128)(2,1)S(1)} %copy-done.1, f32[2048]{0:T(1024)S(1)} %bitcast.81, f32[128]{0:T(128)S(1)} %add_rsqrt_fusion.1), kind=kOutput, calls=%fused_computation.3 | convolution fusion | flops 370147328 | bytes 4039168 | tf_op jit(solution)/shard_map/dot_general | solution.py:19
  210.5 7.2 %convolution_bitcast_fusion.2 = f32[4,128,512]{1,2,0:T(8,128)} fusion(bf16[4,512,704]{2,1,0:T(8,128)(2,1)S(1)} %bitcast.77, bf16[2048,2112]{1,0:T(8,128)(2,1)} %all-gather.2.cloned.1.call-done, f32[128,704]{0,1:T(8,128)} %fusion.2, bf16[128,2048]{1,0:T(8,128)(2,1)} %copy-done, f32[2048]{0:T(1024)S(1)} %bitcast.82, f32[128]{0:T(128)S(1)} %add_rsqrt_fusion.1), kind=kOutput, calls=%fused_computation.17 | convolution fusion | flops 739786752 | bytes 7971328 | tf_op jit(solution)/shard_map/th,qfh->qtf/dot_general | solution.py:198
  217.7 34.6 %all-to-all-done.5 = bf16[4,1024,512]{2,1,0:T(8,128)(2,1)} async-done(((bf16[4,1024,512]{2,1,0:T(8,128)(2,1)}), bf16[4,1024,512]{2,1,0:T(8,128)(2,1)}, u32[]{:S(2)}, u32[]{:S(2)}) %all-to-all-start.5) | async-done | bytes 4194336 | tf_op jit(solution)/shard_map/all_to_all | solution.py:175
  252.3 3.5 %all-to-all-start.2 = ((f32[4,128,512]{1,2,0:T(8,128)}), f32[4,128,512]{1,2,0:T(8,128)S(1)}, u32[]{:S(2)}, u32[]{:S(2)}) async-start(f32[4,128,512]{1,2,0:T(8,128)} %convolution_bitcast_fusion.2), calls=%async_computation.2 | async-start | bytes 2097152 | tf_op jit(solution)/shard_map/all_to_all | solution.py:77
  255.8 4.1 %reduce_sum.81 = bf16[1024,512]{1,0:T(8,128)(2,1)} reduce(bf16[4,1024,512]{2,1,0:T(8,128)(2,1)} %all-to-all-done.5, bf16[]{:T(256)} %constant.25.clone.1), dimensions={0}, to_apply=%region_9.10 | reduce | flops 1572864 | bytes 5242882 | tf_op jit(solution)/shard_map/reduce_sum | solution.py:176
  259.9 8.4 %all-to-all-done.2 = f32[4,128,512]{1,2,0:T(8,128)S(1)} async-done(((f32[4,128,512]{1,2,0:T(8,128)}), f32[4,128,512]{1,2,0:T(8,128)S(1)}, u32[]{:S(2)}, u32[]{:S(2)}) %all-to-all-start.2) | async-done | bytes 1048608 | tf_op jit(solution)/shard_map/all_to_all | solution.py:77
  268.3 9.8 %all-to-all-start.6 = ((bf16[64,16,512]{2,1,0:T(8,128)(2,1)}), bf16[64,16,512]{2,1,0:T(8,128)(2,1)S(1)}, u32[]{:S(2)}, u32[]{:S(2)}) async-start(bf16[64,16,512]{2,1,0:T(8,128)(2,1)} %bitcast.18), calls=%async_computation.6 | async-start | bytes 2097152 | tf_op jit(solution)/shard_map/all_to_all | solution.py:177
  278.1 0.4 select_reduce_fusion
  278.6 0.1 copy.69
  278.7 28.1 %all-to-all-done.6 = bf16[64,16,512]{2,1,0:T(8,128)(2,1)S(1)} async-done(((bf16[64,16,512]{2,1,0:T(8,128)(2,1)}), bf16[64,16,512]{2,1,0:T(8,128)(2,1)S(1)}, u32[]{:S(2)}, u32[]{:S(2)}) %all-to-all-start.6) | async-done | bytes 1048608 | tf_op jit(solution)/shard_map/all_to_all | solution.py:177
  306.9 0.7 fusion.41
  307.6 8.9 %psum.7 = f32[128]{0:T(128)S(1)} all-reduce(f32[128]{0:T(128)S(1)} %get-tuple-element.4), channel_id=1, replica_groups=mesh['g'=32,'c'=2,'mp'=4] {'mp'}, use_global_device_ids=true, to_apply=%region_11.12 | all-reduce | flops 128 | bytes 1024 | tf_op jit(solution)/shard_map/psum | solution.py:207
  316.5 0.8 fusion.43
  (37 shorter events, 0.4 us)
Async XLA Ops:
  7.2 198.1 %all-gather.2.cloned.1.call-start = ((), (), s32[]{:S(2)}) async-start(), calls=%async_computation.7 | async-start | bytes 9052160 | tf_op jit(solution)/shard_map/all_gather | solution.py:192
  50.1 4.7 %copy-start.7 = (f32[512]{0:T(512)S(1)}, f32[512]{0:T(512)}, u32[]{:S(2)}) copy-start(f32[512]{0:T(512)} %param.17) | copy-start | bytes 6148
  55.1 6.0 %copy-start.9 = (s32[128,6]{0,1:T(8,128)S(1)}, s32[128,6]{0,1:T(8,128)}, u32[]{:S(2)}) copy-start(s32[128,6]{0,1:T(8,128)} %param.24) | copy-start | bytes 9220
  56.7 7.0 %copy-start.11 = (s32[64]{0:T(128)S(1)}, s32[64]{0:T(128)}, u32[]{:S(2)}) copy-start(s32[64]{0:T(128)} %param.26) | copy-start | bytes 772
  56.7 20.6 %copy-start.6 = (bf16[128,512]{1,0:T(8,128)(2,1)S(1)}, bf16[128,512]{1,0:T(8,128)(2,1)}, u32[]{:S(2)}) copy-start(bf16[128,512]{1,0:T(8,128)(2,1)} %param.15) | copy-start | bytes 393220
  56.7 20.5 %all-to-all-start.1 = ((f32[4,129,512]{2,1,0:T(8,128)}), f32[4,129,512]{2,1,0:T(8,128)S(1)}, u32[]{:S(2)}, u32[]{:S(2)}) async-start(f32[4,129,512]{2,1,0:T(8,128)} %copy.57), calls=%async_computation.1 | async-start | bytes 2228224 | tf_op jit(solution)/shard_map/all_to_all | solution.py:126
  90.8 0.8 copy-start
  132.6 5.2 %copy-start.2 = (bf16[1,2048,352]{1,2,0:T(8,128)(2,1)S(1)}, bf16[1,2048,352]{1,2,0:T(8,128)(2,1)}, u32[]{:S(2)}) copy-start(bf16[1,2048,352]{1,2,0:T(8,128)(2,1)} %param.21) | copy-start | bytes 4325380
  132.6 53.2 %all-to-all-start.4 = ((bf16[4,1024,512]{2,1,0:T(8,128)(2,1)}), bf16[4,1024,512]{2,1,0:T(8,128)(2,1)}, u32[]{:S(2)}, u32[]{:S(2)}) async-start(bf16[4,1024,512]{2,1,0:T(8,128)(2,1)} %broadcast_in_dim.22), calls=%async_computation.4 | async-start | bytes 8388608 | tf_op jit(solution)/shard_map/all_to_all | solution.py:165
  139.8 4.5 %copy-start.3 = (bf16[1,352,2048]{2,1,0:T(8,128)(2,1)S(1)}, bf16[1,352,2048]{2,1,0:T(8,128)(2,1)}, u32[]{:S(2)}) copy-start(bf16[1,352,2048]{2,1,0:T(8,128)(2,1)} %param.23) | copy-start | bytes 4325380
  146.3 44.9 %copy-start.4 = (bf16[4,512,352]{1,0,2:T(4,128)(2,1)S(1)}, bf16[4,512,352]{1,0,2:T(4,128)(2,1)}, u32[]{:S(2)}) copy-start(bf16[4,512,352]{1,0,2:T(4,128)(2,1)} %reshape_squeeze.10) | copy-start | bytes 4325380
  200.2 52.1 %all-to-all-start.5 = ((bf16[4,1024,512]{2,1,0:T(8,128)(2,1)}), bf16[4,1024,512]{2,1,0:T(8,128)(2,1)}, u32[]{:S(2)}, u32[]{:S(2)}) async-start(bf16[4,1024,512]{2,1,0:T(8,128)(2,1)} %convert_bitcast_fusion), calls=%async_computation.5 | async-start | bytes 8388608 | tf_op jit(solution)/shard_map/all_to_all | solution.py:175
  205.3 1.0 copy-start.1
  206.3 4.1 %slice-start = ((bf16[2048,2112]{1,0:T(8,128)(2,1)}), bf16[2048,704]{1,0:T(8,128)(2,1)S(1)}, s32[]{:S(2)}) async-start(bf16[2048,2112]{1,0:T(8,128)(2,1)} %all-gather.2.cloned.1.call-done), calls=%async_computation.8 | async-start | bytes 6291456 | tf_op jit(solution)/shard_map/slice | solution.py:201
  252.3 16.0 %all-to-all-start.2 = ((f32[4,128,512]{1,2,0:T(8,128)}), f32[4,128,512]{1,2,0:T(8,128)S(1)}, u32[]{:S(2)}, u32[]{:S(2)}) async-start(f32[4,128,512]{1,2,0:T(8,128)} %convolution_bitcast_fusion.2), calls=%async_computation.2 | async-start | bytes 2097152 | tf_op jit(solution)/shard_map/all_to_all | solution.py:77
  259.9 18.1 %copy-start.8 = (f32[128,6]{0,1:T(8,128)S(1)}, f32[128,6]{0,1:T(8,128)}, u32[]{:S(2)}) copy-start(f32[128,6]{0,1:T(8,128)} %param.25) | copy-start | bytes 9220
  268.3 38.6 %all-to-all-start.6 = ((bf16[64,16,512]{2,1,0:T(8,128)(2,1)}), bf16[64,16,512]{2,1,0:T(8,128)(2,1)S(1)}, u32[]{:S(2)}, u32[]{:S(2)}) async-start(bf16[64,16,512]{2,1,0:T(8,128)(2,1)} %bitcast.18), calls=%async_computation.6 | async-start | bytes 2097152 | tf_op jit(solution)/shard_map/all_to_all | solution.py:177
  278.5 38.0 %copy-start.10 = (f32[512]{0:T(512)S(1)}, f32[512]{0:T(512)}, u32[]{:S(2)}) copy-start(f32[512]{0:T(512)} %param.27) | copy-start | bytes 6148
  307.6 9.7 %copy-start.5 = (bf16[128,512]{1,0:T(8,128)(2,1)}, bf16[128,512]{1,0:T(8,128)(2,1)S(1)}, u32[]{:S(2)}) copy-start(bf16[128,512]{1,0:T(8,128)(2,1)S(1)} %get-tuple-element.5) | copy-start | bytes 393220
Sparse Core Ops, SparseCore 0:
  10.7 87.1 all-gather.1

commit v9 on v8

--- a/solution.py
+++ b/solution.py
@@ -138,7 +138,6 @@
     squares = jnp.sum(whole_hidden * whole_hidden, axis=1)
     scale = lax.rsqrt(squares / model_width + EPSILON)[:, None]
     whole_rows = (whole_hidden * scale * gain).astype(jnp.bfloat16)
-    normed = (hidden_float * scale * ffn_gain).astype(jnp.bfloat16)
 
     flat_ids = route_ids.reshape(-1)
     expert_iota = jnp.arange(experts, dtype=jnp.int32)
@@ -153,34 +152,25 @@
     flat_scores = route_scores.reshape(tok_rows, top_count)
     combine = jnp.sum(jnp.where(hit, flat_scores[:, :, None], 0.0), axis=1)
     pick = jnp.any(hit, axis=1).astype(jnp.bfloat16)
-    outgoing = matmul(pick.T, normed).astype(jnp.bfloat16)
-    arrived = lax.all_to_all(
-        outgoing.reshape(experts, capacity, block_width),
+    outgoing = matmul(pick.T, whole_rows).astype(jnp.bfloat16)
+    in_rows = lax.all_to_all(
+        outgoing.reshape(experts, capacity, model_width),
         dp,
         split_axis=0,
         concat_axis=0,
         tiled=True,
-    ).reshape(slots, block_width)
-    copies = jnp.broadcast_to(arrived[None], (mp_count, slots, block_width))
-    in_rows = lax.all_to_all(copies, "mp", split_axis=0, concat_axis=0, tiled=True)
-    gate_block = expert_gate[0].reshape(mp_count, block_width, -1)
-    up_block = expert_up[0].reshape(mp_count, block_width, -1)
-    gate_val = jnp.einsum("qsf,qfh->sh", in_rows, gate_block, preferred_element_type=jnp.float32)
-    up_val = jnp.einsum("qsf,qfh->sh", in_rows, up_block, preferred_element_type=jnp.float32)
+    ).reshape(slots, model_width)
+    gate_val = matmul(in_rows, expert_gate[0])
+    up_val = matmul(in_rows, expert_up[0])
     activated = (jax.nn.silu(gate_val) * up_val).astype(jnp.bfloat16)
-    down_block = expert_down[0].reshape(-1, mp_count, block_width)
-    partial_out = jnp.einsum(
-        "sh,hqf->qsf", activated, down_block, preferred_element_type=jnp.float32
-    ).astype(jnp.bfloat16)
-    summed = lax.all_to_all(partial_out, "mp", split_axis=0, concat_axis=0, tiled=True)
-    expert_out = jnp.sum(summed.astype(jnp.float32), axis=0).astype(jnp.bfloat16)
+    partial_out = matmul(activated, expert_down[0]).astype(jnp.bfloat16)
     returned = lax.all_to_all(
-        expert_out.reshape(experts, capacity, block_width),
+        partial_out.reshape(experts, capacity, model_width),
         dp,
         split_axis=0,
         concat_axis=0,
         tiled=True,
-    ).reshape(slots, block_width)
+    ).reshape(slots, model_width)
     routed = jnp.dot(
         combine,
         returned.astype(jnp.float32),
@@ -201,7 +191,8 @@
         shared_all[:, 2 * hidden_units :].reshape(mp_count, block_width, hidden_units),
         preferred_element_type=jnp.float32,
     )
-    mixture = reduce_scatter_mp(shared_part) + routed
+    routed_blocks = jnp.transpose(routed.reshape(tok_rows, mp_count, block_width), (1, 0, 2))
+    mixture = reduce_scatter_mp(shared_part + routed_blocks)
     final = (hidden_float + mixture).astype(jnp.bfloat16)
     final_float = final.astype(jnp.float32)
     final_squares = lax.psum(jnp.sum(final_float * final_float, axis=1), "mp")

time: 325 us -> 361 us (1.11)
  blocking collectives: 67.2 us -> 151 us
  waiting for transfers between devices: 123 us -> 92 us
  starting transfers between devices: 28 us -> 10.2 us
  other arithmetic: 8.33 us -> 3.76 us
    all_to_all x1 -> x2, blocking collectives: 38.1 us -> 122 us  [the longest x1 106 us: local(): lax.all_to_all(outgoing.reshape(experts, capacity, model_width), dp, spli...]
    all_to_all x4 -> x1, waiting for transfers between devices: 111 us -> 80.3 us  [local(): lax.all_to_all(partial_out.reshape(experts, capacity, model_width), dp, s...]
    all_to_all x4 -> x1, starting transfers between devices: 23.5 us -> 5.89 us  [local(): lax.all_to_all(partial_out.reshape(experts, capacity, model_width), dp, s...]
    dot_general x2 -> x0, matrix products: 14.5 us -> none  [the longest x1 9.04 us: local(): jnp.einsum('sh,hqf->qsf', activated, down_block, preferred_element_type=j...]
    dot_general x2 -> x4, matrix products: 4.63 us -> 16.6 us  [matmul(): return jnp.dot(left, right, preferred_element_type=jnp.float32)]
    another operation x3 -> x0, local copies, waits for them, and re-layouts: 8.5 us -> none  [the longest x1 4.51 us: local(): up_block = expert_up[0].reshape(mp_count, block_width, -1)]
    reshape x0 -> x1, local copies, waits for them, and re-layouts: none -> 6.49 us  [local(): returned = lax.all_to_all(partial_out.reshape(experts, capacity, model_wi...]
    dot_general x1, matrix products: 0.69 us -> 5.32 us  [local(): jnp.dot(combine, returned.astype(jnp.float32), precision=lax.Precision.HI...]
  transfers between devices with their start and end apart: 6 -> 3, of which waited for: 5 -> 2; matrix products, arithmetic and copies ran while one was open for 15% -> 11% of each run, Pallas kernels for 11% -> 10%
where the time goes in v9:
time: 361 us; the launch traced here: 360 us
  blocking collectives  151 us (42%)
  waiting for transfers between devices  92 us (25%)
  Pallas kernels  37.4 us (10%)
  matrix products  31.9 us (9%)
  local copies, waits for them, and re-layouts  19.6 us (5%)
  between operations  14.3 us (4%)
  starting transfers between devices  10.2 us (3%)
  other arithmetic  3.76 us (1%)
    all_to_all x1, blocking collectives, local(): lax.all_to_all(outgoing.reshape(experts, capacity, model_width), dp, spli...  106 us
    all_to_all x1, waiting for transfers between devices, local(): lax.all_to_all(partial_out.reshape(experts, capacity, model_width), dp, s...  80.3 us
    pallas_call x1, Pallas kernels, gather_g(): pl.pallas_call(functools.partial(_gather_kernel, n), out_shape=jax.ShapeD...  37.4 us
    dot_general x4, matrix products, matmul(): return jnp.dot(left, right, preferred_element_type=jnp.float32)  16.6 us
    all_to_all x1, blocking collectives, reduce_scatter_mp(): lax.all_to_all(blocks, 'mp', split_axis=0, concat_axis=0, tiled=True)  15.7 us
    all_gather x1, blocking collectives, local(): lax.all_gather(hidden, 'mp', axis=1, tiled=True).astype(jnp.float32)  13.4 us
    all_to_all x1, waiting for transfers between devices, local(): lax.all_to_all(jnp.concatenate([partial_value, gain_row], axis=1), 'mp',...  11.7 us
    psum x1, blocking collectives, local(): final_squares = lax.psum(jnp.sum(final_float * final_float, axis=1), 'mp')  8.89 us
  transfers between devices with their start and end apart: 3, of which 2 were waited for; matrix products, arithmetic and copies ran while one was open for 11% of the time, Pallas kernels for 10%

profile of v9, /device:TPU:8, one launch (start us, length us, event | category | flops | bytes accessed | tf_op | source)
XLA Modules:
  0.0 360.0 jit_solution(3933049754592116292)
XLA Ops:
  7.2 0.0 all-gather.2.cloned.1.call-start
  7.2 1.7 concatenate.7
  9.0 2.2 all_gather.9
  11.2 37.4 %shard_map.149 = bf16[1024,512]{1,0:T(8,128)(2,1)} custom-call(bf16[32,512]{1,0:T(8,128)(2,1)} %bitcast.83), custom_call_target="tpu_custom_call" | custom-call | tf_op jit(solution)/shard_map/pallas_call | solution.py:66
  48.6 1.7 fusion.51
  50.3 0.3 copy.55
  50.6 4.6 %all_to_all.25 = f32[2,128,1024]{1,2,0:T(8,128)S(1)} all-to-all(f32[2,128,1024]{1,2,0:T(8,128)S(1)} %copy.55), channel_id=1, replica_groups=mesh['g'=32,'c'=2,'mp'=4] {'c'}, dimensions={0} | all-to-all | bytes 2097152 | tf_op jit(solution)/shard_map/all_to_all | solution.py:81
  55.2 0.1 copy.56
  55.3 0.1 broadcast_in_dim.10
  55.5 0.1 pad_maximum_fusion
  55.6 1.6 copy.57
  57.2 4.3 %all-to-all-start.1 = ((f32[4,129,512]{2,1,0:T(8,128)}), f32[4,129,512]{2,1,0:T(8,128)S(1)}, u32[]{:S(2)}, u32[]{:S(2)}) async-start(f32[4,129,512]{2,1,0:T(8,128)} %copy.57), calls=%async_computation.1 | async-start | bytes 2228224 | tf_op jit(solution)/shard_map/all_to_all | solution.py:126
  61.5 0.1 copy.61
  61.6 0.1 eq.43
  61.7 0.1 eq.39
  61.9 1.0 copy.54
  62.9 1.8 reduce-window.6
  64.7 0.3 slice_reduce_fusion.1
  65.0 0.1 select_reduce_fusion.1
  65.2 0.1 add.43
  65.3 0.1 copy.64
  65.4 0.5 fusion.4
  65.9 11.7 %all-to-all-done.1 = f32[4,129,512]{2,1,0:T(8,128)S(1)} async-done(((f32[4,129,512]{2,1,0:T(8,128)}), f32[4,129,512]{2,1,0:T(8,128)S(1)}, u32[]{:S(2)}, u32[]{:S(2)}) %all-to-all-start.1) | async-done | bytes 1056800 | tf_op jit(solution)/shard_map/all_to_all | solution.py:126
  77.6 0.1 slice_reduce_fusion
  77.7 0.1 copy.72
  77.8 13.4 %all_gather.11 = bf16[128,2048]{0,1:T(8,128)(2,1)S(1)} all-gather(bf16[128,512]{0,1:T(8,128)(2,1)S(1)} %add_convert_fusion.1), channel_id=1, replica_groups=mesh['g'=32,'c'=2,'mp'=4] {'mp'}, dimensions={1}, use_global_device_ids=true | all-gather | bytes 655360 | tf_op jit(solution)/shard_map/all_gather | solution.py:137
  91.3 0.3 fusion.24
  91.6 1.4 convolution_convert_fusion.1
  93.0 105.9 %all_to_all.26 = bf16[64,16,2048]{2,1,0:T(8,128)(2,1)S(1)} all-to-all(bf16[64,16,2048]{2,1,0:T(8,128)(2,1)S(1)} %bitcast.70), channel_id=1, replica_groups=mesh['g'=32,'c'=2,'mp'=4] {'g','c'}, dimensions={0} | all-to-all | bytes 8388608 | tf_op jit(solution)/shard_map/all_to_all | solution.py:156
  198.9 1.9 copy-done.1
  200.9 2.8 fusion.7
  203.7 9.0 %convolution_convert_fusion = bf16[1024,2048]{1,0:T(8,128)(2,1)} fusion(bf16[1,352,2048]{2,1,0:T(8,128)(2,1)S(1)} %copy-done, bf16[1024,2048]{1,0:T(8,128)(2,1)} %bitcast.74, bf16[1,2048,352]{1,2,0:T(8,128)(2,1)} %param.22, f32[1024,352]{0,1:T(8,128)} %fusion.7), kind=kOutput, calls=%fused_computation | convolution fusion | flops 2957049856 | bytes 12713984 | tf_op jit(solution)/shard_map/dot_general | solution.py:19
  212.7 5.9 %all-to-all-start.3 = ((bf16[64,16,2048]{2,1,0:T(8,128)(2,1)}), bf16[64,16,2048]{2,1,0:T(8,128)(2,1)}, u32[]{:S(2)}, u32[]{:S(2)}) async-start(bf16[64,16,2048]{2,1,0:T(8,128)(2,1)} %bitcast.72), calls=%async_computation.3 | async-start | bytes 8388608 | tf_op jit(solution)/shard_map/all_to_all | solution.py:167
  218.6 0.4 select_reduce_fusion
  219.0 0.0 all-gather.2.cloned.1.call-done
  219.0 3.7 %slice.29 = bf16[2048,704]{1,0:T(8,128)(2,1)} slice(bf16[2048,2112]{1,0:T(8,128)(2,1)} %all-gather.2.cloned.1.call-done), slice={[0:2048], [1408:2112]} | slice | bytes 5767168 | tf_op jit(solution)/shard_map/slice | solution.py:191
  222.8 3.4 fusion.2
  226.2 8.3 %convolution_bitcast_fusion.1 = f32[4,128,512]{1,2,0:T(8,128)} fusion(bf16[4,512,704]{2,1,0:T(8,128)(2,1)} %bitcast.78, bf16[2048,2112]{1,0:T(8,128)(2,1)} %all-gather.2.cloned.1.call-done, f32[128,704]{0,1:T(8,128)S(1)} %fusion.2, bf16[128,2048]{0,1:T(8,128)(2,1)S(1)} %all_gather.11, f32[2048]{0:T(1024)S(1)} %bitcast.82, f32[128]{0:T(128)S(1)} %add_rsqrt_fusion.1), kind=kOutput, calls=%fused_computation.18 | convolution fusion | flops 739786752 | bytes 8233472 | tf_op jit(solution)/shard_map/th,qfh->qtf/dot_general | solution.py:188
  234.5 80.3 %all-to-all-done.3 = bf16[64,16,2048]{2,1,0:T(8,128)(2,1)} async-done(((bf16[64,16,2048]{2,1,0:T(8,128)(2,1)}), bf16[64,16,2048]{2,1,0:T(8,128)(2,1)}, u32[]{:S(2)}, u32[]{:S(2)}) %all-to-all-start.3) | async-done | bytes 4194336 | tf_op jit(solution)/shard_map/all_to_all | solution.py:167
  314.8 6.5 %copy.65 = bf16[1024,2048]{0,1:T(8,128)(2,1)} copy(bf16[1024,2048]{1,0:T(8,128)(2,1)} %bitcast.19) | data formatting | bytes 8388608 | tf_op jit(solution)/shard_map/reshape | solution.py:173
  321.3 5.3 %fusion.12 = f32[4,128,512]{1,2,0:T(8,128)S(1)} fusion(f32[4,128,512]{1,2,0:T(8,128)S(1)} %copy-done.2, bf16[4,512,1024]{2,1,0:T(8,128)(2,1)} %bitcast.71, f32[128,1024]{1,0:T(8,128)S(1)} %select_reduce_fusion), kind=kOutput, calls=%fused_computation.17 | convolution fusion | flops 3221487616 | bytes 6815744 | tf_op jit(solution)/shard_map/dot_general | solution.py:174
  326.6 15.7 %all_to_all.27 = f32[4,128,512]{1,2,0:T(8,128)S(1)} all-to-all(f32[4,128,512]{1,2,0:T(8,128)S(1)} %fusion.12), channel_id=1, replica_groups=mesh['g'=32,'c'=2,'mp'=4] {'mp'}, dimensions={0} | all-to-all | bytes 2097152 | tf_op jit(solution)/shard_map/all_to_all | solution.py:77
  342.4 0.1 reduce_sum.68
  342.4 0.1 fusion.36
  342.5 8.9 %psum.7 = f32[128]{0:T(128)S(1)} all-reduce(f32[128]{0:T(128)S(1)} %get-tuple-element.8), channel_id=1, replica_groups=mesh['g'=32,'c'=2,'mp'=4] {'mp'}, use_global_device_ids=true, to_apply=%region_10.11 | all-reduce | flops 128 | bytes 1024 | tf_op jit(solution)/shard_map/psum | solution.py:198
  351.4 0.8 copy.67
  352.2 0.1 fusion.38
  352.3 0.8 copy.68
  (25 shorter events, 0.2 us)
Async XLA Ops:
  7.2 196.5 %copy-start = (bf16[1,352,2048]{2,1,0:T(8,128)(2,1)S(1)}, bf16[1,352,2048]{2,1,0:T(8,128)(2,1)}, u32[]{:S(2)}) copy-start(bf16[1,352,2048]{2,1,0:T(8,128)(2,1)} %param.23) | copy-start | bytes 4325380
  7.2 211.9 %all-gather.2.cloned.1.call-start = ((), (), s32[]{:S(2)}) async-start(), calls=%async_computation.5 | async-start | bytes 9052160 | tf_op jit(solution)/shard_map/all_gather | solution.py:182
  50.3 5.0 %copy-start.5 = (f32[512]{0:T(512)S(1)}, f32[512]{0:T(512)}, u32[]{:S(2)}) copy-start(f32[512]{0:T(512)} %param.17) | copy-start | bytes 6148
  55.6 5.9 %copy-start.4 = (s32[128,6]{0,1:T(8,128)S(1)}, s32[128,6]{0,1:T(8,128)}, u32[]{:S(2)}) copy-start(s32[128,6]{0,1:T(8,128)} %param.24) | copy-start | bytes 9220
  55.6 9.4 %copy-start.7 = (s32[64]{0:T(128)S(1)}, s32[64]{0:T(128)}, u32[]{:S(2)}) copy-start(s32[64]{0:T(128)} %param.26) | copy-start | bytes 772
  57.2 20.4 %all-to-all-start.1 = ((f32[4,129,512]{2,1,0:T(8,128)}), f32[4,129,512]{2,1,0:T(8,128)S(1)}, u32[]{:S(2)}, u32[]{:S(2)}) async-start(f32[4,129,512]{2,1,0:T(8,128)} %copy.57), calls=%async_computation.1 | async-start | bytes 2228224 | tf_op jit(solution)/shard_map/all_to_all | solution.py:126
  93.0 107.9 %copy-start.8 = (bf16[1,2048,352]{1,2,0:T(8,128)(2,1)S(1)}, bf16[1,2048,352]{1,2,0:T(8,128)(2,1)}, u32[]{:S(2)}) copy-start(bf16[1,2048,352]{1,2,0:T(8,128)(2,1)} %param.21) | copy-start | bytes 4325380
  198.9 1.9 copy-start.1
  212.7 5.9 %copy-start.3 = (f32[128,6]{0,1:T(8,128)S(1)}, f32[128,6]{0,1:T(8,128)}, u32[]{:S(2)}) copy-start(f32[128,6]{0,1:T(8,128)} %param.25) | copy-start | bytes 9220
  212.7 102.1 %all-to-all-start.3 = ((bf16[64,16,2048]{2,1,0:T(8,128)(2,1)}), bf16[64,16,2048]{2,1,0:T(8,128)(2,1)}, u32[]{:S(2)}, u32[]{:S(2)}) async-start(bf16[64,16,2048]{2,1,0:T(8,128)(2,1)} %bitcast.72), calls=%async_computation.3 | async-start | bytes 8388608 | tf_op jit(solution)/shard_map/all_to_all | solution.py:167
  314.8 6.5 %copy-start.2 = (f32[4,128,512]{1,2,0:T(8,128)S(1)}, f32[4,128,512]{1,2,0:T(8,128)}, u32[]{:S(2)}) copy-start(f32[4,128,512]{1,2,0:T(8,128)} %convolution_bitcast_fusion.1) | copy-start | bytes 3145732
  326.6 25.6 %copy-start.6 = (f32[512]{0:T(512)S(1)}, f32[512]{0:T(512)}, u32[]{:S(2)}) copy-start(f32[512]{0:T(512)} %param.27) | copy-start | bytes 6148
Sparse Core Ops, SparseCore 0:
  10.8 88.3 all-gather.1

commit v10 on v8

--- a/solution.py
+++ b/solution.py
@@ -25,16 +25,20 @@
     )
 
 
-def _gather_kernel(n, x_ref, o_ref, send_sem, recv_sem):
-    me = lax.axis_index("g")
-    core = lax.axis_index("c")
-    col = lax.axis_index("mp")
+def _gather_kernel(axis, x_ref, o_ref, send_sem, recv_sem):
+    coords = {name: lax.axis_index(name) for name in ("g", "c", "mp")}
+    n = lax.axis_size(axis)
+    me = coords[axis]
     rows = x_ref.shape[0]
+
+    def device(peer):
+        return tuple(peer if name == axis else coords[name] for name in ("g", "c", "mp"))
+
     barrier = pltpu.get_barrier_semaphore()
 
     def greet(p, carry):
         peer = lax.rem(me + p, n)
-        pl.semaphore_signal(barrier, inc=1, device_id=(peer, core, col), device_id_type=MESH)
+        pl.semaphore_signal(barrier, inc=1, device_id=device(peer), device_id_type=MESH)
         return carry
 
     lax.fori_loop(1, n, greet, 0)
@@ -49,7 +53,7 @@
             dst_ref=own,
             send_sem=send_sem,
             recv_sem=recv_sem,
-            device_id=(peer, core, col),
+            device_id=device(peer),
             device_id_type=MESH,
         ).start()
         return carry
@@ -60,11 +64,11 @@
     pltpu.make_async_copy(o_ref, o_ref, recv_sem).wait()
 
 
-def gather_g(x, collective_id):
-    n = lax.axis_size("g")
+def gather_rows(x, axis, collective_id):
+    n = lax.axis_size(axis)
     rows, cols = x.shape
     return pl.pallas_call(
-        functools.partial(_gather_kernel, n),
+        functools.partial(_gather_kernel, axis),
         out_shape=jax.ShapeDtypeStruct((n * rows, cols), x.dtype),
         in_specs=[pl.BlockSpec(memory_space=pl.ANY)],
         out_specs=pl.BlockSpec(memory_space=pl.ANY),
@@ -118,7 +122,7 @@
     model_width = D
     block_width = model_width // mp_count
 
-    w_half = gather_g(out_weight.T, 0)
+    w_half = gather_rows(out_weight.T, "g", 0)
     att_pair = lax.all_gather(attention, "c", axis=0, tiled=True)
     part_half = matmul_t(att_pair, w_half)
     partial_value = natural_blocks(swap_halves(part_half, tok_rows), mp_count)
@@ -134,7 +138,9 @@
     gain = exchanged[:, tok_rows, :].reshape(model_width)
     hidden = (residual.astype(jnp.float32) + projected).astype(jnp.bfloat16)
     hidden_float = hidden.astype(jnp.float32)
-    whole_hidden = lax.all_gather(hidden, "mp", axis=1, tiled=True).astype(jnp.float32)
+    hidden_blocks = gather_rows(hidden, "mp", 1).reshape(mp_count, tok_rows, block_width)
+    whole_hidden = jnp.transpose(hidden_blocks, (1, 0, 2)).reshape(tok_rows, model_width)
+    whole_hidden = whole_hidden.astype(jnp.float32)
     squares = jnp.sum(whole_hidden * whole_hidden, axis=1)
     scale = lax.rsqrt(squares / model_width + EPSILON)[:, None]
     whole_rows = (whole_hidden * scale * gain).astype(jnp.bfloat16)
@@ -204,7 +210,11 @@
     mixture = reduce_scatter_mp(shared_part) + routed
     final = (hidden_float + mixture).astype(jnp.bfloat16)
     final_float = final.astype(jnp.float32)
-    final_squares = lax.psum(jnp.sum(final_float * final_float, axis=1), "mp")
+    own_squares = jnp.sum(final_float * final_float, axis=1)
+    square_rows = jnp.broadcast_to(own_squares[None, :], (8, tok_rows))
+    final_squares = jnp.sum(
+        gather_rows(square_rows, "mp", 2).reshape(mp_count, 8, tok_rows)[:, 0, :], axis=0
+    )
     next_normed = (
         final_float * lax.rsqrt(final_squares / model_width + EPSILON)[:, None] * next_gain
     ).astype(jnp.bfloat16)

time: 325 us -> 321 us (0.988)
  blocking collectives: 67.2 us -> 44.8 us
  Pallas kernels: 37.1 us -> 51.6 us
  other arithmetic: 8.33 us -> 12 us
    pallas_call x1 -> x3, Pallas kernels: 37.1 us -> 51.6 us  [gather_rows(): pl.pallas_call(functools.partial(_gather_kernel, axis), out_shape=jax.Sha...]
    all_gather x1 -> x0, blocking collectives: 13.4 us -> none  [local(): lax.all_gather(hidden, 'mp', axis=1, tiled=True).astype(jnp.float32)]
    psum x1 -> x0, blocking collectives: 8.9 us -> none  [local(): final_squares = lax.psum(jnp.sum(final_float * final_float, axis=1), 'mp')]
  transfers between devices with their start and end apart: 6 -> 6, of which waited for: 5 -> 5; matrix products, arithmetic and copies ran while one was open for 15% -> 16% of each run, Pallas kernels for 11% -> 14%
where the time goes in v10:
time: 321 us; the launch traced here: 320 us
  waiting for transfers between devices  123 us (38%)
  Pallas kernels  51.6 us (16%)
  blocking collectives  44.8 us (14%)
  matrix products  28.8 us (9%)
  starting transfers between devices  28.3 us (9%)
  local copies, waits for them, and re-layouts  17.4 us (5%)
  between operations  14.3 us (4%)
  other arithmetic  12 us (4%)
    pallas_call x3, Pallas kernels, gather_rows(): pl.pallas_call(functools.partial(_gather_kernel, axis), out_shape=jax.Sha...  51.6 us
    all_to_all x1, waiting for transfers between devices, local(): lax.all_to_all(copies, 'mp', split_axis=0, concat_axis=0, tiled=True)  39.4 us
    all_to_all x1, blocking collectives, local(): lax.all_to_all(outgoing.reshape(experts, capacity, block_width), dp, spli...  38 us
    all_to_all x1, waiting for transfers between devices, local(): lax.all_to_all(partial_out, 'mp', split_axis=0, concat_axis=0, tiled=True)  34 us
    all_to_all x1, waiting for transfers between devices, local(): lax.all_to_all(expert_out.reshape(experts, capacity, block_width), dp, sp...  28.1 us
    all_to_all x1, waiting for transfers between devices, local(): lax.all_to_all(jnp.concatenate([partial_value, gain_row], axis=1), 'mp',...  12.7 us
    all_to_all x1, starting transfers between devices, local(): lax.all_to_all(expert_out.reshape(experts, capacity, block_width), dp, sp...  9.89 us
    dot_general x1, matrix products, local(): jnp.einsum('sh,hqf->qsf', activated, down_block, preferred_element_type=j...  9.04 us
  transfers between devices with their start and end apart: 6, of which 5 were waited for; matrix products, arithmetic and copies ran while one was open for 16% of the time, Pallas kernels for 14%

profile of v10, /device:TPU:8, one launch (start us, length us, event | category | flops | bytes accessed | tf_op | source)
XLA Modules:
  0.0 319.9 jit_solution(11560662890725437567)
XLA Ops:
  7.2 1.6 concatenate.7
  8.8 37.1 %shard_map.149 = bf16[1024,512]{1,0:T(8,128)(2,1)} custom-call(bf16[32,512]{1,0:T(8,128)(2,1)} %bitcast.96), custom_call_target="tpu_custom_call" | custom-call | tf_op jit(solution)/shard_map/pallas_call | solution.py:70
  45.9 2.2 all_gather.6
  48.1 1.7 fusion.53
  49.8 0.3 copy.58
  50.2 4.6 %all_to_all.35 = f32[2,128,1024]{1,2,0:T(8,128)S(1)} all-to-all(f32[2,128,1024]{1,2,0:T(8,128)S(1)} %copy.58), channel_id=1, replica_groups=mesh['g'=32,'c'=2,'mp'=4] {'c'}, dimensions={0} | all-to-all | bytes 2097152 | tf_op jit(solution)/shard_map/all_to_all | solution.py:85
  54.8 0.1 broadcast_in_dim.20
  55.0 0.1 pad_maximum_fusion
  55.1 1.6 copy.60
  56.7 4.4 %all-to-all-start.1 = ((f32[4,129,512]{2,1,0:T(8,128)}), f32[4,129,512]{2,1,0:T(8,128)S(1)}, u32[]{:S(2)}, u32[]{:S(2)}) async-start(f32[4,129,512]{2,1,0:T(8,128)} %copy.60), calls=%async_computation.1 | async-start | bytes 2228224 | tf_op jit(solution)/shard_map/all_to_all | solution.py:130
  61.3 0.1 eq.43
  61.4 0.1 eq.39
  61.6 1.8 reduce-window.6
  63.4 0.3 slice_reduce_fusion.1
  63.7 0.1 select_reduce_fusion.1
  64.0 0.5 fusion.4
  64.5 12.7 %all-to-all-done.1 = f32[4,129,512]{2,1,0:T(8,128)S(1)} async-done(((f32[4,129,512]{2,1,0:T(8,128)}), f32[4,129,512]{2,1,0:T(8,128)S(1)}, u32[]{:S(2)}, u32[]{:S(2)}) %all-to-all-start.1) | async-done | bytes 1056800 | tf_op jit(solution)/shard_map/all_to_all | solution.py:130
  77.3 0.7 add_convert_fusion.x_ref
  78.0 9.0 %shard_map.150 = bf16[512,512]{1,0:T(8,128)(2,1)} custom-call(bf16[128,512]{1,0:T(8,128)(2,1)} %add_convert_fusion.x_ref), custom_call_target="tpu_custom_call" | custom-call | tf_op jit(solution)/shard_map/pallas_call | solution.py:70
  87.1 1.3 multiply_reduce_fusion
  88.3 1.4 convolution_convert_fusion
  89.8 38.0 %all_to_all.36 = bf16[64,16,512]{2,1,0:T(8,128)(2,1)S(1)} all-to-all(bf16[64,16,512]{2,1,0:T(8,128)(2,1)S(1)} %bitcast.91), channel_id=1, replica_groups=mesh['g'=32,'c'=2,'mp'=4] {'g','c'}, dimensions={0} | all-to-all | bytes 2097152 | tf_op jit(solution)/shard_map/all_to_all | solution.py:163
  127.8 2.3 broadcast_in_dim.24
  130.1 5.2 %all-to-all-start.4 = ((bf16[4,1024,512]{2,1,0:T(8,128)(2,1)}), bf16[4,1024,512]{2,1,0:T(8,128)(2,1)}, u32[]{:S(2)}, u32[]{:S(2)}) async-start(bf16[4,1024,512]{2,1,0:T(8,128)(2,1)} %broadcast_in_dim.24), calls=%async_computation.4 | async-start | bytes 8388608 | tf_op jit(solution)/shard_map/all_to_all | solution.py:171
  135.3 2.0 reshape_squeeze.9
  137.3 4.5 %reshape_squeeze.10 = bf16[4,512,352]{1,0,2:T(4,128)(2,1)} reshape(bf16[1,2048,352]{1,2,0:T(8,128)(2,1)} %param.22) | data formatting | bytes 2883584 | tf_op jit(solution)/shard_map/reshape;squeeze | solution.py:173
  141.8 2.0 reshape_squeeze.11
  143.8 39.4 %all-to-all-done.4 = bf16[4,1024,512]{2,1,0:T(8,128)(2,1)} async-done(((bf16[4,1024,512]{2,1,0:T(8,128)(2,1)}), bf16[4,1024,512]{2,1,0:T(8,128)(2,1)}, u32[]{:S(2)}, u32[]{:S(2)}) %all-to-all-start.4) | async-done | bytes 4194336 | tf_op jit(solution)/shard_map/all_to_all | solution.py:171
  183.3 5.4 %convolution_bitcast_fusion.1 = f32[1024,352]{0,1:T(8,128)} fusion(bf16[4,1024,512]{2,1,0:T(8,128)(2,1)} %all-to-all-done.4, bf16[4,512,352]{1,0,2:T(4,128)(2,1)} %reshape_squeeze.9), kind=kOutput, calls=%fused_computation.12 | convolution fusion | flops 1476395008 | bytes 7077888 | tf_op jit(solution)/shard_map/qsf,qfh->sh/dot_general | solution.py:174
  188.7 9.0 %convert_bitcast_fusion = bf16[4,1024,512]{2,1,0:T(8,128)(2,1)} fusion(bf16[352,4,512]{2,1,0:T(4,128)(2,1)} %reshape_squeeze.11, bf16[4,1024,512]{2,1,0:T(8,128)(2,1)} %all-to-all-done.4, bf16[4,512,352]{1,0,2:T(4,128)(2,1)S(1)} %copy-done.4, f32[1024,352]{0,1:T(8,128)} %convolution_bitcast_fusion.1), kind=kOutput, calls=%fused_computation | convolution fusion | flops 2957049856 | bytes 12713984 | tf_op jit(solution)/shard_map/sh,hqf->qsf/dot_general | solution.py:178
  197.7 5.2 %all-to-all-start.5 = ((bf16[4,1024,512]{2,1,0:T(8,128)(2,1)}), bf16[4,1024,512]{2,1,0:T(8,128)(2,1)}, u32[]{:S(2)}, u32[]{:S(2)}) async-start(bf16[4,1024,512]{2,1,0:T(8,128)(2,1)} %convert_bitcast_fusion), calls=%async_computation.5 | async-start | bytes 8388608 | tf_op jit(solution)/shard_map/all_to_all | solution.py:181
  203.0 0.2 copy.64
  203.2 1.2 fusion.29
  204.4 1.0 copy-done.6
  205.4 3.3 %fusion.2 = f32[128,704]{0,1:T(8,128)S(1)} fusion(bf16[128,2048]{0,1:T(8,128)(2,1)S(1)} %copy-done.6, bf16[2048,2112]{1,0:T(8,128)(2,1)} %all-gather.2.cloned.1.call-done), kind=kOutput, calls=%fused_computation.3 | convolution fusion | flops 369098752 | bytes 4030464 | tf_op jit(solution)/shard_map/dot_general | solution.py:19
  208.8 7.2 %convolution_bitcast_fusion.2 = f32[4,128,512]{1,2,0:T(8,128)} fusion(bf16[4,512,704]{2,1,0:T(8,128)(2,1)S(1)} %bitcast.93, bf16[128,2048]{0,1:T(8,128)(2,1)} %fusion.29, bf16[2048,2112]{1,0:T(8,128)(2,1)} %all-gather.2.cloned.1.call-done, f32[128,704]{0,1:T(8,128)S(1)} %fusion.2), kind=kOutput, calls=%fused_computation.17 | convolution fusion | flops 738738176 | bytes 7962624 | tf_op jit(solution)/shard_map/th,qfh->qtf/dot_general | solution.py:204
  215.9 34.0 %all-to-all-done.5 = bf16[4,1024,512]{2,1,0:T(8,128)(2,1)} async-done(((bf16[4,1024,512]{2,1,0:T(8,128)(2,1)}), bf16[4,1024,512]{2,1,0:T(8,128)(2,1)}, u32[]{:S(2)}, u32[]{:S(2)}) %all-to-all-start.5) | async-done | bytes 4194336 | tf_op jit(solution)/shard_map/all_to_all | solution.py:181
  250.0 3.5 %all-to-all-start.2 = ((f32[4,128,512]{1,2,0:T(8,128)}), f32[4,128,512]{1,2,0:T(8,128)S(1)}, u32[]{:S(2)}, u32[]{:S(2)}) async-start(f32[4,128,512]{1,2,0:T(8,128)} %convolution_bitcast_fusion.2), calls=%async_computation.2 | async-start | bytes 2097152 | tf_op jit(solution)/shard_map/all_to_all | solution.py:81
  253.5 4.1 %reduce_sum.99 = bf16[1024,512]{1,0:T(8,128)(2,1)} reduce(bf16[4,1024,512]{2,1,0:T(8,128)(2,1)} %all-to-all-done.5, bf16[]{:T(256)} %constant.25.clone.1), dimensions={0}, to_apply=%region_10.11 | reduce | flops 1572864 | bytes 5242882 | tf_op jit(solution)/shard_map/reduce_sum | solution.py:182
  257.6 8.4 %all-to-all-done.2 = f32[4,128,512]{1,2,0:T(8,128)S(1)} async-done(((f32[4,128,512]{1,2,0:T(8,128)}), f32[4,128,512]{1,2,0:T(8,128)S(1)}, u32[]{:S(2)}, u32[]{:S(2)}) %all-to-all-start.2) | async-done | bytes 1048608 | tf_op jit(solution)/shard_map/all_to_all | solution.py:81
  266.0 9.9 %all-to-all-start.6 = ((bf16[64,16,512]{2,1,0:T(8,128)(2,1)}), bf16[64,16,512]{2,1,0:T(8,128)(2,1)S(1)}, u32[]{:S(2)}, u32[]{:S(2)}) async-start(bf16[64,16,512]{2,1,0:T(8,128)(2,1)} %bitcast.22), calls=%async_computation.6 | async-start | bytes 2097152 | tf_op jit(solution)/shard_map/all_to_all | solution.py:183
  275.9 0.4 select_reduce_fusion
  276.6 28.1 %all-to-all-done.6 = bf16[64,16,512]{2,1,0:T(8,128)(2,1)S(1)} async-done(((bf16[64,16,512]{2,1,0:T(8,128)(2,1)}), bf16[64,16,512]{2,1,0:T(8,128)(2,1)S(1)}, u32[]{:S(2)}, u32[]{:S(2)}) %all-to-all-start.6) | async-done | bytes 1048608 | tf_op jit(solution)/shard_map/all_to_all | solution.py:183
  304.7 0.7 fusion.40
  305.4 0.6 broadcast_in_dim.25.x_ref
  306.0 5.5 %shard_map.151 = f32[32,128]{1,0:T(8,128)} custom-call(f32[8,128]{1,0:T(8,128)} %broadcast_in_dim.25.x_ref), custom_call_target="tpu_custom_call" | custom-call | tf_op jit(solution)/shard_map/pallas_call | solution.py:70
  311.6 0.7 slice_reduce_fusion.2
  312.3 0.8 fusion.42
  (44 shorter events, 0.9 us)
Async XLA Ops:
  7.2 197.2 %all-gather.2.cloned.1.call-start = ((), (), s32[]{:S(2)}) async-start(), calls=%async_computation.7 | async-start | bytes 9052160 | tf_op jit(solution)/shard_map/all_gather | solution.py:198
  50.1 4.7 %copy-start.8 = (f32[512]{0:T(512)S(1)}, f32[512]{0:T(512)}, u32[]{:S(2)}) copy-start(f32[512]{0:T(512)} %param.17) | copy-start | bytes 6148
  55.1 6.0 %copy-start.10 = (s32[128,6]{0,1:T(8,128)S(1)}, s32[128,6]{0,1:T(8,128)}, u32[]{:S(2)}) copy-start(s32[128,6]{0,1:T(8,128)} %param.24) | copy-start | bytes 9220
  56.7 7.0 %copy-start.12 = (s32[64]{0:T(128)S(1)}, s32[64]{0:T(128)}, u32[]{:S(2)}) copy-start(s32[64]{0:T(128)} %param.26) | copy-start | bytes 772
  56.7 20.6 %copy-start.7 = (bf16[128,512]{1,0:T(8,128)(2,1)S(1)}, bf16[128,512]{1,0:T(8,128)(2,1)}, u32[]{:S(2)}) copy-start(bf16[128,512]{1,0:T(8,128)(2,1)} %param.15) | copy-start | bytes 393220
  56.7 20.5 %all-to-all-start.1 = ((f32[4,129,512]{2,1,0:T(8,128)}), f32[4,129,512]{2,1,0:T(8,128)S(1)}, u32[]{:S(2)}, u32[]{:S(2)}) async-start(f32[4,129,512]{2,1,0:T(8,128)} %copy.60), calls=%async_computation.1 | async-start | bytes 2228224 | tf_op jit(solution)/shard_map/all_to_all | solution.py:130
  130.1 5.2 %copy-start.2 = (bf16[1,2048,352]{1,2,0:T(8,128)(2,1)S(1)}, bf16[1,2048,352]{1,2,0:T(8,128)(2,1)}, u32[]{:S(2)}) copy-start(bf16[1,2048,352]{1,2,0:T(8,128)(2,1)} %param.21) | copy-start | bytes 4325380
  130.1 53.2 %all-to-all-start.4 = ((bf16[4,1024,512]{2,1,0:T(8,128)(2,1)}), bf16[4,1024,512]{2,1,0:T(8,128)(2,1)}, u32[]{:S(2)}, u32[]{:S(2)}) async-start(bf16[4,1024,512]{2,1,0:T(8,128)(2,1)} %broadcast_in_dim.24), calls=%async_computation.4 | async-start | bytes 8388608 | tf_op jit(solution)/shard_map/all_to_all | solution.py:171
  137.3 4.5 %copy-start.3 = (bf16[1,352,2048]{2,1,0:T(8,128)(2,1)S(1)}, bf16[1,352,2048]{2,1,0:T(8,128)(2,1)}, u32[]{:S(2)}) copy-start(bf16[1,352,2048]{2,1,0:T(8,128)(2,1)} %param.23) | copy-start | bytes 4325380
  143.8 44.9 %copy-start.4 = (bf16[4,512,352]{1,0,2:T(4,128)(2,1)S(1)}, bf16[4,512,352]{1,0,2:T(4,128)(2,1)}, u32[]{:S(2)}) copy-start(bf16[4,512,352]{1,0,2:T(4,128)(2,1)} %reshape_squeeze.10) | copy-start | bytes 4325380
  197.7 5.2 %copy-start = (bf16[512,512]{1,0:T(8,128)(2,1)S(1)}, bf16[512,512]{1,0:T(8,128)(2,1)}, u32[]{:S(2)}) copy-start(bf16[512,512]{1,0:T(8,128)(2,1)} %shard_map.150) | copy-start | bytes 1572868
  197.7 52.2 %all-to-all-start.5 = ((bf16[4,1024,512]{2,1,0:T(8,128)(2,1)}), bf16[4,1024,512]{2,1,0:T(8,128)(2,1)}, u32[]{:S(2)}, u32[]{:S(2)}) async-start(bf16[4,1024,512]{2,1,0:T(8,128)(2,1)} %convert_bitcast_fusion), calls=%async_computation.5 | async-start | bytes 8388608 | tf_op jit(solution)/shard_map/all_to_all | solution.py:181
  204.4 1.0 copy-start.6
  205.4 3.3 %slice-start = ((bf16[2048,2112]{1,0:T(8,128)(2,1)}), bf16[2048,704]{1,0:T(8,128)(2,1)S(1)}, s32[]{:S(2)}) async-start(bf16[2048,2112]{1,0:T(8,128)(2,1)} %all-gather.2.cloned.1.call-done), calls=%async_computation.8 | async-start | bytes 6291456 | tf_op jit(solution)/shard_map/slice | solution.py:207
  250.0 16.0 %all-to-all-start.2 = ((f32[4,128,512]{1,2,0:T(8,128)}), f32[4,128,512]{1,2,0:T(8,128)S(1)}, u32[]{:S(2)}, u32[]{:S(2)}) async-start(f32[4,128,512]{1,2,0:T(8,128)} %convolution_bitcast_fusion.2), calls=%async_computation.2 | async-start | bytes 2097152 | tf_op jit(solution)/shard_map/all_to_all | solution.py:81
  257.6 18.3 %copy-start.9 = (f32[128,6]{0,1:T(8,128)S(1)}, f32[128,6]{0,1:T(8,128)}, u32[]{:S(2)}) copy-start(f32[128,6]{0,1:T(8,128)} %param.25) | copy-start | bytes 9220
  266.0 38.7 %copy-start.1 = (bf16[128,512]{1,0:T(8,128)(2,1)S(1)}, bf16[128,512]{1,0:T(8,128)(2,1)}, u32[]{:S(2)}) copy-start(bf16[128,512]{1,0:T(8,128)(2,1)} %add_convert_fusion.x_ref) | copy-start | bytes 393220
  266.0 38.7 %all-to-all-start.6 = ((bf16[64,16,512]{2,1,0:T(8,128)(2,1)}), bf16[64,16,512]{2,1,0:T(8,128)(2,1)S(1)}, u32[]{:S(2)}, u32[]{:S(2)}) async-start(bf16[64,16,512]{2,1,0:T(8,128)(2,1)} %bitcast.22), calls=%async_computation.6 | async-start | bytes 2097152 | tf_op jit(solution)/shard_map/all_to_all | solution.py:183
  276.3 36.0 %copy-start.11 = (f32[512]{0:T(512)S(1)}, f32[512]{0:T(512)}, u32[]{:S(2)}) copy-start(f32[512]{0:T(512)} %param.27) | copy-start | bytes 6148
  305.4 7.7 %copy-start.5 = (bf16[128,512]{1,0:T(8,128)(2,1)}, bf16[128,512]{1,0:T(8,128)(2,1)S(1)}, u32[]{:S(2)}) copy-start(bf16[128,512]{1,0:T(8,128)(2,1)S(1)} %get-tuple-element.5) | copy-start | bytes 393220
Sparse Core Ops, SparseCore 0:
  10.7 87.1 all-gather.1

commit v11 on v10

--- a/solution.py
+++ b/solution.py
@@ -77,8 +77,56 @@
     )(x)
 
 
-def reduce_scatter_mp(blocks):
-    return jnp.sum(lax.all_to_all(blocks, "mp", split_axis=0, concat_axis=0, tiled=True), axis=0)
+def _exchange_kernel(axis, x_ref, o_ref, send_sem, recv_sem):
+    coords = {name: lax.axis_index(name) for name in ("g", "c", "mp")}
+    n = lax.axis_size(axis)
+    me = coords[axis]
+
+    def device(peer):
+        return tuple(peer if name == axis else coords[name] for name in ("g", "c", "mp"))
+
+    barrier = pltpu.get_barrier_semaphore()
+
+    def greet(p, carry):
+        peer = lax.rem(me + p, n)
+        pl.semaphore_signal(barrier, inc=1, device_id=device(peer), device_id_type=MESH)
+        return carry
+
+    lax.fori_loop(1, n, greet, 0)
+    pl.semaphore_wait(barrier, n - 1)
+    pltpu.make_async_copy(x_ref.at[me], o_ref.at[me], recv_sem).start()
+
+    def send(p, carry):
+        peer = lax.rem(me + p, n)
+        pltpu.make_async_remote_copy(
+            src_ref=x_ref.at[peer],
+            dst_ref=o_ref.at[me],
+            send_sem=send_sem,
+            recv_sem=recv_sem,
+            device_id=device(peer),
+            device_id_type=MESH,
+        ).start()
+        return carry
+
+    lax.fori_loop(1, n, send, 0)
+    sent = o_ref.at[pl.ds(0, n - 1)]
+    pltpu.make_async_copy(sent, sent, send_sem).wait()
+    pltpu.make_async_copy(o_ref, o_ref, recv_sem).wait()
+
+
+def exchange(x, axis, collective_id):
+    return pl.pallas_call(
+        functools.partial(_exchange_kernel, axis),
+        out_shape=jax.ShapeDtypeStruct(x.shape, x.dtype),
+        in_specs=[pl.BlockSpec(memory_space=pl.ANY)],
+        out_specs=pl.BlockSpec(memory_space=pl.ANY),
+        scratch_shapes=[pltpu.SemaphoreType.DMA(()), pltpu.SemaphoreType.DMA(())],
+        compiler_params=pltpu.CompilerParams(collective_id=collective_id, has_side_effects=True),
+    )(x)
+
+
+def reduce_scatter_mp(blocks, collective_id):
+    return jnp.sum(exchange(blocks, "mp", collective_id), axis=0)
 
 
 def swap_halves(value, tok_rows):
@@ -127,13 +175,7 @@
     part_half = matmul_t(att_pair, w_half)
     partial_value = natural_blocks(swap_halves(part_half, tok_rows), mp_count)
     gain_row = jnp.broadcast_to(ffn_gain[None, None, :], (mp_count, 1, block_width))
-    exchanged = lax.all_to_all(
-        jnp.concatenate([partial_value, gain_row], axis=1),
-        "mp",
-        split_axis=0,
-        concat_axis=0,
-        tiled=True,
-    )
+    exchanged = exchange(jnp.concatenate([partial_value, gain_row], axis=1), "mp", 3)
     projected = jnp.sum(exchanged[:, :tok_rows, :], axis=0)
     gain = exchanged[:, tok_rows, :].reshape(model_width)
     hidden = (residual.astype(jnp.float32) + projected).astype(jnp.bfloat16)
@@ -207,7 +249,7 @@
         shared_all[:, 2 * hidden_units :].reshape(mp_count, block_width, hidden_units),
         preferred_element_type=jnp.float32,
     )
-    mixture = reduce_scatter_mp(shared_part) + routed
+    mixture = reduce_scatter_mp(shared_part, 4) + routed
     final = (hidden_float + mixture).astype(jnp.bfloat16)
     final_float = final.astype(jnp.float32)
     own_squares = jnp.sum(final_float * final_float, axis=1)

time: 321 us -> 315 us (0.981)
  waiting for transfers between devices: 123 us -> 41.2 us
  blocking collectives: 44.8 us -> 93 us
  Pallas kernels: 51.6 us -> 85.6 us
  starting transfers between devices: 28.3 us -> 16.9 us
  local copies, waits for them, and re-layouts: 17.4 us -> 20.9 us
    all_to_all x3 -> x1, waiting for transfers between devices: 55.1 us -> 1.7 us  [swap_halves(): lax.all_to_all(value.reshape(2, tok_rows, value.shape[1]), 'c', split_axi...]
    all_to_all x1, blocking collectives: 4.58 us -> 52.8 us  [local(): lax.all_to_all(partial_out, 'mp', split_axis=0, concat_axis=0, tiled=True)]
    pallas_call x0 -> x2, Pallas kernels: none -> 33 us  [exchange(): pl.pallas_call(functools.partial(_exchange_kernel, axis), out_shape=jax.S...]
    all_to_all x1, waiting for transfers between devices: 28.1 us -> 0.01 us  [local(): lax.all_to_all(expert_out.reshape(experts, capacity, block_width), dp, sp...]
    all_to_all x3 -> x1, starting transfers between devices: 13.2 us -> 3.71 us  [swap_halves(): lax.all_to_all(value.reshape(2, tok_rows, value.shape[1]), 'c', split_axi...]
    slice x2 -> x1, local copies, waits for them, and re-layouts: 0.01 us -> 3.84 us  [local(): shared_all[:, 2 * hidden_units:]]
  transfers between devices with their start and end apart: 6 -> 4, of which waited for: 5 -> 2; matrix products, arithmetic and copies ran while one was open for 16% -> 19% of each run, Pallas kernels for 14% -> 26%
where the time goes in v11:
time: 315 us; the launch traced here: 314 us
  blocking collectives  93 us (30%)
  Pallas kernels  85.6 us (27%)
  waiting for transfers between devices  41.2 us (13%)
  matrix products  28.7 us (9%)
  local copies, waits for them, and re-layouts  20.9 us (7%)
  starting transfers between devices  16.9 us (5%)
  between operations  14.3 us (5%)
  other arithmetic  13.5 us (4%)
    all_to_all x1, blocking collectives, local(): lax.all_to_all(partial_out, 'mp', split_axis=0, concat_axis=0, tiled=True)  52.8 us
    pallas_call x3, Pallas kernels, gather_rows(): pl.pallas_call(functools.partial(_gather_kernel, axis), out_shape=jax.Sha...  52.6 us
    all_to_all x1, waiting for transfers between devices, local(): lax.all_to_all(copies, 'mp', split_axis=0, concat_axis=0, tiled=True)  39.5 us
    all_to_all x1, blocking collectives, local(): lax.all_to_all(outgoing.reshape(experts, capacity, block_width), dp, spli...  38.2 us
    pallas_call x2, Pallas kernels, exchange(): pl.pallas_call(functools.partial(_exchange_kernel, axis), out_shape=jax.S...  33 us
    dot_general x1, matrix products, local(): jnp.einsum('sh,hqf->qsf', activated, down_block, preferred_element_type=j...  9.07 us
    dot_general x1, matrix products, local(): jnp.einsum('th,qfh->qtf', shared_act, shared_all[:, 2 * hidden_units:].re...  8.08 us
    all_to_all x1, starting transfers between devices, local(): lax.all_to_all(expert_out.reshape(experts, capacity, block_width), dp, sp...  8.01 us
  transfers between devices with their start and end apart: 4, of which 2 were waited for; matrix products, arithmetic and copies ran while one was open for 19% of the time, Pallas kernels for 26%

profile of v11, /device:TPU:8, one launch (start us, length us, event | category | flops | bytes accessed | tf_op | source)
XLA Modules:
  0.0 314.2 jit_solution(10498601615290723103)
XLA Ops:
  7.2 1.6 concatenate.7
  8.9 37.1 %shard_map.149 = bf16[1024,512]{1,0:T(8,128)(2,1)} custom-call(bf16[32,512]{1,0:T(8,128)(2,1)} %bitcast.96), custom_call_target="tpu_custom_call" | custom-call | tf_op jit(solution)/shard_map/pallas_call | solution.py:70
  46.0 2.0 all_gather.6
  48.0 1.7 fusion.53
  49.6 1.3 copy.33
  51.0 3.7 %all-to-all-start = ((f32[2,128,1024]{1,2,0:T(8,128)}), f32[2,128,1024]{1,2,0:T(8,128)S(1)}, u32[]{:S(2)}, u32[]{:S(2)}) async-start(f32[2,128,1024]{1,2,0:T(8,128)} %copy.33), calls=%async_computation | async-start | bytes 2097152 | tf_op jit(solution)/shard_map/all_to_all | solution.py:133
  54.8 0.1 eq.39
  55.0 0.1 eq.43
  55.1 1.7 all-to-all-done
  56.9 0.3 copy.35
  57.2 0.3 copy-done.8
  57.6 1.1 pad_maximum_fusion.x_ref
  58.7 17.2 %shard_map.150 = f32[4,129,512]{2,1,0:T(8,128)} custom-call(f32[4,129,512]{2,1,0:T(8,128)} %pad_maximum_fusion.x_ref), custom_call_target="tpu_custom_call" | custom-call | tf_op jit(solution)/shard_map/pallas_call | solution.py:118
  75.9 1.3 slice_reduce_fusion
  77.2 0.7 add_convert_fusion.x_ref
  77.9 10.0 %shard_map.151 = bf16[512,512]{1,0:T(8,128)(2,1)} custom-call(bf16[128,512]{1,0:T(8,128)(2,1)} %add_convert_fusion.x_ref), custom_call_target="tpu_custom_call" | custom-call | tf_op jit(solution)/shard_map/pallas_call | solution.py:70
  88.0 1.8 reduce-window.6
  89.8 0.3 slice_reduce_fusion.1
  90.1 0.1 select_reduce_fusion.1
  90.5 0.2 multiply_reduce_fusion
  90.7 0.5 fusion.4
  91.2 0.5 convolution_convert_fusion
  91.8 38.2 %all_to_all.25 = bf16[64,16,512]{2,1,0:T(8,128)(2,1)S(1)} all-to-all(bf16[64,16,512]{2,1,0:T(8,128)(2,1)S(1)} %bitcast.92), channel_id=1, replica_groups=mesh['g'=32,'c'=2,'mp'=4] {'g','c'}, dimensions={0} | all-to-all | bytes 2097152 | tf_op jit(solution)/shard_map/all_to_all | solution.py:205
  129.9 2.3 broadcast_in_dim.24
  132.2 5.2 %all-to-all-start.2 = ((bf16[4,1024,512]{2,1,0:T(8,128)(2,1)}), bf16[4,1024,512]{2,1,0:T(8,128)(2,1)}, u32[]{:S(2)}, u32[]{:S(2)}) async-start(bf16[4,1024,512]{2,1,0:T(8,128)(2,1)} %broadcast_in_dim.24), calls=%async_computation.2 | async-start | bytes 8388608 | tf_op jit(solution)/shard_map/all_to_all | solution.py:213
  137.4 2.0 reshape_squeeze.11
  139.4 4.5 %reshape_squeeze.10 = bf16[4,512,352]{1,0,2:T(4,128)(2,1)} reshape(bf16[1,2048,352]{1,2,0:T(8,128)(2,1)} %param.22) | data formatting | bytes 2883584 | tf_op jit(solution)/shard_map/reshape;squeeze | solution.py:215
  143.9 2.0 reshape_squeeze.9
  145.9 39.5 %all-to-all-done.2 = bf16[4,1024,512]{2,1,0:T(8,128)(2,1)} async-done(((bf16[4,1024,512]{2,1,0:T(8,128)(2,1)}), bf16[4,1024,512]{2,1,0:T(8,128)(2,1)}, u32[]{:S(2)}, u32[]{:S(2)}) %all-to-all-start.2) | async-done | bytes 4194336 | tf_op jit(solution)/shard_map/all_to_all | solution.py:213
  185.3 5.4 %convolution_bitcast_fusion.1 = f32[1024,352]{0,1:T(8,128)} fusion(bf16[4,1024,512]{2,1,0:T(8,128)(2,1)} %all-to-all-done.2, bf16[4,512,352]{1,0,2:T(4,128)(2,1)} %reshape_squeeze.9), kind=kOutput, calls=%fused_computation.11 | convolution fusion | flops 1476395008 | bytes 7077888 | tf_op jit(solution)/shard_map/qsf,qfh->sh/dot_general | solution.py:216
  190.8 9.1 %convert_bitcast_fusion = bf16[4,1024,512]{2,1,0:T(8,128)(2,1)} fusion(bf16[352,4,512]{2,1,0:T(4,128)(2,1)S(1)} %copy-done.4, bf16[4,1024,512]{2,1,0:T(8,128)(2,1)} %all-to-all-done.2, bf16[4,512,352]{1,0,2:T(4,128)(2,1)} %reshape_squeeze.10, f32[1024,352]{0,1:T(8,128)} %convolution_bitcast_fusion.1), kind=kOutput, calls=%fused_computation | convolution fusion | flops 2957049856 | bytes 12713984 | tf_op jit(solution)/shard_map/sh,hqf->qsf/dot_general | solution.py:220
  199.8 52.8 %all_to_all.26 = bf16[4,1024,512]{2,1,0:T(8,128)(2,1)} all-to-all(bf16[4,1024,512]{2,1,0:T(8,128)(2,1)} %convert_bitcast_fusion), channel_id=1, replica_groups=mesh['g'=32,'c'=2,'mp'=4] {'mp'}, dimensions={0} | all-to-all | bytes 8388608 | tf_op jit(solution)/shard_map/all_to_all | solution.py:223
  252.7 4.1 %reduce_sum.99 = bf16[1024,512]{1,0:T(8,128)(2,1)} reduce(bf16[4,1024,512]{2,1,0:T(8,128)(2,1)} %all_to_all.26, bf16[]{:T(256)} %constant.25.clone.1), dimensions={0}, to_apply=%region_10.11 | reduce | flops 1572864 | bytes 5242882 | tf_op jit(solution)/shard_map/reduce_sum | solution.py:224
  256.8 8.0 %all-to-all-start.4 = ((bf16[64,16,512]{2,1,0:T(8,128)(2,1)}), bf16[64,16,512]{2,1,0:T(8,128)(2,1)S(1)}, u32[]{:S(2)}, u32[]{:S(2)}) async-start(bf16[64,16,512]{2,1,0:T(8,128)(2,1)} %bitcast.22), calls=%async_computation.4 | async-start | bytes 2097152 | tf_op jit(solution)/shard_map/all_to_all | solution.py:225
  264.8 0.8 slice.26
  265.7 0.2 copy.37
  265.9 0.4 select_reduce_fusion
  266.3 0.3 fusion.29
  266.7 3.8 %slice.32 = bf16[2048,704]{1,0:T(8,128)(2,1)} slice(bf16[2048,2112]{1,0:T(8,128)(2,1)} %all-gather.2.cloned.1.call-done), slice={[0:2048], [1408:2112]} | slice | bytes 5767168 | tf_op jit(solution)/shard_map/slice | solution.py:249
  270.5 3.2 %fusion.2 = f32[128,704]{0,1:T(8,128)S(1)} fusion(bf16[128,2048]{0,1:T(8,128)(2,1)S(1)} %fusion.29, bf16[2048,2112]{1,0:T(8,128)(2,1)} %all-gather.2.cloned.1.call-done), kind=kOutput, calls=%fused_computation.3 | convolution fusion | flops 369098752 | bytes 4030464 | tf_op jit(solution)/shard_map/dot_general | solution.py:19
  273.7 8.1 %convolution_bitcast_fusion.2.x_ref = f32[4,128,512]{2,1,0:T(8,128)} fusion(bf16[4,512,704]{2,1,0:T(8,128)(2,1)} %bitcast.93, bf16[128,2048]{0,1:T(8,128)(2,1)S(1)} %fusion.29, bf16[2048,2112]{1,0:T(8,128)(2,1)} %all-gather.2.cloned.1.call-done, f32[128,704]{0,1:T(8,128)S(1)} %fusion.2), kind=kOutput, calls=%fused_computation.16 | convolution fusion | flops 738738176 | bytes 8224768 | tf_op jit(solution)/shard_map/th,qfh->qtf/dot_general | solution.py:246
  281.8 15.8 %shard_map.152 = f32[4,128,512]{2,1,0:T(8,128)} custom-call(f32[4,128,512]{2,1,0:T(8,128)} %convolution_bitcast_fusion.2.x_ref), custom_call_target="tpu_custom_call" | custom-call | tf_op jit(solution)/shard_map/pallas_call | solution.py:118
  297.6 1.3 reduce_sum.95
  299.0 0.7 fusion.40
  299.7 0.6 broadcast_in_dim.25.x_ref
  300.3 5.5 %shard_map.153 = f32[32,128]{1,0:T(8,128)} custom-call(f32[8,128]{1,0:T(8,128)} %broadcast_in_dim.25.x_ref), custom_call_target="tpu_custom_call" | custom-call | tf_op jit(solution)/shard_map/pallas_call | solution.py:70
  305.8 0.7 slice_reduce_fusion.2
  306.6 0.8 fusion.42
  (40 shorter events, 0.6 us)
Async XLA Ops:
  7.2 38.8 %copy-start.6 = (bf16[128,512]{1,0:T(8,128)(2,1)S(1)}, bf16[128,512]{1,0:T(8,128)(2,1)}, u32[]{:S(2)}) copy-start(bf16[128,512]{1,0:T(8,128)(2,1)} %param.14) | copy-start | bytes 393220
  7.2 259.5 %all-gather.2.cloned.1.call-start = ((), (), s32[]{:S(2)}) async-start(), calls=%async_computation.5 | async-start | bytes 9052160 | tf_op jit(solution)/shard_map/all_gather | solution.py:240
  51.0 3.7 %copy-start.10 = (s32[128,6]{0,1:T(8,128)S(1)}, s32[128,6]{0,1:T(8,128)}, u32[]{:S(2)}) copy-start(s32[128,6]{0,1:T(8,128)} %param.24) | copy-start | bytes 9220
  51.0 5.8 %all-to-all-start = ((f32[2,128,1024]{1,2,0:T(8,128)}), f32[2,128,1024]{1,2,0:T(8,128)S(1)}, u32[]{:S(2)}, u32[]{:S(2)}) async-start(f32[2,128,1024]{1,2,0:T(8,128)} %copy.33), calls=%async_computation | async-start | bytes 2097152 | tf_op jit(solution)/shard_map/all_to_all | solution.py:133
  56.9 0.7 copy-start.8
  58.7 18.6 %copy-start.7 = (bf16[128,512]{1,0:T(8,128)(2,1)S(1)}, bf16[128,512]{1,0:T(8,128)(2,1)}, u32[]{:S(2)}) copy-start(bf16[128,512]{1,0:T(8,128)(2,1)} %param.15) | copy-start | bytes 393220
  75.9 14.2 %copy-start.12 = (s32[64]{0:T(128)S(1)}, s32[64]{0:T(128)}, u32[]{:S(2)}) copy-start(s32[64]{0:T(128)} %param.26) | copy-start | bytes 772
  77.9 13.3 %copy-start.1 = (bf16[128,512]{1,0:T(8,128)(2,1)S(1)}, bf16[128,512]{1,0:T(8,128)(2,1)}, u32[]{:S(2)}) copy-start(bf16[128,512]{1,0:T(8,128)(2,1)} %add_convert_fusion.x_ref) | copy-start | bytes 393220
  88.0 2.5 copy-start
  132.2 5.2 %copy-start.2 = (bf16[1,352,2048]{2,1,0:T(8,128)(2,1)S(1)}, bf16[1,352,2048]{2,1,0:T(8,128)(2,1)}, u32[]{:S(2)}) copy-start(bf16[1,352,2048]{2,1,0:T(8,128)(2,1)} %param.23) | copy-start | bytes 4325380
  132.2 53.1 %all-to-all-start.2 = ((bf16[4,1024,512]{2,1,0:T(8,128)(2,1)}), bf16[4,1024,512]{2,1,0:T(8,128)(2,1)}, u32[]{:S(2)}, u32[]{:S(2)}) async-start(bf16[4,1024,512]{2,1,0:T(8,128)(2,1)} %broadcast_in_dim.24), calls=%async_computation.2 | async-start | bytes 8388608 | tf_op jit(solution)/shard_map/all_to_all | solution.py:213
  139.4 4.5 %copy-start.3 = (bf16[1,2048,352]{1,2,0:T(8,128)(2,1)S(1)}, bf16[1,2048,352]{1,2,0:T(8,128)(2,1)}, u32[]{:S(2)}) copy-start(bf16[1,2048,352]{1,2,0:T(8,128)(2,1)} %param.21) | copy-start | bytes 4325380
  145.9 44.9 %copy-start.4 = (bf16[352,4,512]{2,1,0:T(4,128)(2,1)S(1)}, bf16[352,4,512]{2,1,0:T(4,128)(2,1)}, u32[]{:S(2)}) copy-start(bf16[352,4,512]{2,1,0:T(4,128)(2,1)} %reshape_squeeze.11) | copy-start | bytes 4325380
  256.8 9.1 %copy-start.9 = (f32[128,6]{0,1:T(8,128)S(1)}, f32[128,6]{0,1:T(8,128)}, u32[]{:S(2)}) copy-start(f32[128,6]{0,1:T(8,128)} %param.25) | copy-start | bytes 9220
  256.8 42.2 %all-to-all-start.4 = ((bf16[64,16,512]{2,1,0:T(8,128)(2,1)}), bf16[64,16,512]{2,1,0:T(8,128)(2,1)S(1)}, u32[]{:S(2)}, u32[]{:S(2)}) async-start(bf16[64,16,512]{2,1,0:T(8,128)(2,1)} %bitcast.22), calls=%async_computation.4 | async-start | bytes 2097152 | tf_op jit(solution)/shard_map/all_to_all | solution.py:225
  297.6 9.0 %copy-start.11 = (f32[512]{0:T(512)S(1)}, f32[512]{0:T(512)}, u32[]{:S(2)}) copy-start(f32[512]{0:T(512)} %param.27) | copy-start | bytes 6148
  299.7 7.7 %copy-start.5 = (bf16[128,512]{1,0:T(8,128)(2,1)}, bf16[128,512]{1,0:T(8,128)(2,1)S(1)}, u32[]{:S(2)}) copy-start(bf16[128,512]{1,0:T(8,128)(2,1)S(1)} %get-tuple-element.5) | copy-start | bytes 393220
Sparse Core Ops, SparseCore 0:
  10.7 87.1 all-gather.1

commit v12 on v11

--- a/solution.py
+++ b/solution.py
@@ -79,11 +79,20 @@
 
 def _exchange_kernel(axis, x_ref, o_ref, send_sem, recv_sem):
     coords = {name: lax.axis_index(name) for name in ("g", "c", "mp")}
-    n = lax.axis_size(axis)
-    me = coords[axis]
-
-    def device(peer):
-        return tuple(peer if name == axis else coords[name] for name in ("g", "c", "mp"))
+    if axis == "dp":
+        cores = lax.axis_size("c")
+        n = lax.axis_size("g") * cores
+        me = coords["g"] * cores + coords["c"]
+
+        def device(peer):
+            return (peer // cores, peer % cores, coords["mp"])
+
+    else:
+        n = lax.axis_size(axis)
+        me = coords[axis]
+
+        def device(peer):
+            return tuple(peer if name == axis else coords[name] for name in ("g", "c", "mp"))
 
     barrier = pltpu.get_barrier_semaphore()
 
@@ -202,13 +211,8 @@
     combine = jnp.sum(jnp.where(hit, flat_scores[:, :, None], 0.0), axis=1)
     pick = jnp.any(hit, axis=1).astype(jnp.bfloat16)
     outgoing = matmul(pick.T, normed).astype(jnp.bfloat16)
-    arrived = lax.all_to_all(
-        outgoing.reshape(experts, capacity, block_width),
-        dp,
-        split_axis=0,
-        concat_axis=0,
-        tiled=True,
-    ).reshape(slots, block_width)
+    arrived = exchange(outgoing.reshape(experts, capacity, block_width), "dp", 5)
+    arrived = arrived.reshape(slots, block_width)
     copies = jnp.broadcast_to(arrived[None], (mp_count, slots, block_width))
     in_rows = lax.all_to_all(copies, "mp", split_axis=0, concat_axis=0, tiled=True)
     gate_block = expert_gate[0].reshape(mp_count, block_width, -1)

time: 315 us -> 315 us (level)
  blocking collectives: 93 us -> 56.1 us
  Pallas kernels: 85.6 us -> 117 us
    all_to_all x1 -> x0, blocking collectives: 38.2 us -> none  [local(): lax.all_to_all(outgoing.reshape(experts, capacity, block_width), dp, spli...]
    pallas_call x2 -> x3, Pallas kernels: 33 us -> 64.3 us  [exchange(): pl.pallas_call(functools.partial(_exchange_kernel, axis), out_shape=jax.S...]
  transfers between devices with their start and end apart: 4 -> 4, of which waited for: 2 -> 2; matrix products, arithmetic and copies ran while one was open for 19% -> 19% of each run, Pallas kernels for 26% -> 35%
where the time goes in v12:
time: 315 us; the launch traced here: 314 us
  Pallas kernels  117 us (37%)
  blocking collectives  56.1 us (18%)
  waiting for transfers between devices  42.4 us (13%)
  matrix products  29.5 us (9%)
  local copies, waits for them, and re-layouts  22.1 us (7%)
  starting transfers between devices  18.9 us (6%)
  between operations  14.3 us (5%)
  other arithmetic  13.5 us (4%)
    pallas_call x3, Pallas kernels, exchange(): pl.pallas_call(functools.partial(_exchange_kernel, axis), out_shape=jax.S...  64.3 us
    all_to_all x1, blocking collectives, local(): lax.all_to_all(partial_out, 'mp', split_axis=0, concat_axis=0, tiled=True)  54.1 us
    pallas_call x3, Pallas kernels, gather_rows(): pl.pallas_call(functools.partial(_gather_kernel, axis), out_shape=jax.Sha...  52.6 us
    all_to_all x1, waiting for transfers between devices, local(): lax.all_to_all(copies, 'mp', split_axis=0, concat_axis=0, tiled=True)  40.7 us
    all_to_all x1, starting transfers between devices, local(): lax.all_to_all(expert_out.reshape(experts, capacity, block_width), dp, sp...  10 us
    dot_general x1, matrix products, local(): jnp.einsum('sh,hqf->qsf', activated, down_block, preferred_element_type=j...  8.99 us
    dot_general x1, matrix products, local(): jnp.einsum('th,qfh->qtf', shared_act, shared_all[:, 2 * hidden_units:].re...  8.08 us
  transfers between devices with their start and end apart: 4, of which 2 were waited for; matrix products, arithmetic and copies ran while one was open for 19% of the time, Pallas kernels for 35%

profile of v12, /device:TPU:8, one launch (start us, length us, event | category | flops | bytes accessed | tf_op | source)
XLA Modules:
  0.0 313.9 jit_solution(18162375692123017855)
XLA Ops:
  7.2 1.6 concatenate.7
  8.9 37.1 %shard_map.149 = bf16[1024,512]{1,0:T(8,128)(2,1)} custom-call(bf16[32,512]{1,0:T(8,128)(2,1)} %bitcast.96), custom_call_target="tpu_custom_call" | custom-call | tf_op jit(solution)/shard_map/pallas_call | solution.py:70
  46.0 2.0 all_gather.6
  48.0 1.7 fusion.53
  49.6 1.3 copy.33
  51.0 3.7 %all-to-all-start = ((f32[2,128,1024]{1,2,0:T(8,128)}), f32[2,128,1024]{1,2,0:T(8,128)S(1)}, u32[]{:S(2)}, u32[]{:S(2)}) async-start(f32[2,128,1024]{1,2,0:T(8,128)} %copy.33), calls=%async_computation | async-start | bytes 2097152 | tf_op jit(solution)/shard_map/all_to_all | solution.py:142
  54.8 0.1 eq.39
  55.0 0.1 eq.43
  55.1 1.7 all-to-all-done
  56.9 0.3 copy.35
  57.2 0.3 copy-done.8
  57.6 1.1 pad_maximum_fusion.x_ref
  58.7 17.2 %shard_map.150 = f32[4,129,512]{2,1,0:T(8,128)} custom-call(f32[4,129,512]{2,1,0:T(8,128)} %pad_maximum_fusion.x_ref), custom_call_target="tpu_custom_call" | custom-call | tf_op jit(solution)/shard_map/pallas_call | solution.py:127
  75.9 1.3 slice_reduce_fusion
  77.2 0.7 add_convert_fusion.x_ref
  77.9 10.0 %shard_map.151 = bf16[512,512]{1,0:T(8,128)(2,1)} custom-call(bf16[128,512]{1,0:T(8,128)(2,1)} %add_convert_fusion.x_ref), custom_call_target="tpu_custom_call" | custom-call | tf_op jit(solution)/shard_map/pallas_call | solution.py:70
  88.0 1.8 reduce-window.6
  89.8 0.3 slice_reduce_fusion.1
  90.1 0.1 select_reduce_fusion.1
  90.5 0.2 multiply_reduce_fusion
  90.7 0.5 fusion.4
  91.2 1.5 convolution_convert_fusion
  92.7 31.2 %shard_map.153 = bf16[64,16,512]{2,1,0:T(8,128)(2,1)} custom-call(bf16[64,16,512]{2,1,0:T(8,128)(2,1)} %bitcast.92), custom_call_target="tpu_custom_call" | custom-call | tf_op jit(solution)/shard_map/pallas_call | solution.py:127
  124.0 3.5 %broadcast_in_dim.24 = bf16[4,1024,512]{2,1,0:T(8,128)(2,1)} broadcast(bf16[1024,512]{1,0:T(8,128)(2,1)} %bitcast.86), dimensions={1,2} | broadcast | bytes 5242880 | tf_op jit(solution)/shard_map/broadcast_in_dim | solution.py:216
  127.5 5.2 %all-to-all-start.1 = ((bf16[4,1024,512]{2,1,0:T(8,128)(2,1)}), bf16[4,1024,512]{2,1,0:T(8,128)(2,1)}, u32[]{:S(2)}, u32[]{:S(2)}) async-start(bf16[4,1024,512]{2,1,0:T(8,128)(2,1)} %broadcast_in_dim.24), calls=%async_computation.1 | async-start | bytes 8388608 | tf_op jit(solution)/shard_map/all_to_all | solution.py:217
  132.7 2.0 reshape_squeeze.11
  134.6 4.5 %reshape_squeeze.10 = bf16[4,512,352]{1,0,2:T(4,128)(2,1)} reshape(bf16[1,2048,352]{1,2,0:T(8,128)(2,1)} %param.22) | data formatting | bytes 2883584 | tf_op jit(solution)/shard_map/reshape;squeeze | solution.py:219
  139.1 2.0 reshape_squeeze.9
  141.1 40.7 %all-to-all-done.1 = bf16[4,1024,512]{2,1,0:T(8,128)(2,1)} async-done(((bf16[4,1024,512]{2,1,0:T(8,128)(2,1)}), bf16[4,1024,512]{2,1,0:T(8,128)(2,1)}, u32[]{:S(2)}, u32[]{:S(2)}) %all-to-all-start.1) | async-done | bytes 4194336 | tf_op jit(solution)/shard_map/all_to_all | solution.py:217
  181.8 5.4 %convolution_bitcast_fusion.1 = f32[1024,352]{0,1:T(8,128)} fusion(bf16[4,1024,512]{2,1,0:T(8,128)(2,1)} %all-to-all-done.1, bf16[4,512,352]{1,0,2:T(4,128)(2,1)} %reshape_squeeze.9), kind=kOutput, calls=%fused_computation.11 | convolution fusion | flops 1476395008 | bytes 7077888 | tf_op jit(solution)/shard_map/qsf,qfh->sh/dot_general | solution.py:220
  187.2 9.0 %convert_bitcast_fusion = bf16[4,1024,512]{2,1,0:T(8,128)(2,1)} fusion(bf16[352,4,512]{2,1,0:T(4,128)(2,1)S(1)} %copy-done.4, bf16[4,1024,512]{2,1,0:T(8,128)(2,1)} %all-to-all-done.1, bf16[4,512,352]{1,0,2:T(4,128)(2,1)} %reshape_squeeze.10, f32[1024,352]{0,1:T(8,128)} %convolution_bitcast_fusion.1), kind=kOutput, calls=%fused_computation | convolution fusion | flops 2957049856 | bytes 12713984 | tf_op jit(solution)/shard_map/sh,hqf->qsf/dot_general | solution.py:224
  196.2 54.1 %all_to_all.20 = bf16[4,1024,512]{2,1,0:T(8,128)(2,1)} all-to-all(bf16[4,1024,512]{2,1,0:T(8,128)(2,1)} %convert_bitcast_fusion), channel_id=1, replica_groups=mesh['g'=32,'c'=2,'mp'=4] {'mp'}, dimensions={0} | all-to-all | bytes 8388608 | tf_op jit(solution)/shard_map/all_to_all | solution.py:227
  250.3 4.1 %reduce_sum.99 = bf16[1024,512]{1,0:T(8,128)(2,1)} reduce(bf16[4,1024,512]{2,1,0:T(8,128)(2,1)} %all_to_all.20, bf16[]{:T(256)} %constant.25.clone.1), dimensions={0}, to_apply=%region_10.11 | reduce | flops 1572864 | bytes 5242882 | tf_op jit(solution)/shard_map/reduce_sum | solution.py:228
  254.5 10.0 %all-to-all-start.3 = ((bf16[64,16,512]{2,1,0:T(8,128)(2,1)}), bf16[64,16,512]{2,1,0:T(8,128)(2,1)S(1)}, u32[]{:S(2)}, u32[]{:S(2)}) async-start(bf16[64,16,512]{2,1,0:T(8,128)(2,1)} %bitcast.22), calls=%async_computation.3 | async-start | bytes 2097152 | tf_op jit(solution)/shard_map/all_to_all | solution.py:229
  264.5 0.8 slice.26
  265.3 0.2 copy.37
  265.6 0.4 select_reduce_fusion
  266.0 0.3 fusion.29
  266.4 3.8 %slice.32 = bf16[2048,704]{1,0:T(8,128)(2,1)} slice(bf16[2048,2112]{1,0:T(8,128)(2,1)} %all-gather.2.cloned.1.call-done), slice={[0:2048], [1408:2112]} | slice | bytes 5767168 | tf_op jit(solution)/shard_map/slice | solution.py:253
  270.2 3.2 %fusion.2 = f32[128,704]{0,1:T(8,128)S(1)} fusion(bf16[128,2048]{0,1:T(8,128)(2,1)S(1)} %fusion.29, bf16[2048,2112]{1,0:T(8,128)(2,1)} %all-gather.2.cloned.1.call-done), kind=kOutput, calls=%fused_computation.3 | convolution fusion | flops 369098752 | bytes 4030464 | tf_op jit(solution)/shard_map/dot_general | solution.py:19
  273.4 8.1 %convolution_bitcast_fusion.2.x_ref = f32[4,128,512]{2,1,0:T(8,128)} fusion(bf16[4,512,704]{2,1,0:T(8,128)(2,1)} %bitcast.93, bf16[128,2048]{0,1:T(8,128)(2,1)S(1)} %fusion.29, bf16[2048,2112]{1,0:T(8,128)(2,1)} %all-gather.2.cloned.1.call-done, f32[128,704]{0,1:T(8,128)S(1)} %fusion.2), kind=kOutput, calls=%fused_computation.16 | convolution fusion | flops 738738176 | bytes 8224768 | tf_op jit(solution)/shard_map/th,qfh->qtf/dot_general | solution.py:250
  281.5 15.8 %shard_map.152 = f32[4,128,512]{2,1,0:T(8,128)} custom-call(f32[4,128,512]{2,1,0:T(8,128)} %convolution_bitcast_fusion.2.x_ref), custom_call_target="tpu_custom_call" | custom-call | tf_op jit(solution)/shard_map/pallas_call | solution.py:127
  297.3 1.3 reduce_sum.95
  298.6 0.7 fusion.40
  299.3 0.6 broadcast_in_dim.25.x_ref
  300.0 5.5 %shard_map.154 = f32[32,128]{1,0:T(8,128)} custom-call(f32[8,128]{1,0:T(8,128)} %broadcast_in_dim.25.x_ref), custom_call_target="tpu_custom_call" | custom-call | tf_op jit(solution)/shard_map/pallas_call | solution.py:70
  305.5 0.7 slice_reduce_fusion.2
  306.2 0.8 fusion.42
  (40 shorter events, 0.6 us)
Async XLA Ops:
  7.2 38.8 %copy-start.6 = (bf16[128,512]{1,0:T(8,128)(2,1)S(1)}, bf16[128,512]{1,0:T(8,128)(2,1)}, u32[]{:S(2)}) copy-start(bf16[128,512]{1,0:T(8,128)(2,1)} %param.14) | copy-start | bytes 393220
  7.2 259.2 %all-gather.2.cloned.1.call-start = ((), (), s32[]{:S(2)}) async-start(), calls=%async_computation.4 | async-start | bytes 9052160 | tf_op jit(solution)/shard_map/all_gather | solution.py:244
  51.0 3.7 %copy-start.10 = (s32[128,6]{0,1:T(8,128)S(1)}, s32[128,6]{0,1:T(8,128)}, u32[]{:S(2)}) copy-start(s32[128,6]{0,1:T(8,128)} %param.24) | copy-start | bytes 9220
  51.0 5.8 %all-to-all-start = ((f32[2,128,1024]{1,2,0:T(8,128)}), f32[2,128,1024]{1,2,0:T(8,128)S(1)}, u32[]{:S(2)}, u32[]{:S(2)}) async-start(f32[2,128,1024]{1,2,0:T(8,128)} %copy.33), calls=%async_computation | async-start | bytes 2097152 | tf_op jit(solution)/shard_map/all_to_all | solution.py:142
  56.9 0.7 copy-start.8
  58.7 18.6 %copy-start.7 = (bf16[128,512]{1,0:T(8,128)(2,1)S(1)}, bf16[128,512]{1,0:T(8,128)(2,1)}, u32[]{:S(2)}) copy-start(bf16[128,512]{1,0:T(8,128)(2,1)} %param.15) | copy-start | bytes 393220
  75.9 14.2 %copy-start.12 = (s32[64]{0:T(128)S(1)}, s32[64]{0:T(128)}, u32[]{:S(2)}) copy-start(s32[64]{0:T(128)} %param.26) | copy-start | bytes 772
  77.9 13.3 %copy-start.1 = (bf16[128,512]{1,0:T(8,128)(2,1)S(1)}, bf16[128,512]{1,0:T(8,128)(2,1)}, u32[]{:S(2)}) copy-start(bf16[128,512]{1,0:T(8,128)(2,1)} %add_convert_fusion.x_ref) | copy-start | bytes 393220
  88.0 2.5 copy-start
  127.5 5.2 %copy-start.2 = (bf16[1,352,2048]{2,1,0:T(8,128)(2,1)S(1)}, bf16[1,352,2048]{2,1,0:T(8,128)(2,1)}, u32[]{:S(2)}) copy-start(bf16[1,352,2048]{2,1,0:T(8,128)(2,1)} %param.23) | copy-start | bytes 4325380
  127.5 54.3 %all-to-all-start.1 = ((bf16[4,1024,512]{2,1,0:T(8,128)(2,1)}), bf16[4,1024,512]{2,1,0:T(8,128)(2,1)}, u32[]{:S(2)}, u32[]{:S(2)}) async-start(bf16[4,1024,512]{2,1,0:T(8,128)(2,1)} %broadcast_in_dim.24), calls=%async_computation.1 | async-start | bytes 8388608 | tf_op jit(solution)/shard_map/all_to_all | solution.py:217
  134.6 4.5 %copy-start.3 = (bf16[1,2048,352]{1,2,0:T(8,128)(2,1)S(1)}, bf16[1,2048,352]{1,2,0:T(8,128)(2,1)}, u32[]{:S(2)}) copy-start(bf16[1,2048,352]{1,2,0:T(8,128)(2,1)} %param.21) | copy-start | bytes 4325380
  141.1 46.1 %copy-start.4 = (bf16[352,4,512]{2,1,0:T(4,128)(2,1)S(1)}, bf16[352,4,512]{2,1,0:T(4,128)(2,1)}, u32[]{:S(2)}) copy-start(bf16[352,4,512]{2,1,0:T(4,128)(2,1)} %reshape_squeeze.11) | copy-start | bytes 4325380
  254.5 11.1 %copy-start.9 = (f32[128,6]{0,1:T(8,128)S(1)}, f32[128,6]{0,1:T(8,128)}, u32[]{:S(2)}) copy-start(f32[128,6]{0,1:T(8,128)} %param.25) | copy-start | bytes 9220
  254.5 44.2 %all-to-all-start.3 = ((bf16[64,16,512]{2,1,0:T(8,128)(2,1)}), bf16[64,16,512]{2,1,0:T(8,128)(2,1)S(1)}, u32[]{:S(2)}, u32[]{:S(2)}) async-start(bf16[64,16,512]{2,1,0:T(8,128)(2,1)} %bitcast.22), calls=%async_computation.3 | async-start | bytes 2097152 | tf_op jit(solution)/shard_map/all_to_all | solution.py:229
  297.3 9.0 %copy-start.11 = (f32[512]{0:T(512)S(1)}, f32[512]{0:T(512)}, u32[]{:S(2)}) copy-start(f32[512]{0:T(512)} %param.27) | copy-start | bytes 6148
  299.3 7.7 %copy-start.5 = (bf16[128,512]{1,0:T(8,128)(2,1)}, bf16[128,512]{1,0:T(8,128)(2,1)S(1)}, u32[]{:S(2)}) copy-start(bf16[128,512]{1,0:T(8,128)(2,1)S(1)} %get-tuple-element.5) | copy-start | bytes 393220
Sparse Core Ops, SparseCore 0:
  10.7 87.1 all-gather.1

commit v13 on v12

--- a/solution.py
+++ b/solution.py
@@ -210,15 +210,25 @@
     flat_scores = route_scores.reshape(tok_rows, top_count)
     combine = jnp.sum(jnp.where(hit, flat_scores[:, :, None], 0.0), axis=1)
     pick = jnp.any(hit, axis=1).astype(jnp.bfloat16)
-    outgoing = matmul(pick.T, normed).astype(jnp.bfloat16)
-    arrived = exchange(outgoing.reshape(experts, capacity, block_width), "dp", 5)
-    arrived = arrived.reshape(slots, block_width)
-    copies = jnp.broadcast_to(arrived[None], (mp_count, slots, block_width))
-    in_rows = lax.all_to_all(copies, "mp", split_axis=0, concat_axis=0, tiled=True)
+    half = block_width // 2
     gate_block = expert_gate[0].reshape(mp_count, block_width, -1)
     up_block = expert_up[0].reshape(mp_count, block_width, -1)
-    gate_val = jnp.einsum("qsf,qfh->sh", in_rows, gate_block, preferred_element_type=jnp.float32)
-    up_val = jnp.einsum("qsf,qfh->sh", in_rows, up_block, preferred_element_type=jnp.float32)
+    gate_val = None
+    up_val = None
+    for part in range(2):
+        columns = slice(part * half, (part + 1) * half)
+        outgoing = matmul(pick.T, normed[:, columns]).astype(jnp.bfloat16)
+        arrived = exchange(outgoing.reshape(experts, capacity, half), "dp", 5 + part)
+        copies = jnp.broadcast_to(arrived.reshape(1, slots, half), (mp_count, slots, half))
+        in_rows = lax.all_to_all(copies, "mp", split_axis=0, concat_axis=0, tiled=True)
+        gate_part = jnp.einsum(
+            "qsf,qfh->sh", in_rows, gate_block[:, columns, :], preferred_element_type=jnp.float32
+        )
+        up_part = jnp.einsum(
+            "qsf,qfh->sh", in_rows, up_block[:, columns, :], preferred_element_type=jnp.float32
+        )
+        gate_val = gate_part if gate_val is None else gate_val + gate_part
+        up_val = up_part if up_val is None else up_val + up_part
     activated = (jax.nn.silu(gate_val) * up_val).astype(jnp.bfloat16)
     down_block = expert_down[0].reshape(-1, mp_count, block_width)
     partial_out = jnp.einsum(

time: 315 us -> 310 us (0.984)
  waiting for transfers between devices: 42.4 us -> 16.4 us
  Pallas kernels: 117 us -> 127 us
  local copies, waits for them, and re-layouts: 22.1 us -> 27.5 us
    all_to_all x1 -> x2, waiting for transfers between devices: 40.7 us -> 14.7 us  [local(): lax.all_to_all(copies, 'mp', split_axis=0, concat_axis=0, tiled=True)]
    pallas_call x3 -> x4, Pallas kernels: 64.3 us -> 74 us  [exchange(): pl.pallas_call(functools.partial(_exchange_kernel, axis), out_shape=jax.S...]
    another operation x1, local copies, waits for them, and re-layouts: 4.51 us -> 1.11 us  [local(): up_block = expert_up[0].reshape(mp_count, block_width, -1)]
    all_to_all x1 -> x2, starting transfers between devices: 5.16 us -> 8.29 us  [local(): lax.all_to_all(copies, 'mp', split_axis=0, concat_axis=0, tiled=True)]
    dot_general x1 -> x3, matrix products: 5.43 us -> 7.89 us  [the longest x2 5.81 us: local(): jnp.einsum('qsf,qfh->sh', in_rows, up_block[:, columns, :], preferred_ele...]
  transfers between devices with their start and end apart: 4 -> 5, of which waited for: 2 -> 3; matrix products, arithmetic and copies ran while one was open for 19% -> 22% of each run, Pallas kernels for 35% -> 39%
where the time goes in v13:
time: 310 us; the launch traced here: 309 us
  Pallas kernels  127 us (41%)
  blocking collectives  55.5 us (18%)
  matrix products  32.2 us (10%)
  local copies, waits for them, and re-layouts  27.5 us (9%)
  starting transfers between devices  21.7 us (7%)
  waiting for transfers between devices  16.4 us (5%)
  other arithmetic  14.8 us (5%)
  between operations  14.4 us (5%)
    pallas_call x4, Pallas kernels, exchange(): pl.pallas_call(functools.partial(_exchange_kernel, axis), out_shape=jax.S...  74 us
    all_to_all x1, blocking collectives, local(): lax.all_to_all(partial_out, 'mp', split_axis=0, concat_axis=0, tiled=True)  53.2 us
    pallas_call x3, Pallas kernels, gather_rows(): pl.pallas_call(functools.partial(_gather_kernel, axis), out_shape=jax.Sha...  52.6 us
    all_to_all x2, waiting for transfers between devices, local(): lax.all_to_all(copies, 'mp', split_axis=0, concat_axis=0, tiled=True)  14.7 us
    all_to_all x1, starting transfers between devices, local(): lax.all_to_all(expert_out.reshape(experts, capacity, block_width), dp, sp...  9.85 us
    all_to_all x2, starting transfers between devices, local(): lax.all_to_all(copies, 'mp', split_axis=0, concat_axis=0, tiled=True)  8.29 us
    dot_general x1, matrix products, local(): jnp.einsum('sh,hqf->qsf', activated, down_block, preferred_element_type=j...  8.26 us
    dot_general x1, matrix products, local(): jnp.einsum('th,qfh->qtf', shared_act, shared_all[:, 2 * hidden_units:].re...  8.04 us
  transfers between devices with their start and end apart: 5, of which 3 were waited for; matrix products, arithmetic and copies ran while one was open for 22% of the time, Pallas kernels for 39%

profile of v13, /device:TPU:8, one launch (start us, length us, event | category | flops | bytes accessed | tf_op | source)
XLA Modules:
  0.0 309.0 jit_solution(14892690446008315192)
XLA Ops:
  7.2 1.6 concatenate.7
  8.8 37.1 %shard_map.149 = bf16[1024,512]{1,0:T(8,128)(2,1)} custom-call(bf16[32,512]{1,0:T(8,128)(2,1)} %bitcast.105), custom_call_target="tpu_custom_call" | custom-call | tf_op jit(solution)/shard_map/pallas_call | solution.py:70
  45.9 2.2 all_gather.6
  48.1 1.7 fusion.49
  49.8 1.4 copy.47
  51.2 3.6 %all-to-all-start = ((f32[2,128,1024]{1,2,0:T(8,128)}), f32[2,128,1024]{1,2,0:T(8,128)S(1)}, u32[]{:S(2)}, u32[]{:S(2)}) async-start(f32[2,128,1024]{1,2,0:T(8,128)} %copy.47), calls=%async_computation | async-start | bytes 2097152 | tf_op jit(solution)/shard_map/all_to_all | solution.py:142
  55.2 1.7 all-to-all-done
  57.6 1.2 pad_maximum_fusion.x_ref
  58.8 17.2 %shard_map.150 = f32[4,129,512]{2,1,0:T(8,128)} custom-call(f32[4,129,512]{2,1,0:T(8,128)} %pad_maximum_fusion.x_ref), custom_call_target="tpu_custom_call" | custom-call | tf_op jit(solution)/shard_map/pallas_call | solution.py:127
  76.0 1.3 slice_reduce_fusion
  77.3 0.7 add_convert_fusion.x_ref
  78.0 10.1 %shard_map.151 = bf16[512,512]{1,0:T(8,128)(2,1)} custom-call(bf16[128,512]{1,0:T(8,128)(2,1)} %add_convert_fusion.x_ref), custom_call_target="tpu_custom_call" | custom-call | tf_op jit(solution)/shard_map/pallas_call | solution.py:70
  88.1 1.8 reduce-window.6
  90.6 1.2 multiply_reduce_fusion
  92.4 1.2 convolution_convert_fusion
  93.7 20.4 %shard_map.154 = bf16[64,16,256]{2,1,0:T(8,128)(2,1)} custom-call(bf16[64,16,256]{2,1,0:T(8,128)(2,1)} %bitcast.102), custom_call_target="tpu_custom_call" | custom-call | tf_op jit(solution)/shard_map/pallas_call | solution.py:127
  114.0 2.5 broadcast_in_dim.30
  116.6 3.6 %all-to-all-start.2 = ((bf16[4,1024,256]{2,1,0:T(8,128)(2,1)}), bf16[4,1024,256]{2,1,0:T(8,128)(2,1)S(1)}, u32[]{:S(2)}, u32[]{:S(2)}) async-start(bf16[4,1024,256]{2,1,0:T(8,128)(2,1)} %broadcast_in_dim.30), calls=%async_computation.2 | async-start | bytes 4194304 | tf_op jit(solution)/shard_map/all_to_all | solution.py:223
  120.2 1.2 convolution_convert_fusion.1
  121.4 20.7 %shard_map.153 = bf16[64,16,256]{2,1,0:T(8,128)(2,1)} custom-call(bf16[64,16,256]{2,1,0:T(8,128)(2,1)} %bitcast.101), custom_call_target="tpu_custom_call" | custom-call | tf_op jit(solution)/shard_map/pallas_call | solution.py:127
  142.0 5.0 %all-to-all-done.2 = bf16[4,1024,256]{2,1,0:T(8,128)(2,1)S(1)} async-done(((bf16[4,1024,256]{2,1,0:T(8,128)(2,1)}), bf16[4,1024,256]{2,1,0:T(8,128)(2,1)S(1)}, u32[]{:S(2)}, u32[]{:S(2)}) %all-to-all-start.2) | async-done | bytes 2097184 | tf_op jit(solution)/shard_map/all_to_all | solution.py:223
  147.0 2.9 broadcast_in_dim.28
  149.9 4.7 %all-to-all-start.1 = ((bf16[4,1024,256]{2,1,0:T(8,128)(2,1)}), bf16[4,1024,256]{2,1,0:T(8,128)(2,1)}, u32[]{:S(2)}, u32[]{:S(2)}) async-start(bf16[4,1024,256]{2,1,0:T(8,128)(2,1)} %broadcast_in_dim.28), calls=%async_computation.1 | async-start | bytes 4194304 | tf_op jit(solution)/shard_map/all_to_all | solution.py:223
  154.6 4.5 %reshape_squeeze.11 = bf16[352,4,512]{2,1,0:T(4,128)(2,1)} reshape(bf16[1,352,2048]{2,1,0:T(8,128)(2,1)} %param.23) | data formatting | bytes 2883584 | tf_op jit(solution)/shard_map/reshape;squeeze | solution.py:233
  159.1 1.1 reshape_squeeze.10
  160.2 3.5 %reshape_squeeze.9 = bf16[4,512,352]{1,0,2:T(4,128)(2,1)S(1)} reshape(bf16[1,2048,352]{1,2,0:T(8,128)(2,1)} %param.21) | data formatting | bytes 2883584 | tf_op jit(solution)/shard_map/reshape;squeeze | solution.py:214
  163.7 1.3 fusion.48
  165.1 0.5 fusion.47
  165.6 1.1 copy-done.3
  166.7 2.1 convolution_bitcast_fusion
  168.7 2.1 convolution_bitcast_fusion.2
  170.8 9.7 %all-to-all-done.1 = bf16[4,1024,256]{2,1,0:T(8,128)(2,1)} async-done(((bf16[4,1024,256]{2,1,0:T(8,128)(2,1)}), bf16[4,1024,256]{2,1,0:T(8,128)(2,1)}, u32[]{:S(2)}, u32[]{:S(2)}) %all-to-all-start.1) | async-done | bytes 2097184 | tf_op jit(solution)/shard_map/all_to_all | solution.py:223
  180.5 3.8 %convolution_bitcast_fusion.1 = f32[1024,352]{0,1:T(8,128)} fusion(bf16[4,1024,256]{2,1,0:T(8,128)(2,1)} %all-to-all-done.1, bf16[4,256,352]{1,0,2:T(4,128)(2,1)S(1)} %copy-done.6), kind=kOutput, calls=%fused_computation.9 | convolution fusion | flops 738197504 | bytes 4259840 | tf_op jit(solution)/shard_map/qsf,qfh->sh/dot_general | solution.py:227
  184.2 8.3 %convert_bitcast_fusion = bf16[4,1024,512]{2,1,0:T(8,128)(2,1)} fusion(bf16[352,4,512]{2,1,0:T(4,128)(2,1)S(1)} %copy-done.5, f32[1024,352]{0,1:T(8,128)} %convolution_bitcast_fusion.1, f32[1024,352]{0,1:T(8,128)} %convolution_bitcast_fusion, f32[1024,352]{0,1:T(8,128)} %convolution_bitcast_fusion.2, bf16[4,1024,256]{2,1,0:T(8,128)(2,1)} %all-to-all-done.1, ...), kind=kOutput, calls=%fused_computation | convolution fusion | flops 2219573248 | bytes 12779520 | tf_op jit(solution)/shard_map/sh,hqf->qsf/dot_general | solution.py:234
  192.5 53.2 %all_to_all.25 = bf16[4,1024,512]{2,1,0:T(8,128)(2,1)} all-to-all(bf16[4,1024,512]{2,1,0:T(8,128)(2,1)} %convert_bitcast_fusion), channel_id=1, replica_groups=mesh['g'=32,'c'=2,'mp'=4] {'mp'}, dimensions={0} | all-to-all | bytes 8388608 | tf_op jit(solution)/shard_map/all_to_all | solution.py:237
  245.8 4.1 %reduce_sum.99 = bf16[1024,512]{1,0:T(8,128)(2,1)} reduce(bf16[4,1024,512]{2,1,0:T(8,128)(2,1)} %all_to_all.25, bf16[]{:T(256)} %constant.25.clone.1), dimensions={0}, to_apply=%region_10.11 | reduce | flops 1572864 | bytes 5242882 | tf_op jit(solution)/shard_map/reduce_sum | solution.py:238
  249.9 9.8 %all-to-all-start.4 = ((bf16[64,16,512]{2,1,0:T(8,128)(2,1)}), bf16[64,16,512]{2,1,0:T(8,128)(2,1)S(1)}, u32[]{:S(2)}, u32[]{:S(2)}) async-start(bf16[64,16,512]{2,1,0:T(8,128)(2,1)} %bitcast.26), calls=%async_computation.4 | async-start | bytes 2097152 | tf_op jit(solution)/shard_map/all_to_all | solution.py:239
  259.8 0.8 slice.44
  261.6 3.8 %slice.56 = bf16[2048,704]{1,0:T(8,128)(2,1)} slice(bf16[2048,2112]{1,0:T(8,128)(2,1)} %all-gather.2.cloned.1.call-done), slice={[0:2048], [1408:2112]} | slice | bytes 5767168 | tf_op jit(solution)/shard_map/slice | solution.py:263
  265.4 3.2 %fusion.2 = f32[128,704]{0,1:T(8,128)S(1)} fusion(bf16[128,2048]{0,1:T(8,128)(2,1)S(1)} %fusion.21, bf16[2048,2112]{1,0:T(8,128)(2,1)} %all-gather.2.cloned.1.call-done), kind=kOutput, calls=%fused_computation.3 | convolution fusion | flops 369098752 | bytes 4030464 | tf_op jit(solution)/shard_map/dot_general | solution.py:19
  268.6 8.0 %convolution_bitcast_fusion.4.x_ref = f32[4,128,512]{2,1,0:T(8,128)} fusion(bf16[4,512,704]{2,1,0:T(8,128)(2,1)} %bitcast.98, bf16[128,2048]{0,1:T(8,128)(2,1)S(1)} %fusion.21, bf16[2048,2112]{1,0:T(8,128)(2,1)} %all-gather.2.cloned.1.call-done, f32[128,704]{0,1:T(8,128)S(1)} %fusion.2), kind=kOutput, calls=%fused_computation.14 | convolution fusion | flops 738738176 | bytes 8224768 | tf_op jit(solution)/shard_map/th,qfh->qtf/dot_general | solution.py:260
  276.6 15.8 %shard_map.152 = f32[4,128,512]{2,1,0:T(8,128)} custom-call(f32[4,128,512]{2,1,0:T(8,128)} %convolution_bitcast_fusion.4.x_ref), custom_call_target="tpu_custom_call" | custom-call | tf_op jit(solution)/shard_map/pallas_call | solution.py:127
  292.4 1.3 reduce_sum.95
  293.8 0.7 fusion.35
  294.5 0.6 broadcast_in_dim.54.x_ref
  295.1 5.5 %shard_map.155 = f32[32,128]{1,0:T(8,128)} custom-call(f32[8,128]{1,0:T(8,128)} %broadcast_in_dim.54.x_ref), custom_call_target="tpu_custom_call" | custom-call | tf_op jit(solution)/shard_map/pallas_call | solution.py:70
  300.6 0.7 slice_reduce_fusion.2
  301.4 0.8 fusion.37
  (52 shorter events, 3.4 us)
Async XLA Ops:
  7.2 254.4 %all-gather.2.cloned.1.call-start = ((), (), s32[]{:S(2)}) async-start(), calls=%async_computation.5 | async-start | bytes 9052160 | tf_op jit(solution)/shard_map/all_gather | solution.py:254
  49.8 5.0 %copy-start.11 = (s32[128,6]{0,1:T(8,128)S(1)}, s32[128,6]{0,1:T(8,128)}, u32[]{:S(2)}) copy-start(s32[128,6]{0,1:T(8,128)} %param.24) | copy-start | bytes 9220
  51.2 5.7 %all-to-all-start = ((f32[2,128,1024]{1,2,0:T(8,128)}), f32[2,128,1024]{1,2,0:T(8,128)S(1)}, u32[]{:S(2)}, u32[]{:S(2)}) async-start(f32[2,128,1024]{1,2,0:T(8,128)} %copy.47), calls=%async_computation | async-start | bytes 2097152 | tf_op jit(solution)/shard_map/all_to_all | solution.py:142
  56.9 0.7 copy-start.9
  58.8 18.6 %copy-start.8 = (bf16[128,512]{1,0:T(8,128)(2,1)S(1)}, bf16[128,512]{1,0:T(8,128)(2,1)}, u32[]{:S(2)}) copy-start(bf16[128,512]{1,0:T(8,128)(2,1)} %param.15) | copy-start | bytes 393220
  76.0 14.2 %copy-start.13 = (s32[64]{0:T(128)S(1)}, s32[64]{0:T(128)}, u32[]{:S(2)}) copy-start(s32[64]{0:T(128)} %param.26) | copy-start | bytes 772
  78.0 14.3 %copy-start.1 = (bf16[128,512]{1,0:T(8,128)(2,1)S(1)}, bf16[128,512]{1,0:T(8,128)(2,1)}, u32[]{:S(2)}) copy-start(bf16[128,512]{1,0:T(8,128)(2,1)} %add_convert_fusion.x_ref) | copy-start | bytes 393220
  116.6 30.4 %all-to-all-start.2 = ((bf16[4,1024,256]{2,1,0:T(8,128)(2,1)}), bf16[4,1024,256]{2,1,0:T(8,128)(2,1)S(1)}, u32[]{:S(2)}, u32[]{:S(2)}) async-start(bf16[4,1024,256]{2,1,0:T(8,128)(2,1)} %broadcast_in_dim.30), calls=%async_computation.2 | async-start | bytes 4194304 | tf_op jit(solution)/shard_map/all_to_all | solution.py:223
  147.0 2.9 copy-start.2
  149.9 30.6 %all-to-all-start.1 = ((bf16[4,1024,256]{2,1,0:T(8,128)(2,1)}), bf16[4,1024,256]{2,1,0:T(8,128)(2,1)}, u32[]{:S(2)}, u32[]{:S(2)}) async-start(bf16[4,1024,256]{2,1,0:T(8,128)(2,1)} %broadcast_in_dim.28), calls=%async_computation.1 | async-start | bytes 4194304 | tf_op jit(solution)/shard_map/all_to_all | solution.py:223
  154.6 4.5 %copy-start.4 = (bf16[1,2048,352]{1,2,0:T(8,128)(2,1)S(1)}, bf16[1,2048,352]{1,2,0:T(8,128)(2,1)}, u32[]{:S(2)}) copy-start(bf16[1,2048,352]{1,2,0:T(8,128)(2,1)} %param.22) | copy-start | bytes 4325380
  165.1 1.6 copy-start.3
  168.7 11.8 %copy-start.6 = (bf16[4,256,352]{1,0,2:T(4,128)(2,1)S(1)}, bf16[4,256,352]{1,0,2:T(4,128)(2,1)}, u32[]{:S(2)}) copy-start(bf16[4,256,352]{1,0,2:T(4,128)(2,1)} %get-tuple-element.7) | copy-start | bytes 2162692
  180.5 3.8 %copy-start.5 = (bf16[352,4,512]{2,1,0:T(4,128)(2,1)S(1)}, bf16[352,4,512]{2,1,0:T(4,128)(2,1)}, u32[]{:S(2)}) copy-start(bf16[352,4,512]{2,1,0:T(4,128)(2,1)} %reshape_squeeze.11) | copy-start | bytes 4325380
  249.9 10.7 %copy-start = (bf16[512,512]{1,0:T(8,128)(2,1)S(1)}, bf16[512,512]{1,0:T(8,128)(2,1)}, u32[]{:S(2)}) copy-start(bf16[512,512]{1,0:T(8,128)(2,1)} %shard_map.151) | copy-start | bytes 1572868
  249.9 10.9 %copy-start.10 = (f32[128,6]{0,1:T(8,128)S(1)}, f32[128,6]{0,1:T(8,128)}, u32[]{:S(2)}) copy-start(f32[128,6]{0,1:T(8,128)} %param.25) | copy-start | bytes 9220
  249.9 43.9 %all-to-all-start.4 = ((bf16[64,16,512]{2,1,0:T(8,128)(2,1)}), bf16[64,16,512]{2,1,0:T(8,128)(2,1)S(1)}, u32[]{:S(2)}, u32[]{:S(2)}) async-start(bf16[64,16,512]{2,1,0:T(8,128)(2,1)} %bitcast.26), calls=%async_computation.4 | async-start | bytes 2097152 | tf_op jit(solution)/shard_map/all_to_all | solution.py:239
  292.4 9.0 %copy-start.12 = (f32[512]{0:T(512)S(1)}, f32[512]{0:T(512)}, u32[]{:S(2)}) copy-start(f32[512]{0:T(512)} %param.27) | copy-start | bytes 6148
  294.5 7.7 %copy-start.7 = (bf16[128,512]{1,0:T(8,128)(2,1)}, bf16[128,512]{1,0:T(8,128)(2,1)S(1)}, u32[]{:S(2)}) copy-start(bf16[128,512]{1,0:T(8,128)(2,1)S(1)} %get-tuple-element.9) | copy-start | bytes 393220
Sparse Core Ops, SparseCore 0:
  10.7 87.2 all-gather.1

commit v14 on v13

--- a/solution.py
+++ b/solution.py
@@ -210,6 +210,19 @@
     flat_scores = route_scores.reshape(tok_rows, top_count)
     combine = jnp.sum(jnp.where(hit, flat_scores[:, :, None], 0.0), axis=1)
     pick = jnp.any(hit, axis=1).astype(jnp.bfloat16)
+    hidden_units = shared_gate.shape[1]
+    shared_all = lax.all_gather(
+        jnp.concatenate([shared_gate, shared_up, shared_down.T], axis=1), dp, axis=0, tiled=True
+    )
+    shared_gval = matmul(whole_rows, shared_all[:, :hidden_units])
+    shared_uval = matmul(whole_rows, shared_all[:, hidden_units : 2 * hidden_units])
+    shared_act = (jax.nn.silu(shared_gval) * shared_uval).astype(jnp.bfloat16)
+    shared_part = jnp.einsum(
+        "th,qfh->qtf",
+        shared_act,
+        shared_all[:, 2 * hidden_units :].reshape(mp_count, block_width, hidden_units),
+        preferred_element_type=jnp.float32,
+    )
     half = block_width // 2
     gate_block = expert_gate[0].reshape(mp_count, block_width, -1)
     up_block = expert_up[0].reshape(mp_count, block_width, -1)
@@ -221,6 +234,8 @@
         arrived = exchange(outgoing.reshape(experts, capacity, half), "dp", 5 + part)
         copies = jnp.broadcast_to(arrived.reshape(1, slots, half), (mp_count, slots, half))
         in_rows = lax.all_to_all(copies, "mp", split_axis=0, concat_axis=0, tiled=True)
+        if part == 1:
+            in_rows, shared_part = lax.optimization_barrier((in_rows, shared_part))
         gate_part = jnp.einsum(
             "qsf,qfh->sh", in_rows, gate_block[:, columns, :], preferred_element_type=jnp.float32
         )
@@ -250,19 +265,6 @@
         preferred_element_type=jnp.float32,
     )
 
-    hidden_units = shared_gate.shape[1]
-    shared_all = lax.all_gather(
-        jnp.concatenate([shared_gate, shared_up, shared_down.T], axis=1), dp, axis=0, tiled=True
-    )
-    shared_gval = matmul(whole_rows, shared_all[:, :hidden_units])
-    shared_uval = matmul(whole_rows, shared_all[:, hidden_units : 2 * hidden_units])
-    shared_act = (jax.nn.silu(shared_gval) * shared_uval).astype(jnp.bfloat16)
-    shared_part = jnp.einsum(
-        "th,qfh->qtf",
-        shared_act,
-        shared_all[:, 2 * hidden_units :].reshape(mp_count, block_width, hidden_units),
-        preferred_element_type=jnp.float32,
-    )
     mixture = reduce_scatter_mp(shared_part, 4) + routed
     final = (hidden_float + mixture).astype(jnp.bfloat16)
     final_float = final.astype(jnp.float32)

time: 310 us -> 323 us (1.042)
  waiting for transfers between devices: 16.4 us -> 22.6 us
  matrix products: 32.2 us -> 35.6 us
    all_to_all x1, waiting for transfers between devices: 0.01 us -> 11 us  [local(): lax.all_to_all(expert_out.reshape(experts, capacity, block_width), dp, sp...]
    all_to_all x2, waiting for transfers between devices: 14.7 us -> 9.88 us  [local(): lax.all_to_all(copies, 'mp', split_axis=0, concat_axis=0, tiled=True)]
    slice x1 -> x2, local copies, waits for them, and re-layouts: 3.76 us -> 0.01 us  [local(): shared_all[:, 2 * hidden_units:]]
  transfers between devices with their start and end apart: 5 -> 5, of which waited for: 3 -> 3; matrix products, arithmetic and copies ran while one was open for 22% -> 16% of each run, Pallas kernels for 39% -> 38%
where the time goes in v14:
time: 323 us; the launch traced here: 321 us
  Pallas kernels  127 us (39%)
  blocking collectives  56.5 us (17%)
  matrix products  35.6 us (11%)
  local copies, waits for them, and re-layouts  26.8 us (8%)
  starting transfers between devices  23.3 us (7%)
  waiting for transfers between devices  22.6 us (7%)
  other arithmetic  15.5 us (5%)
  between operations  14.3 us (4%)
    pallas_call x4, Pallas kernels, exchange(): pl.pallas_call(functools.partial(_exchange_kernel, axis), out_shape=jax.S...  74.1 us
    all_to_all x1, blocking collectives, local(): lax.all_to_all(partial_out, 'mp', split_axis=0, concat_axis=0, tiled=True)  54.3 us
    pallas_call x3, Pallas kernels, gather_rows(): pl.pallas_call(functools.partial(_gather_kernel, axis), out_shape=jax.Sha...  52.6 us
    all_to_all x1, waiting for transfers between devices, local(): lax.all_to_all(expert_out.reshape(experts, capacity, block_width), dp, sp...  11 us
    all_to_all x1, starting transfers between devices, local(): lax.all_to_all(expert_out.reshape(experts, capacity, block_width), dp, sp...  10.2 us
    all_to_all x2, waiting for transfers between devices, local(): lax.all_to_all(copies, 'mp', split_axis=0, concat_axis=0, tiled=True)  9.88 us
    all_to_all x2, starting transfers between devices, local(): lax.all_to_all(copies, 'mp', split_axis=0, concat_axis=0, tiled=True)  9.53 us
    dot_general x1, matrix products, local(): jnp.einsum('sh,hqf->qsf', activated, down_block, preferred_element_type=j...  8.2 us
  transfers between devices with their start and end apart: 5, of which 3 were waited for; matrix products, arithmetic and copies ran while one was open for 16% of the time, Pallas kernels for 38%

profile of v14, /device:TPU:8, one launch (start us, length us, event | category | flops | bytes accessed | tf_op | source)
XLA Modules:
  0.0 321.4 jit_solution(6602107923138151473)
XLA Ops:
  7.2 1.6 concatenate.7
  8.9 37.1 %shard_map.149 = bf16[1024,512]{1,0:T(8,128)(2,1)} custom-call(bf16[32,512]{1,0:T(8,128)(2,1)} %bitcast.105), custom_call_target="tpu_custom_call" | custom-call | tf_op jit(solution)/shard_map/pallas_call | solution.py:70
  45.9 2.2 all_gather.6
  48.1 1.7 fusion.49
  49.8 1.4 copy.47
  51.2 3.6 %all-to-all-start = ((f32[2,128,1024]{1,2,0:T(8,128)}), f32[2,128,1024]{1,2,0:T(8,128)S(1)}, u32[]{:S(2)}, u32[]{:S(2)}) async-start(f32[2,128,1024]{1,2,0:T(8,128)} %copy.47), calls=%async_computation | async-start | bytes 2097152 | tf_op jit(solution)/shard_map/all_to_all | solution.py:142
  55.2 1.7 all-to-all-done
  57.6 1.2 pad_maximum_fusion.x_ref
  58.8 17.2 %shard_map.150 = f32[4,129,512]{2,1,0:T(8,128)} custom-call(f32[4,129,512]{2,1,0:T(8,128)} %pad_maximum_fusion.x_ref), custom_call_target="tpu_custom_call" | custom-call | tf_op jit(solution)/shard_map/pallas_call | solution.py:127
  76.0 1.3 slice_reduce_fusion
  77.3 0.7 add_convert_fusion.x_ref
  78.0 10.1 %shard_map.151 = bf16[512,512]{1,0:T(8,128)(2,1)} custom-call(bf16[128,512]{1,0:T(8,128)(2,1)} %add_convert_fusion.x_ref), custom_call_target="tpu_custom_call" | custom-call | tf_op jit(solution)/shard_map/pallas_call | solution.py:70
  88.1 1.8 reduce-window.6
  90.6 1.2 multiply_reduce_fusion
  92.5 1.1 convolution_convert_fusion
  93.6 19.8 %shard_map.154 = bf16[64,16,256]{2,1,0:T(8,128)(2,1)} custom-call(bf16[64,16,256]{2,1,0:T(8,128)(2,1)} %bitcast.102), custom_call_target="tpu_custom_call" | custom-call | tf_op jit(solution)/shard_map/pallas_call | solution.py:127
  113.4 2.5 broadcast_in_dim.30
  115.9 4.7 %all-to-all-start.2 = ((bf16[4,1024,256]{2,1,0:T(8,128)(2,1)}), bf16[4,1024,256]{2,1,0:T(8,128)(2,1)}, u32[]{:S(2)}, u32[]{:S(2)}) async-start(bf16[4,1024,256]{2,1,0:T(8,128)(2,1)} %broadcast_in_dim.30), calls=%async_computation.2 | async-start | bytes 4194304 | tf_op jit(solution)/shard_map/all_to_all | solution.py:236
  120.6 0.8 slice.47
  121.4 1.2 copy.55
  122.6 1.1 convolution_convert_fusion.1
  123.8 21.2 %shard_map.152 = bf16[64,16,256]{2,1,0:T(8,128)(2,1)} custom-call(bf16[64,16,256]{2,1,0:T(8,128)(2,1)} %bitcast.101), custom_call_target="tpu_custom_call" | custom-call | tf_op jit(solution)/shard_map/pallas_call | solution.py:127
  144.9 3.5 %reshape_squeeze.10 = bf16[4,512,352]{1,0,2:T(4,128)(2,1)S(1)} reshape(bf16[1,2048,352]{1,2,0:T(8,128)(2,1)} %param.22) | data formatting | bytes 2883584 | tf_op jit(solution)/shard_map/reshape;squeeze | solution.py:228
  148.4 3.5 %reshape_squeeze.9 = bf16[4,512,352]{1,0,2:T(4,128)(2,1)S(1)} reshape(bf16[1,2048,352]{1,2,0:T(8,128)(2,1)} %param.21) | data formatting | bytes 2883584 | tf_op jit(solution)/shard_map/reshape;squeeze | solution.py:227
  151.9 4.4 %reshape_squeeze.11 = bf16[352,4,512]{2,1,0:T(4,128)(2,1)} reshape(bf16[1,352,2048]{2,1,0:T(8,128)(2,1)} %param.23) | data formatting | bytes 2883584 | tf_op jit(solution)/shard_map/reshape;squeeze | solution.py:248
  156.3 1.6 fusion.48
  157.9 1.6 fusion.47
  159.5 1.4 broadcast_in_dim.26
  160.9 4.9 %all-to-all-start.1 = ((bf16[4,1024,256]{2,1,0:T(8,128)(2,1)}), bf16[4,1024,256]{2,1,0:T(8,128)(2,1)}, u32[]{:S(2)}, u32[]{:S(2)}) async-start(bf16[4,1024,256]{2,1,0:T(8,128)(2,1)} %broadcast_in_dim.26), calls=%async_computation.1 | async-start | bytes 4194304 | tf_op jit(solution)/shard_map/all_to_all | solution.py:236
  165.8 1.1 fusion.21
  167.0 3.6 %convolution_bitcast_fusion.1 = f32[1024,352]{0,1:T(8,128)} fusion(bf16[4,1024,256]{2,1,0:T(8,128)(2,1)} %all-to-all-done.2, bf16[4,256,352]{1,0,2:T(4,128)(2,1)S(1)} %copy-done.7), kind=kOutput, calls=%fused_computation.9 | convolution fusion | flops 738197504 | bytes 4259840 | tf_op jit(solution)/shard_map/qsf,qfh->sh/dot_general | solution.py:242
  170.6 1.0 copy-done.9
  171.7 4.1 %fusion.2 = f32[128,704]{0,1:T(8,128)} fusion(bf16[128,2048]{0,1:T(8,128)(2,1)S(1)} %copy-done.9, bf16[2048,2112]{1,0:T(8,128)(2,1)} %all-gather.2.cloned.1.call-done), kind=kOutput, calls=%fused_computation.3 | convolution fusion | flops 369098752 | bytes 4030464 | tf_op jit(solution)/shard_map/dot_general | solution.py:19
  175.7 7.3 %convolution_bitcast_fusion.4.x_ref = f32[4,128,512]{2,1,0:T(8,128)} fusion(bf16[4,512,704]{2,1,0:T(8,128)(2,1)S(1)} %bitcast.98, bf16[128,2048]{0,1:T(8,128)(2,1)} %fusion.21, bf16[2048,2112]{1,0:T(8,128)(2,1)} %all-gather.2.cloned.1.call-done, f32[128,704]{0,1:T(8,128)} %fusion.2), kind=kOutput, calls=%fused_computation.14 | convolution fusion | flops 738738176 | bytes 7962624 | tf_op jit(solution)/shard_map/th,qfh->qtf/dot_general | solution.py:220
  183.0 9.9 %all-to-all-done.1 = bf16[4,1024,256]{2,1,0:T(8,128)(2,1)} async-done(((bf16[4,1024,256]{2,1,0:T(8,128)(2,1)}), bf16[4,1024,256]{2,1,0:T(8,128)(2,1)}, u32[]{:S(2)}, u32[]{:S(2)}) %all-to-all-start.1) | async-done | bytes 2097184 | tf_op jit(solution)/shard_map/all_to_all | solution.py:236
  192.9 3.9 %convolution_bitcast_fusion = f32[1024,352]{0,1:T(8,128)} fusion(bf16[4,1024,256]{2,1,0:T(8,128)(2,1)} %all-to-all-done.1, bf16[4,256,352]{1,0,2:T(4,128)(2,1)} %get-tuple-element.10), kind=kOutput, calls=%fused_computation.8 | convolution fusion | flops 738197504 | bytes 4259840 | tf_op jit(solution)/shard_map/qsf,qfh->sh/dot_general | solution.py:242
  196.8 3.8 %convolution_bitcast_fusion.2 = f32[1024,352]{0,1:T(8,128)} fusion(bf16[4,1024,256]{2,1,0:T(8,128)(2,1)} %all-to-all-done.1, bf16[4,256,352]{1,0,2:T(4,128)(2,1)S(1)} %copy-done.6), kind=kOutput, calls=%fused_computation.10 | convolution fusion | flops 738197504 | bytes 4259840 | tf_op jit(solution)/shard_map/qsf,qfh->sh/dot_general | solution.py:239
  200.6 8.2 %convert_bitcast_fusion = bf16[4,1024,512]{2,1,0:T(8,128)(2,1)} fusion(bf16[352,4,512]{2,1,0:T(4,128)(2,1)S(1)} %copy-done.4, f32[1024,352]{0,1:T(8,128)} %convolution_bitcast_fusion.1, f32[1024,352]{0,1:T(8,128)} %convolution_bitcast_fusion, f32[1024,352]{0,1:T(8,128)} %convolution_bitcast_fusion.2, bf16[4,1024,256]{2,1,0:T(8,128)(2,1)} %all-to-all-done.2, ...), kind=kOutput, calls=%fused_computation | convolution fusion | flops 2219573248 | bytes 12779520 | tf_op jit(solution)/shard_map/sh,hqf->qsf/dot_general | solution.py:249
  208.8 54.3 %all_to_all.25 = bf16[4,1024,512]{2,1,0:T(8,128)(2,1)} all-to-all(bf16[4,1024,512]{2,1,0:T(8,128)(2,1)} %convert_bitcast_fusion), channel_id=1, replica_groups=mesh['g'=32,'c'=2,'mp'=4] {'mp'}, dimensions={0} | all-to-all | bytes 8388608 | tf_op jit(solution)/shard_map/all_to_all | solution.py:252
  263.1 4.1 %reduce_sum.99 = bf16[1024,512]{1,0:T(8,128)(2,1)} reduce(bf16[4,1024,512]{2,1,0:T(8,128)(2,1)} %all_to_all.25, bf16[]{:T(256)} %constant.25.clone.1), dimensions={0}, to_apply=%region_10.11 | reduce | flops 1572864 | bytes 5242882 | tf_op jit(solution)/shard_map/reduce_sum | solution.py:253
  267.3 10.2 %all-to-all-start.4 = ((bf16[64,16,512]{2,1,0:T(8,128)(2,1)}), bf16[64,16,512]{2,1,0:T(8,128)(2,1)S(1)}, u32[]{:S(2)}, u32[]{:S(2)}) async-start(bf16[64,16,512]{2,1,0:T(8,128)(2,1)} %bitcast.26), calls=%async_computation.4 | async-start | bytes 2097152 | tf_op jit(solution)/shard_map/all_to_all | solution.py:254
  277.9 16.0 %shard_map.153 = f32[4,128,512]{2,1,0:T(8,128)} custom-call(f32[4,128,512]{2,1,0:T(8,128)} %convolution_bitcast_fusion.4.x_ref), custom_call_target="tpu_custom_call" | custom-call | tf_op jit(solution)/shard_map/pallas_call | solution.py:127
  293.9 1.3 reduce_sum.97
  295.2 11.0 %all-to-all-done.4 = bf16[64,16,512]{2,1,0:T(8,128)(2,1)S(1)} async-done(((bf16[64,16,512]{2,1,0:T(8,128)(2,1)}), bf16[64,16,512]{2,1,0:T(8,128)(2,1)S(1)}, u32[]{:S(2)}, u32[]{:S(2)}) %all-to-all-start.4) | async-done | bytes 1048608 | tf_op jit(solution)/shard_map/all_to_all | solution.py:254
  306.2 0.7 fusion.35
  307.6 5.5 %shard_map.155 = f32[32,128]{1,0:T(8,128)} custom-call(f32[8,128]{1,0:T(8,128)} %broadcast_in_dim.54.x_ref), custom_call_target="tpu_custom_call" | custom-call | tf_op jit(solution)/shard_map/pallas_call | solution.py:70
  313.1 0.7 slice_reduce_fusion.2
  313.8 0.8 fusion.37
  (57 shorter events, 3.5 us)
Async XLA Ops:
  7.2 163.4 %all-gather.2.cloned.1.call-start = ((), (), s32[]{:S(2)}) async-start(), calls=%async_computation.5 | async-start | bytes 9052160 | tf_op jit(solution)/shard_map/all_gather | solution.py:214
  49.8 5.0 %copy-start.13 = (s32[128,6]{0,1:T(8,128)S(1)}, s32[128,6]{0,1:T(8,128)}, u32[]{:S(2)}) copy-start(s32[128,6]{0,1:T(8,128)} %param.24) | copy-start | bytes 9220
  51.2 5.7 %all-to-all-start = ((f32[2,128,1024]{1,2,0:T(8,128)}), f32[2,128,1024]{1,2,0:T(8,128)S(1)}, u32[]{:S(2)}, u32[]{:S(2)}) async-start(f32[2,128,1024]{1,2,0:T(8,128)} %copy.47), calls=%async_computation | async-start | bytes 2097152 | tf_op jit(solution)/shard_map/all_to_all | solution.py:142
  56.9 0.7 copy-start.11
  58.8 18.6 %copy-start.10 = (bf16[128,512]{1,0:T(8,128)(2,1)S(1)}, bf16[128,512]{1,0:T(8,128)(2,1)}, u32[]{:S(2)}) copy-start(bf16[128,512]{1,0:T(8,128)(2,1)} %param.15) | copy-start | bytes 393220
  76.0 14.2 %copy-start.15 = (s32[64]{0:T(128)S(1)}, s32[64]{0:T(128)}, u32[]{:S(2)}) copy-start(s32[64]{0:T(128)} %param.26) | copy-start | bytes 772
  78.0 14.3 %copy-start.3 = (bf16[128,512]{1,0:T(8,128)(2,1)S(1)}, bf16[128,512]{1,0:T(8,128)(2,1)}, u32[]{:S(2)}) copy-start(bf16[128,512]{1,0:T(8,128)(2,1)} %add_convert_fusion.x_ref) | copy-start | bytes 393220
  115.9 5.5 %copy-start = (bf16[512,512]{1,0:T(8,128)(2,1)S(1)}, bf16[512,512]{1,0:T(8,128)(2,1)}, u32[]{:S(2)}) copy-start(bf16[512,512]{1,0:T(8,128)(2,1)} %shard_map.151) | copy-start | bytes 1572868
  115.9 43.6 %all-to-all-start.2 = ((bf16[4,1024,256]{2,1,0:T(8,128)(2,1)}), bf16[4,1024,256]{2,1,0:T(8,128)(2,1)}, u32[]{:S(2)}, u32[]{:S(2)}) async-start(bf16[4,1024,256]{2,1,0:T(8,128)(2,1)} %broadcast_in_dim.30), calls=%async_computation.2 | async-start | bytes 4194304 | tf_op jit(solution)/shard_map/all_to_all | solution.py:236
  157.9 1.6 copy-start.2
  160.9 4.9 %copy-start.1 = (f32[4,128,512]{1,2,0:T(8,128)S(1)}, f32[4,128,512]{1,2,0:T(8,128)}, u32[]{:S(2)}) copy-start(f32[4,128,512]{1,2,0:T(8,128)} %copy.55) | copy-start | bytes 3145732
  160.9 6.0 %copy-start.7 = (bf16[4,256,352]{1,0,2:T(4,128)(2,1)S(1)}, bf16[4,256,352]{1,0,2:T(4,128)(2,1)}, u32[]{:S(2)}) copy-start(bf16[4,256,352]{1,0,2:T(4,128)(2,1)} %get-tuple-element.11) | copy-start | bytes 2162692
  160.9 32.0 %all-to-all-start.1 = ((bf16[4,1024,256]{2,1,0:T(8,128)(2,1)}), bf16[4,1024,256]{2,1,0:T(8,128)(2,1)}, u32[]{:S(2)}, u32[]{:S(2)}) async-start(bf16[4,1024,256]{2,1,0:T(8,128)(2,1)} %broadcast_in_dim.26), calls=%async_computation.1 | async-start | bytes 4194304 | tf_op jit(solution)/shard_map/all_to_all | solution.py:236
  170.6 1.0 copy-start.9
  171.7 4.1 %slice-start = ((bf16[2048,2112]{1,0:T(8,128)(2,1)}), bf16[2048,704]{1,0:T(8,128)(2,1)S(1)}, s32[]{:S(2)}) async-start(bf16[2048,2112]{1,0:T(8,128)(2,1)} %all-gather.2.cloned.1.call-done), calls=%async_computation.6 | async-start | bytes 6291456 | tf_op jit(solution)/shard_map/slice | solution.py:223
  192.9 3.9 %copy-start.6 = (bf16[4,256,352]{1,0,2:T(4,128)(2,1)S(1)}, bf16[4,256,352]{1,0,2:T(4,128)(2,1)}, u32[]{:S(2)}) copy-start(bf16[4,256,352]{1,0,2:T(4,128)(2,1)} %get-tuple-element.9) | copy-start | bytes 2162692
  196.8 3.8 %copy-start.4 = (bf16[352,4,512]{2,1,0:T(4,128)(2,1)S(1)}, bf16[352,4,512]{2,1,0:T(4,128)(2,1)}, u32[]{:S(2)}) copy-start(bf16[352,4,512]{2,1,0:T(4,128)(2,1)} %reshape_squeeze.11) | copy-start | bytes 4325380
  196.8 3.8 %copy-start.5 = (bf16[4,256,352]{1,0,2:T(4,128)(2,1)S(1)}, bf16[4,256,352]{1,0,2:T(4,128)(2,1)}, u32[]{:S(2)}) copy-start(bf16[4,256,352]{1,0,2:T(4,128)(2,1)} %get-tuple-element.8) | copy-start | bytes 2162692
  267.2 10.2 %copy-start.12 = (f32[128,6]{0,1:T(8,128)S(1)}, f32[128,6]{0,1:T(8,128)}, u32[]{:S(2)}) copy-start(f32[128,6]{0,1:T(8,128)} %param.25) | copy-start | bytes 9220
  267.3 39.0 %all-to-all-start.4 = ((bf16[64,16,512]{2,1,0:T(8,128)(2,1)}), bf16[64,16,512]{2,1,0:T(8,128)(2,1)S(1)}, u32[]{:S(2)}, u32[]{:S(2)}) async-start(bf16[64,16,512]{2,1,0:T(8,128)(2,1)} %bitcast.26), calls=%async_computation.4 | async-start | bytes 2097152 | tf_op jit(solution)/shard_map/all_to_all | solution.py:254
  293.9 20.0 %copy-start.14 = (f32[512]{0:T(512)S(1)}, f32[512]{0:T(512)}, u32[]{:S(2)}) copy-start(f32[512]{0:T(512)} %param.27) | copy-start | bytes 6148
  306.9 7.7 %copy-start.8 = (bf16[128,512]{1,0:T(8,128)(2,1)}, bf16[128,512]{1,0:T(8,128)(2,1)S(1)}, u32[]{:S(2)}) copy-start(bf16[128,512]{1,0:T(8,128)(2,1)S(1)} %get-tuple-element.13) | copy-start | bytes 393220
Sparse Core Ops, SparseCore 0:
  10.7 87.3 all-gather.1

commit v15 on v13

--- a/solution.py
+++ b/solution.py
@@ -210,12 +210,13 @@
     flat_scores = route_scores.reshape(tok_rows, top_count)
     combine = jnp.sum(jnp.where(hit, flat_scores[:, :, None], 0.0), axis=1)
     pick = jnp.any(hit, axis=1).astype(jnp.bfloat16)
-    half = block_width // 2
+    chunks = 4
+    half = block_width // chunks
     gate_block = expert_gate[0].reshape(mp_count, block_width, -1)
     up_block = expert_up[0].reshape(mp_count, block_width, -1)
     gate_val = None
     up_val = None
-    for part in range(2):
+    for part in range(chunks):
         columns = slice(part * half, (part + 1) * half)
         outgoing = matmul(pick.T, normed[:, columns]).astype(jnp.bfloat16)
         arrived = exchange(outgoing.reshape(experts, capacity, half), "dp", 5 + part)

time: 310 us -> 349 us (1.13)
  Pallas kernels: 127 us -> 148 us
  starting transfers between devices: 21.7 us -> 30.9 us
  local copies, waits for them, and re-layouts: 27.5 us -> 35.2 us
  matrix products: 32.2 us -> 39.1 us
  waiting for transfers between devices: 16.4 us -> 10.3 us
    pallas_call x4 -> x6, Pallas kernels: 74 us -> 95.2 us  [exchange(): pl.pallas_call(functools.partial(_exchange_kernel, axis), out_shape=jax.S...]
    all_to_all x2 -> x4, starting transfers between devices: 8.29 us -> 17.9 us  [local(): lax.all_to_all(copies, 'mp', split_axis=0, concat_axis=0, tiled=True)]
    all_to_all x2 -> x4, waiting for transfers between devices: 14.7 us -> 8.58 us  [local(): lax.all_to_all(copies, 'mp', split_axis=0, concat_axis=0, tiled=True)]
    dot_general x3 -> x5, matrix products: 5.58 us -> 9 us  [matmul(): return jnp.dot(left, right, preferred_element_type=jnp.float32)]
    broadcast_in_dim x2 -> x4, local copies, waits for them, and re-layouts: 5.45 us -> 8.5 us  [local(): jnp.broadcast_to(arrived.reshape(1, slots, half), (mp_count, slots, half))]
  transfers between devices with their start and end apart: 5 -> 7, of which waited for: 3 -> 2; matrix products, arithmetic and copies ran while one was open for 22% -> 24% of each run, Pallas kernels for 39% -> 41%
where the time goes in v15:
time: 349 us; the launch traced here: 347 us
  Pallas kernels  148 us (42%)
  blocking collectives  55.9 us (16%)
  matrix products  39.1 us (11%)
  local copies, waits for them, and re-layouts  35.2 us (10%)
  starting transfers between devices  30.9 us (9%)
  between operations  14.4 us (4%)
  other arithmetic  13.8 us (4%)
  waiting for transfers between devices  10.3 us (3%)
    pallas_call x6, Pallas kernels, exchange(): pl.pallas_call(functools.partial(_exchange_kernel, axis), out_shape=jax.S...  95.2 us
    all_to_all x1, blocking collectives, local(): lax.all_to_all(partial_out, 'mp', split_axis=0, concat_axis=0, tiled=True)  53.9 us
    pallas_call x3, Pallas kernels, gather_rows(): pl.pallas_call(functools.partial(_gather_kernel, axis), out_shape=jax.Sha...  52.6 us
    all_to_all x4, starting transfers between devices, local(): lax.all_to_all(copies, 'mp', split_axis=0, concat_axis=0, tiled=True)  17.9 us
    all_to_all x1, starting transfers between devices, local(): lax.all_to_all(expert_out.reshape(experts, capacity, block_width), dp, sp...  9.25 us
    dot_general x5, matrix products, matmul(): return jnp.dot(left, right, preferred_element_type=jnp.float32)  9 us
    all_to_all x4, waiting for transfers between devices, local(): lax.all_to_all(copies, 'mp', split_axis=0, concat_axis=0, tiled=True)  8.58 us
    broadcast_in_dim x4, local copies, waits for them, and re-layouts, local(): jnp.broadcast_to(arrived.reshape(1, slots, half), (mp_count, slots, half))  8.5 us
  transfers between devices with their start and end apart: 7, of which 2 were waited for; matrix products, arithmetic and copies ran while one was open for 24% of the time, Pallas kernels for 41%

profile of v15, /device:TPU:8, one launch (start us, length us, event | category | flops | bytes accessed | tf_op | source)
XLA Modules:
  0.0 347.3 jit_solution(14532430938424176892)
XLA Ops:
  7.2 1.7 concatenate.7
  8.9 37.1 %shard_map.149 = bf16[1024,512]{1,0:T(8,128)(2,1)} custom-call(bf16[32,512]{1,0:T(8,128)(2,1)} %bitcast.127), custom_call_target="tpu_custom_call" | custom-call | tf_op jit(solution)/shard_map/pallas_call | solution.py:70
  46.0 2.0 all_gather.6
  48.0 1.7 fusion.55
  49.7 1.4 copy.51
  51.0 3.7 %all-to-all-start = ((f32[2,128,1024]{1,2,0:T(8,128)}), f32[2,128,1024]{1,2,0:T(8,128)S(1)}, u32[]{:S(2)}, u32[]{:S(2)}) async-start(f32[2,128,1024]{1,2,0:T(8,128)} %copy.51), calls=%async_computation | async-start | bytes 2097152 | tf_op jit(solution)/shard_map/all_to_all | solution.py:142
  55.2 1.7 all-to-all-done
  58.8 17.2 %shard_map.150 = f32[4,129,512]{2,1,0:T(8,128)} custom-call(f32[4,129,512]{2,1,0:T(8,128)} %pad_maximum_fusion.x_ref), custom_call_target="tpu_custom_call" | custom-call | tf_op jit(solution)/shard_map/pallas_call | solution.py:127
  76.0 1.4 slice_reduce_fusion
  78.1 10.0 %shard_map.151 = bf16[512,512]{1,0:T(8,128)(2,1)} custom-call(bf16[128,512]{1,0:T(8,128)(2,1)} %add_convert_fusion.x_ref), custom_call_target="tpu_custom_call" | custom-call | tf_op jit(solution)/shard_map/pallas_call | solution.py:70
  88.1 1.8 reduce-window.6
  92.5 15.3 %shard_map.156 = bf16[64,16,128]{2,1,0:T(8,128)(2,1)} custom-call(bf16[64,16,128]{2,1,0:T(8,128)(2,1)} %bitcast.122), custom_call_target="tpu_custom_call" | custom-call | tf_op jit(solution)/shard_map/pallas_call | solution.py:127
  107.8 2.1 broadcast_in_dim.71
  109.9 3.5 %all-to-all-start.4 = ((bf16[4,1024,128]{2,1,0:T(8,128)(2,1)}), bf16[4,1024,128]{2,1,0:T(8,128)(2,1)S(1)}, u32[]{:S(2)}, u32[]{:S(2)}) async-start(bf16[4,1024,128]{2,1,0:T(8,128)(2,1)} %broadcast_in_dim.71), calls=%async_computation.4 | async-start | bytes 2097152 | tf_op jit(solution)/shard_map/all_to_all | solution.py:224
  114.5 15.7 %shard_map.155 = bf16[64,16,128]{2,1,0:T(8,128)(2,1)} custom-call(bf16[64,16,128]{2,1,0:T(8,128)(2,1)} %bitcast.123), custom_call_target="tpu_custom_call" | custom-call | tf_op jit(solution)/shard_map/pallas_call | solution.py:127
  130.2 2.1 broadcast_in_dim.69
  132.3 4.7 %all-to-all-start.3 = ((bf16[4,1024,128]{2,1,0:T(8,128)(2,1)}), bf16[4,1024,128]{2,1,0:T(8,128)(2,1)S(1)}, u32[]{:S(2)}, u32[]{:S(2)}) async-start(bf16[4,1024,128]{2,1,0:T(8,128)(2,1)} %broadcast_in_dim.69), calls=%async_computation.3 | async-start | bytes 2097152 | tf_op jit(solution)/shard_map/all_to_all | solution.py:224
  137.1 3.5 reshape_squeeze.10
  140.6 1.9 convolution_convert_fusion.2
  142.5 15.6 %shard_map.154 = bf16[64,16,128]{2,1,0:T(8,128)(2,1)} custom-call(bf16[64,16,128]{2,1,0:T(8,128)(2,1)} %bitcast.124), custom_call_target="tpu_custom_call" | custom-call | tf_op jit(solution)/shard_map/pallas_call | solution.py:127
  158.1 1.5 fusion.54
  159.6 2.1 broadcast_in_dim.67
  161.8 4.8 %all-to-all-start.2 = ((bf16[4,1024,128]{2,1,0:T(8,128)(2,1)}), bf16[4,1024,128]{2,1,0:T(8,128)(2,1)S(1)}, u32[]{:S(2)}, u32[]{:S(2)}) async-start(bf16[4,1024,128]{2,1,0:T(8,128)(2,1)} %broadcast_in_dim.67), calls=%async_computation.2 | async-start | bytes 2097152 | tf_op jit(solution)/shard_map/all_to_all | solution.py:224
  166.6 1.8 convolution_convert_fusion.3
  168.3 4.4 %reshape_squeeze.11 = bf16[352,4,512]{2,1,0:T(4,128)(2,1)} reshape(bf16[1,352,2048]{2,1,0:T(8,128)(2,1)} %param.23) | data formatting | bytes 2883584 | tf_op jit(solution)/shard_map/reshape;squeeze | solution.py:234
  172.7 15.6 %shard_map.153 = bf16[64,16,128]{2,1,0:T(8,128)(2,1)} custom-call(bf16[64,16,128]{2,1,0:T(8,128)(2,1)} %bitcast.121), custom_call_target="tpu_custom_call" | custom-call | tf_op jit(solution)/shard_map/pallas_call | solution.py:127
  188.4 4.4 %reshape_squeeze.9 = bf16[4,512,352]{1,0,2:T(4,128)(2,1)} reshape(bf16[1,2048,352]{1,2,0:T(8,128)(2,1)} %param.21) | data formatting | bytes 2883584 | tf_op jit(solution)/shard_map/reshape;squeeze | solution.py:215
  192.8 2.7 fusion.53
  195.5 1.7 convolution_bitcast_fusion
  197.2 1.7 convolution_bitcast_fusion.4
  198.9 2.1 broadcast_in_dim.36
  201.0 4.8 %all-to-all-start.1 = ((bf16[4,1024,128]{2,1,0:T(8,128)(2,1)}), bf16[4,1024,128]{2,1,0:T(8,128)(2,1)S(1)}, u32[]{:S(2)}, u32[]{:S(2)}) async-start(bf16[4,1024,128]{2,1,0:T(8,128)(2,1)} %broadcast_in_dim.36), calls=%async_computation.1 | async-start | bytes 2097152 | tf_op jit(solution)/shard_map/all_to_all | solution.py:224
  205.8 1.7 convolution_bitcast_fusion.1
  207.5 1.7 convolution_bitcast_fusion.5
  209.2 1.7 convolution_bitcast_fusion.2
  210.9 1.7 convolution_bitcast_fusion.6
  212.6 8.6 %all-to-all-done.1 = bf16[4,1024,128]{2,1,0:T(8,128)(2,1)S(1)} async-done(((bf16[4,1024,128]{2,1,0:T(8,128)(2,1)}), bf16[4,1024,128]{2,1,0:T(8,128)(2,1)S(1)}, u32[]{:S(2)}, u32[]{:S(2)}) %all-to-all-start.1) | async-done | bytes 1048608 | tf_op jit(solution)/shard_map/all_to_all | solution.py:224
  221.2 1.7 convolution_bitcast_fusion.3
  222.9 7.8 %convert_bitcast_fusion = bf16[4,1024,512]{2,1,0:T(8,128)(2,1)} fusion(bf16[352,4,512]{2,1,0:T(4,128)(2,1)S(1)} %copy-done.6, f32[1024,352]{0,1:T(8,128)} %convolution_bitcast_fusion, f32[1024,352]{0,1:T(8,128)} %convolution_bitcast_fusion.1, f32[1024,352]{0,1:T(8,128)} %convolution_bitcast_fusion.3, f32[1024,352]{0,1:T(8,128)} %convolution_bitcast_fusion.2, ...), kind=kOutput, calls=%fused_computation | convolution fusion | flops 1851916288 | bytes 17137664 | tf_op jit(solution)/shard_map/sh,hqf->qsf/dot_general | solution.py:235
  230.7 53.9 %all_to_all.35 = bf16[4,1024,512]{2,1,0:T(8,128)(2,1)} all-to-all(bf16[4,1024,512]{2,1,0:T(8,128)(2,1)} %convert_bitcast_fusion), channel_id=1, replica_groups=mesh['g'=32,'c'=2,'mp'=4] {'mp'}, dimensions={0} | all-to-all | bytes 8388608 | tf_op jit(solution)/shard_map/all_to_all | solution.py:238
  284.7 4.2 %reduce_sum.99 = bf16[1024,512]{1,0:T(8,128)(2,1)} reduce(bf16[4,1024,512]{2,1,0:T(8,128)(2,1)} %all_to_all.35, bf16[]{:T(256)} %constant.25.clone.1), dimensions={0}, to_apply=%region_10.11 | reduce | flops 1572864 | bytes 5242882 | tf_op jit(solution)/shard_map/reduce_sum | solution.py:239
  288.8 9.2 %all-to-all-start.6 = ((bf16[64,16,512]{2,1,0:T(8,128)(2,1)}), bf16[64,16,512]{2,1,0:T(8,128)(2,1)S(1)}, u32[]{:S(2)}, u32[]{:S(2)}) async-start(bf16[64,16,512]{2,1,0:T(8,128)(2,1)} %bitcast.34), calls=%async_computation.6 | async-start | bytes 2097152 | tf_op jit(solution)/shard_map/all_to_all | solution.py:240
  299.9 3.8 %slice.80 = bf16[2048,704]{1,0:T(8,128)(2,1)} slice(bf16[2048,2112]{1,0:T(8,128)(2,1)} %all-gather.2.cloned.1.call-done), slice={[0:2048], [1408:2112]} | slice | bytes 5767168 | tf_op jit(solution)/shard_map/slice | solution.py:264
  303.7 3.2 fusion.2
  306.9 8.0 %convolution_bitcast_fusion.8.x_ref = f32[4,128,512]{2,1,0:T(8,128)} fusion(bf16[4,512,704]{2,1,0:T(8,128)(2,1)} %bitcast.116, bf16[128,2048]{0,1:T(8,128)(2,1)S(1)} %fusion.21, bf16[2048,2112]{1,0:T(8,128)(2,1)} %all-gather.2.cloned.1.call-done, f32[128,704]{0,1:T(8,128)S(1)} %fusion.2), kind=kOutput, calls=%fused_computation.18 | convolution fusion | flops 738738176 | bytes 8224768 | tf_op jit(solution)/shard_map/th,qfh->qtf/dot_general | solution.py:261
  314.9 15.8 %shard_map.152 = f32[4,128,512]{2,1,0:T(8,128)} custom-call(f32[4,128,512]{2,1,0:T(8,128)} %convolution_bitcast_fusion.8.x_ref), custom_call_target="tpu_custom_call" | custom-call | tf_op jit(solution)/shard_map/pallas_call | solution.py:127
  330.8 1.3 reduce_sum.95
  333.5 5.5 %shard_map.157 = f32[32,128]{1,0:T(8,128)} custom-call(f32[8,128]{1,0:T(8,128)} %broadcast_in_dim.72.x_ref), custom_call_target="tpu_custom_call" | custom-call | tf_op jit(solution)/shard_map/pallas_call | solution.py:70
  (84 shorter events, 11.3 us)
Async XLA Ops:
  7.2 38.8 %copy-start.16 = (bf16[128,512]{1,0:T(8,128)(2,1)S(1)}, bf16[128,512]{1,0:T(8,128)(2,1)}, u32[]{:S(2)}) copy-start(bf16[128,512]{1,0:T(8,128)(2,1)} %param.14) | copy-start | bytes 393220
  7.2 292.7 %all-gather.2.cloned.1.call-start = ((), (), s32[]{:S(2)}) async-start(), calls=%async_computation.7 | async-start | bytes 9052160 | tf_op jit(solution)/shard_map/all_gather | solution.py:255
  51.0 3.7 %copy-start.20 = (s32[128,6]{0,1:T(8,128)S(1)}, s32[128,6]{0,1:T(8,128)}, u32[]{:S(2)}) copy-start(s32[128,6]{0,1:T(8,128)} %param.24) | copy-start | bytes 9220
  51.0 5.8 %all-to-all-start = ((f32[2,128,1024]{1,2,0:T(8,128)}), f32[2,128,1024]{1,2,0:T(8,128)S(1)}, u32[]{:S(2)}, u32[]{:S(2)}) async-start(f32[2,128,1024]{1,2,0:T(8,128)} %copy.51), calls=%async_computation | async-start | bytes 2097152 | tf_op jit(solution)/shard_map/all_to_all | solution.py:142
  57.0 0.7 copy-start.18
  58.8 18.6 %copy-start.17 = (bf16[128,512]{1,0:T(8,128)(2,1)S(1)}, bf16[128,512]{1,0:T(8,128)(2,1)}, u32[]{:S(2)}) copy-start(bf16[128,512]{1,0:T(8,128)(2,1)} %param.15) | copy-start | bytes 393220
  76.0 14.2 %copy-start.22 = (s32[64]{0:T(128)S(1)}, s32[64]{0:T(128)}, u32[]{:S(2)}) copy-start(s32[64]{0:T(128)} %param.26) | copy-start | bytes 772
  78.1 13.2 %copy-start.4 = (bf16[128,512]{1,0:T(8,128)(2,1)S(1)}, bf16[128,512]{1,0:T(8,128)(2,1)}, u32[]{:S(2)}) copy-start(bf16[128,512]{1,0:T(8,128)(2,1)} %add_convert_fusion.x_ref) | copy-start | bytes 393220
  88.1 2.5 copy-start
  91.3 22.1 %copy-start.2 = (pred[128,1024]{1,0:T(8,128)(4,1)}, pred[128,1024]{1,0:T(8,128)(4,1)S(1)}, u32[]{:S(2)}) copy-start(pred[128,1024]{1,0:T(8,128)(4,1)S(1)} %fusion.4) | copy-start | bytes 393220
  91.5 22.0 %copy-start.14 = (bf16[128,512]{1,0:T(8,128)(2,1)}, bf16[128,512]{1,0:T(8,128)(2,1)S(1)}, u32[]{:S(2)}) copy-start(bf16[128,512]{1,0:T(8,128)(2,1)S(1)} %fusion.38) | copy-start | bytes 393220
  109.9 20.3 %all-to-all-start.4 = ((bf16[4,1024,128]{2,1,0:T(8,128)(2,1)}), bf16[4,1024,128]{2,1,0:T(8,128)(2,1)S(1)}, u32[]{:S(2)}, u32[]{:S(2)}) async-start(bf16[4,1024,128]{2,1,0:T(8,128)(2,1)} %broadcast_in_dim.71), calls=%async_computation.4 | async-start | bytes 2097152 | tf_op jit(solution)/shard_map/all_to_all | solution.py:224
  132.3 27.3 %all-to-all-start.3 = ((bf16[4,1024,128]{2,1,0:T(8,128)(2,1)}), bf16[4,1024,128]{2,1,0:T(8,128)(2,1)S(1)}, u32[]{:S(2)}, u32[]{:S(2)}) async-start(bf16[4,1024,128]{2,1,0:T(8,128)(2,1)} %broadcast_in_dim.69), calls=%async_computation.3 | async-start | bytes 2097152 | tf_op jit(solution)/shard_map/all_to_all | solution.py:224
  159.6 6.9 %copy-start.3 = (pred[128,1024]{1,0:T(8,128)(4,1)S(1)}, pred[128,1024]{1,0:T(8,128)(4,1)}, u32[]{:S(2)}) copy-start(pred[128,1024]{1,0:T(8,128)(4,1)} %copy-done.2) | copy-start | bytes 393220
  161.8 37.1 %all-to-all-start.2 = ((bf16[4,1024,128]{2,1,0:T(8,128)(2,1)}), bf16[4,1024,128]{2,1,0:T(8,128)(2,1)S(1)}, u32[]{:S(2)}, u32[]{:S(2)}) async-start(bf16[4,1024,128]{2,1,0:T(8,128)(2,1)} %broadcast_in_dim.67), calls=%async_computation.2 | async-start | bytes 2097152 | tf_op jit(solution)/shard_map/all_to_all | solution.py:224
  192.8 2.8 copy-start.10
  198.9 6.9 %copy-start.9 = (bf16[4,128,352]{1,0,2:T(4,128)(2,1)S(1)}, bf16[4,128,352]{1,0,2:T(4,128)(2,1)}, u32[]{:S(2)}) copy-start(bf16[4,128,352]{1,0,2:T(4,128)(2,1)} %get-tuple-element.9) | copy-start | bytes 1081348
  201.0 20.2 %all-to-all-start.1 = ((bf16[4,1024,128]{2,1,0:T(8,128)(2,1)}), bf16[4,1024,128]{2,1,0:T(8,128)(2,1)S(1)}, u32[]{:S(2)}, u32[]{:S(2)}) async-start(bf16[4,1024,128]{2,1,0:T(8,128)(2,1)} %broadcast_in_dim.36), calls=%async_computation.1 | async-start | bytes 2097152 | tf_op jit(solution)/shard_map/all_to_all | solution.py:224
  205.8 1.7 copy-start.12
  207.5 1.7 copy-start.8
  209.2 1.7 copy-start.11
  210.9 10.3 %copy-start.7 = (bf16[4,128,352]{1,0,2:T(4,128)(2,1)S(1)}, bf16[4,128,352]{1,0,2:T(4,128)(2,1)}, u32[]{:S(2)}) copy-start(bf16[4,128,352]{1,0,2:T(4,128)(2,1)} %get-tuple-element.10) | copy-start | bytes 1081348
  212.6 10.3 %copy-start.6 = (bf16[352,4,512]{2,1,0:T(4,128)(2,1)S(1)}, bf16[352,4,512]{2,1,0:T(4,128)(2,1)}, u32[]{:S(2)}) copy-start(bf16[352,4,512]{2,1,0:T(4,128)(2,1)} %reshape_squeeze.11) | copy-start | bytes 4325380
  212.6 10.3 %copy-start.15 = (bf16[4,128,352]{1,0,2:T(4,128)(2,1)S(1)}, bf16[4,128,352]{1,0,2:T(4,128)(2,1)}, u32[]{:S(2)}) copy-start(bf16[4,128,352]{1,0,2:T(4,128)(2,1)} %get-tuple-element.4) | copy-start | bytes 1081348
  288.8 10.1 %copy-start.1 = (bf16[512,512]{1,0:T(8,128)(2,1)S(1)}, bf16[512,512]{1,0:T(8,128)(2,1)}, u32[]{:S(2)}) copy-start(bf16[512,512]{1,0:T(8,128)(2,1)} %shard_map.151) | copy-start | bytes 1572868
  288.8 10.3 %copy-start.19 = (f32[128,6]{0,1:T(8,128)S(1)}, f32[128,6]{0,1:T(8,128)}, u32[]{:S(2)}) copy-start(f32[128,6]{0,1:T(8,128)} %param.25) | copy-start | bytes 9220
  288.8 43.3 %all-to-all-start.6 = ((bf16[64,16,512]{2,1,0:T(8,128)(2,1)}), bf16[64,16,512]{2,1,0:T(8,128)(2,1)S(1)}, u32[]{:S(2)}, u32[]{:S(2)}) async-start(bf16[64,16,512]{2,1,0:T(8,128)(2,1)} %bitcast.34), calls=%async_computation.6 | async-start | bytes 2097152 | tf_op jit(solution)/shard_map/all_to_all | solution.py:240
  314.9 17.2 %copy-start.5 = (bf16[128,512]{1,0:T(8,128)(2,1)S(1)}, bf16[128,512]{1,0:T(8,128)(2,1)}, u32[]{:S(2)}) copy-start(bf16[128,512]{1,0:T(8,128)(2,1)} %add_convert_fusion.x_ref) | copy-start | bytes 393220
  330.7 9.0 %copy-start.21 = (f32[512]{0:T(512)S(1)}, f32[512]{0:T(512)}, u32[]{:S(2)}) copy-start(f32[512]{0:T(512)} %param.27) | copy-start | bytes 6148
  332.8 7.7 %copy-start.13 = (bf16[128,512]{1,0:T(8,128)(2,1)}, bf16[128,512]{1,0:T(8,128)(2,1)S(1)}, u32[]{:S(2)}) copy-start(bf16[128,512]{1,0:T(8,128)(2,1)S(1)} %get-tuple-element.13) | copy-start | bytes 393220
Sparse Core Ops, SparseCore 0:
  10.7 87.0 all-gather.1

commit v16 on v13

--- a/solution.py
+++ b/solution.py
@@ -251,9 +251,10 @@
     )
 
     hidden_units = shared_gate.shape[1]
-    shared_all = lax.all_gather(
-        jnp.concatenate([shared_gate, shared_up, shared_down.T], axis=1), dp, axis=0, tiled=True
-    )
+    shared_shard, _ = lax.optimization_barrier(
+        (jnp.concatenate([shared_gate, shared_up, shared_down.T], axis=1), arrived)
+    )
+    shared_all = lax.all_gather(shared_shard, dp, axis=0, tiled=True)
     shared_gval = matmul(whole_rows, shared_all[:, :hidden_units])
     shared_uval = matmul(whole_rows, shared_all[:, hidden_units : 2 * hidden_units])
     shared_act = (jax.nn.silu(shared_gval) * shared_uval).astype(jnp.bfloat16)

time: 310 us -> 306 us (0.987)
  waiting for transfers between devices: 16.4 us -> 10.9 us
    all_to_all x2, waiting for transfers between devices: 14.7 us -> 10.8 us  [local(): lax.all_to_all(copies, 'mp', split_axis=0, concat_axis=0, tiled=True)]
  transfers between devices with their start and end apart: 5 -> 5, of which waited for: 3 -> 2; matrix products, arithmetic and copies ran while one was open for 22% -> 20% of each run, Pallas kernels for 39% -> 12%
where the time goes in v16:
time: 306 us; the launch traced here: 304 us
  Pallas kernels  126 us (41%)
  blocking collectives  55.6 us (18%)
  matrix products  32.3 us (11%)
  local copies, waits for them, and re-layouts  29.2 us (10%)
  starting transfers between devices  20.7 us (7%)
  other arithmetic  15.6 us (5%)
  between operations  14.4 us (5%)
  waiting for transfers between devices  10.9 us (4%)
    pallas_call x4, Pallas kernels, exchange(): pl.pallas_call(functools.partial(_exchange_kernel, axis), out_shape=jax.S...  76 us
    all_to_all x1, blocking collectives, local(): lax.all_to_all(partial_out, 'mp', split_axis=0, concat_axis=0, tiled=True)  53.4 us
    pallas_call x3, Pallas kernels, gather_rows(): pl.pallas_call(functools.partial(_gather_kernel, axis), out_shape=jax.Sha...  49.7 us
    all_to_all x2, waiting for transfers between devices, local(): lax.all_to_all(copies, 'mp', split_axis=0, concat_axis=0, tiled=True)  10.8 us
    all_to_all x1, starting transfers between devices, local(): lax.all_to_all(expert_out.reshape(experts, capacity, block_width), dp, sp...  8.77 us
    dot_general x1, matrix products, local(): jnp.einsum('sh,hqf->qsf', activated, down_block, preferred_element_type=j...  8.47 us
    all_to_all x2, starting transfers between devices, local(): lax.all_to_all(copies, 'mp', split_axis=0, concat_axis=0, tiled=True)  8.29 us
    dot_general x1, matrix products, local(): jnp.einsum('th,qfh->qtf', shared_act, shared_all[:, 2 * hidden_units:].re...  8.04 us
  transfers between devices with their start and end apart: 5, of which 2 were waited for; matrix products, arithmetic and copies ran while one was open for 20% of the time, Pallas kernels for 12%

profile of v16, /device:TPU:8, one launch (start us, length us, event | category | flops | bytes accessed | tf_op | source)
XLA Modules:
  0.0 304.3 jit_solution(4436309794111505769)
XLA Ops:
  7.2 34.2 %shard_map.149 = bf16[1024,512]{1,0:T(8,128)(2,1)} custom-call(bf16[32,512]{1,0:T(8,128)(2,1)} %bitcast.105), custom_call_target="tpu_custom_call" | custom-call | tf_op jit(solution)/shard_map/pallas_call | solution.py:70
  41.3 2.2 all_gather.6
  43.6 1.7 fusion.49
  45.3 1.3 copy.47
  46.6 3.6 %all-to-all-start = ((f32[2,128,1024]{1,2,0:T(8,128)}), f32[2,128,1024]{1,2,0:T(8,128)S(1)}, u32[]{:S(2)}, u32[]{:S(2)}) async-start(f32[2,128,1024]{1,2,0:T(8,128)} %copy.47), calls=%async_computation | async-start | bytes 2097152 | tf_op jit(solution)/shard_map/all_to_all | solution.py:142
  50.7 1.8 reduce-window.6
  53.1 0.5 fusion.4
  54.3 1.1 pad_maximum_fusion.x_ref
  55.4 17.5 %shard_map.150 = f32[4,129,512]{2,1,0:T(8,128)} custom-call(f32[4,129,512]{2,1,0:T(8,128)} %pad_maximum_fusion.x_ref), custom_call_target="tpu_custom_call" | custom-call | tf_op jit(solution)/shard_map/pallas_call | solution.py:127
  73.0 1.3 slice_reduce_fusion
  74.3 0.7 add_convert_fusion.x_ref
  75.0 10.0 %shard_map.151 = bf16[512,512]{1,0:T(8,128)(2,1)} custom-call(bf16[128,512]{1,0:T(8,128)(2,1)} %add_convert_fusion.x_ref), custom_call_target="tpu_custom_call" | custom-call | tf_op jit(solution)/shard_map/pallas_call | solution.py:70
  85.0 1.2 multiply_reduce_fusion
  86.3 1.0 fusion.34
  87.3 1.1 convolution_convert_fusion.1
  88.4 20.8 %shard_map.152 = bf16[64,16,256]{2,1,0:T(8,128)(2,1)} custom-call(bf16[64,16,256]{2,1,0:T(8,128)(2,1)} %bitcast.102), custom_call_target="tpu_custom_call" | custom-call | tf_op jit(solution)/shard_map/pallas_call | solution.py:127
  109.2 0.8 concatenate.7
  110.0 2.5 broadcast_in_dim.30
  112.6 3.6 %all-to-all-start.2 = ((bf16[4,1024,256]{2,1,0:T(8,128)(2,1)}), bf16[4,1024,256]{2,1,0:T(8,128)(2,1)S(1)}, u32[]{:S(2)}, u32[]{:S(2)}) async-start(bf16[4,1024,256]{2,1,0:T(8,128)(2,1)} %broadcast_in_dim.30), calls=%async_computation.2 | async-start | bytes 4194304 | tf_op jit(solution)/shard_map/all_to_all | solution.py:223
  116.2 1.2 convolution_convert_fusion
  117.3 22.0 %shard_map.154 = bf16[64,16,256]{2,1,0:T(8,128)(2,1)} custom-call(bf16[64,16,256]{2,1,0:T(8,128)(2,1)} %bitcast.101), custom_call_target="tpu_custom_call" | custom-call | tf_op jit(solution)/shard_map/pallas_call | solution.py:127
  139.3 3.7 %all-to-all-done.2 = bf16[4,1024,256]{2,1,0:T(8,128)(2,1)S(1)} async-done(((bf16[4,1024,256]{2,1,0:T(8,128)(2,1)}), bf16[4,1024,256]{2,1,0:T(8,128)(2,1)S(1)}, u32[]{:S(2)}, u32[]{:S(2)}) %all-to-all-start.2) | async-done | bytes 2097184 | tf_op jit(solution)/shard_map/all_to_all | solution.py:223
  143.0 2.9 broadcast_in_dim.28
  145.9 4.7 %all-to-all-start.1 = ((bf16[4,1024,256]{2,1,0:T(8,128)(2,1)}), bf16[4,1024,256]{2,1,0:T(8,128)(2,1)}, u32[]{:S(2)}, u32[]{:S(2)}) async-start(bf16[4,1024,256]{2,1,0:T(8,128)(2,1)} %broadcast_in_dim.28), calls=%async_computation.1 | async-start | bytes 4194304 | tf_op jit(solution)/shard_map/all_to_all | solution.py:223
  150.6 3.5 %reshape_squeeze.10 = bf16[4,512,352]{1,0,2:T(4,128)(2,1)S(1)} reshape(bf16[1,2048,352]{1,2,0:T(8,128)(2,1)} %param.22) | data formatting | bytes 2883584 | tf_op jit(solution)/shard_map/reshape;squeeze | solution.py:215
  154.1 3.5 %reshape_squeeze.9 = bf16[4,512,352]{1,0,2:T(4,128)(2,1)S(1)} reshape(bf16[1,2048,352]{1,2,0:T(8,128)(2,1)} %param.21) | data formatting | bytes 2883584 | tf_op jit(solution)/shard_map/reshape;squeeze | solution.py:214
  157.6 4.4 %reshape_squeeze.11 = bf16[352,4,512]{2,1,0:T(4,128)(2,1)} reshape(bf16[1,352,2048]{2,1,0:T(8,128)(2,1)} %param.23) | data formatting | bytes 2883584 | tf_op jit(solution)/shard_map/reshape;squeeze | solution.py:233
  162.0 1.3 fusion.48
  163.8 1.5 copy-done.3
  165.3 2.1 convolution_bitcast_fusion
  167.4 2.1 convolution_bitcast_fusion.2
  169.4 7.1 %all-to-all-done.1 = bf16[4,1024,256]{2,1,0:T(8,128)(2,1)} async-done(((bf16[4,1024,256]{2,1,0:T(8,128)(2,1)}), bf16[4,1024,256]{2,1,0:T(8,128)(2,1)}, u32[]{:S(2)}, u32[]{:S(2)}) %all-to-all-start.1) | async-done | bytes 2097184 | tf_op jit(solution)/shard_map/all_to_all | solution.py:223
  176.6 3.8 %convolution_bitcast_fusion.1 = f32[1024,352]{0,1:T(8,128)} fusion(bf16[4,1024,256]{2,1,0:T(8,128)(2,1)} %all-to-all-done.1, bf16[4,256,352]{1,0,2:T(4,128)(2,1)S(1)} %copy-done.5), kind=kOutput, calls=%fused_computation.9 | convolution fusion | flops 738197504 | bytes 4259840 | tf_op jit(solution)/shard_map/qsf,qfh->sh/dot_general | solution.py:227
  180.3 8.5 %convert_bitcast_fusion = bf16[4,1024,512]{2,1,0:T(8,128)(2,1)} fusion(bf16[352,4,512]{2,1,0:T(4,128)(2,1)S(1)} %copy-done.4, f32[1024,352]{0,1:T(8,128)} %convolution_bitcast_fusion.1, f32[1024,352]{0,1:T(8,128)} %convolution_bitcast_fusion, f32[1024,352]{0,1:T(8,128)} %convolution_bitcast_fusion.2, bf16[4,1024,256]{2,1,0:T(8,128)(2,1)} %all-to-all-done.1, ...), kind=kOutput, calls=%fused_computation | convolution fusion | flops 2219573248 | bytes 12779520 | tf_op jit(solution)/shard_map/sh,hqf->qsf/dot_general | solution.py:234
  188.8 53.4 %all_to_all.25 = bf16[4,1024,512]{2,1,0:T(8,128)(2,1)} all-to-all(bf16[4,1024,512]{2,1,0:T(8,128)(2,1)} %convert_bitcast_fusion), channel_id=1, replica_groups=mesh['g'=32,'c'=2,'mp'=4] {'mp'}, dimensions={0} | all-to-all | bytes 8388608 | tf_op jit(solution)/shard_map/all_to_all | solution.py:237
  242.2 4.1 %reduce_sum.99 = bf16[1024,512]{1,0:T(8,128)(2,1)} reduce(bf16[4,1024,512]{2,1,0:T(8,128)(2,1)} %all_to_all.25, bf16[]{:T(256)} %constant.25.clone.1), dimensions={0}, to_apply=%region_10.11 | reduce | flops 1572864 | bytes 5242882 | tf_op jit(solution)/shard_map/reduce_sum | solution.py:238
  246.3 8.8 %all-to-all-start.4 = ((bf16[64,16,512]{2,1,0:T(8,128)(2,1)}), bf16[64,16,512]{2,1,0:T(8,128)(2,1)S(1)}, u32[]{:S(2)}, u32[]{:S(2)}) async-start(bf16[64,16,512]{2,1,0:T(8,128)(2,1)} %bitcast.26), calls=%async_computation.4 | async-start | bytes 2097152 | tf_op jit(solution)/shard_map/all_to_all | solution.py:239
  255.1 0.8 slice.47
  256.9 3.8 %slice.58 = bf16[2048,704]{1,0:T(8,128)(2,1)} slice(bf16[2048,2112]{1,0:T(8,128)(2,1)} %all-gather.2.cloned.1.call-done), slice={[0:2048], [1408:2112]} | slice | bytes 5767168 | tf_op jit(solution)/shard_map/slice | solution.py:264
  260.7 3.2 %fusion.2 = f32[128,704]{0,1:T(8,128)S(1)} fusion(bf16[128,2048]{0,1:T(8,128)(2,1)S(1)} %fusion.21, bf16[2048,2112]{1,0:T(8,128)(2,1)} %all-gather.2.cloned.1.call-done), kind=kOutput, calls=%fused_computation.3 | convolution fusion | flops 369098752 | bytes 4030464 | tf_op jit(solution)/shard_map/dot_general | solution.py:19
  263.9 8.0 %convolution_bitcast_fusion.4.x_ref = f32[4,128,512]{2,1,0:T(8,128)} fusion(bf16[4,512,704]{2,1,0:T(8,128)(2,1)} %bitcast.98, bf16[128,2048]{0,1:T(8,128)(2,1)S(1)} %fusion.21, bf16[2048,2112]{1,0:T(8,128)(2,1)} %all-gather.2.cloned.1.call-done, f32[128,704]{0,1:T(8,128)S(1)} %fusion.2), kind=kOutput, calls=%fused_computation.14 | convolution fusion | flops 738738176 | bytes 8224768 | tf_op jit(solution)/shard_map/th,qfh->qtf/dot_general | solution.py:261
  271.9 15.8 %shard_map.153 = f32[4,128,512]{2,1,0:T(8,128)} custom-call(f32[4,128,512]{2,1,0:T(8,128)} %convolution_bitcast_fusion.4.x_ref), custom_call_target="tpu_custom_call" | custom-call | tf_op jit(solution)/shard_map/pallas_call | solution.py:127
  287.8 1.3 reduce_sum.97
  289.1 0.7 fusion.35
  289.8 0.6 broadcast_in_dim.54.x_ref
  290.5 5.5 %shard_map.155 = f32[32,128]{1,0:T(8,128)} custom-call(f32[8,128]{1,0:T(8,128)} %broadcast_in_dim.54.x_ref), custom_call_target="tpu_custom_call" | custom-call | tf_op jit(solution)/shard_map/pallas_call | solution.py:70
  296.0 0.7 slice_reduce_fusion.2
  296.7 0.8 fusion.37
  (56 shorter events, 3.3 us)
Async XLA Ops:
  45.2 5.0 %copy-start.13 = (s32[128,6]{0,1:T(8,128)S(1)}, s32[128,6]{0,1:T(8,128)}, u32[]{:S(2)}) copy-start(s32[128,6]{0,1:T(8,128)} %param.24) | copy-start | bytes 9220
  45.3 7.5 %copy-start.15 = (s32[64]{0:T(128)S(1)}, s32[64]{0:T(128)}, u32[]{:S(2)}) copy-start(s32[64]{0:T(128)} %param.26) | copy-start | bytes 772
  46.6 7.0 %all-to-all-start = ((f32[2,128,1024]{1,2,0:T(8,128)}), f32[2,128,1024]{1,2,0:T(8,128)S(1)}, u32[]{:S(2)}, u32[]{:S(2)}) async-start(f32[2,128,1024]{1,2,0:T(8,128)} %copy.47), calls=%async_computation | async-start | bytes 2097152 | tf_op jit(solution)/shard_map/all_to_all | solution.py:142
  50.2 206.8 %all-gather.2.cloned.1.call-start = ((), (), s32[]{:S(2)}) async-start(), calls=%async_computation.5 | async-start | bytes 9052160 | tf_op jit(solution)/shard_map/all_gather | solution.py:257
  53.7 0.7 copy-start.11
  55.4 18.8 %copy-start.7 = (bf16[128,512]{1,0:T(8,128)(2,1)S(1)}, bf16[128,512]{1,0:T(8,128)(2,1)}, u32[]{:S(2)}) copy-start(bf16[128,512]{1,0:T(8,128)(2,1)} %param.15) | copy-start | bytes 393220
  74.3 34.9 %copy-start.8 = (bf16[32,704]{1,0:T(8,128)(2,1)S(1)}, bf16[32,704]{1,0:T(8,128)(2,1)}, u32[]{:S(2)}) copy-start(bf16[32,704]{1,0:T(8,128)(2,1)} %param.18) | copy-start | bytes 135172
  74.3 34.9 %copy-start.9 = (bf16[32,704]{1,0:T(8,128)(2,1)S(1)}, bf16[32,704]{1,0:T(8,128)(2,1)}, u32[]{:S(2)}) copy-start(bf16[32,704]{1,0:T(8,128)(2,1)} %param.19) | copy-start | bytes 135172
  74.3 34.9 %copy-start.10 = (bf16[704,32]{0,1:T(8,128)(2,1)S(1)}, bf16[704,32]{0,1:T(8,128)(2,1)}, u32[]{:S(2)}) copy-start(bf16[704,32]{0,1:T(8,128)(2,1)} %param.20) | copy-start | bytes 135172
  112.6 30.5 %all-to-all-start.2 = ((bf16[4,1024,256]{2,1,0:T(8,128)(2,1)}), bf16[4,1024,256]{2,1,0:T(8,128)(2,1)S(1)}, u32[]{:S(2)}, u32[]{:S(2)}) async-start(bf16[4,1024,256]{2,1,0:T(8,128)(2,1)} %broadcast_in_dim.30), calls=%async_computation.2 | async-start | bytes 4194304 | tf_op jit(solution)/shard_map/all_to_all | solution.py:223
  143.0 2.9 copy-start.2
  145.9 30.6 %all-to-all-start.1 = ((bf16[4,1024,256]{2,1,0:T(8,128)(2,1)}), bf16[4,1024,256]{2,1,0:T(8,128)(2,1)}, u32[]{:S(2)}, u32[]{:S(2)}) async-start(bf16[4,1024,256]{2,1,0:T(8,128)(2,1)} %broadcast_in_dim.28), calls=%async_computation.1 | async-start | bytes 4194304 | tf_op jit(solution)/shard_map/all_to_all | solution.py:223
  163.3 2.0 copy-start.3
  167.4 9.2 %copy-start.5 = (bf16[4,256,352]{1,0,2:T(4,128)(2,1)S(1)}, bf16[4,256,352]{1,0,2:T(4,128)(2,1)}, u32[]{:S(2)}) copy-start(bf16[4,256,352]{1,0,2:T(4,128)(2,1)} %get-tuple-element.9) | copy-start | bytes 2162692
  176.6 3.8 %copy-start.4 = (bf16[352,4,512]{2,1,0:T(4,128)(2,1)S(1)}, bf16[352,4,512]{2,1,0:T(4,128)(2,1)}, u32[]{:S(2)}) copy-start(bf16[352,4,512]{2,1,0:T(4,128)(2,1)} %reshape_squeeze.11) | copy-start | bytes 4325380
  246.3 9.6 %copy-start = (bf16[512,512]{1,0:T(8,128)(2,1)S(1)}, bf16[512,512]{1,0:T(8,128)(2,1)}, u32[]{:S(2)}) copy-start(bf16[512,512]{1,0:T(8,128)(2,1)} %shard_map.151) | copy-start | bytes 1572868
  246.3 9.8 %copy-start.12 = (f32[128,6]{0,1:T(8,128)S(1)}, f32[128,6]{0,1:T(8,128)}, u32[]{:S(2)}) copy-start(f32[128,6]{0,1:T(8,128)} %param.25) | copy-start | bytes 9220
  246.3 42.8 %all-to-all-start.4 = ((bf16[64,16,512]{2,1,0:T(8,128)(2,1)}), bf16[64,16,512]{2,1,0:T(8,128)(2,1)S(1)}, u32[]{:S(2)}, u32[]{:S(2)}) async-start(bf16[64,16,512]{2,1,0:T(8,128)(2,1)} %bitcast.26), calls=%async_computation.4 | async-start | bytes 2097152 | tf_op jit(solution)/shard_map/all_to_all | solution.py:239
  271.9 17.2 %copy-start.1 = (bf16[128,512]{1,0:T(8,128)(2,1)S(1)}, bf16[128,512]{1,0:T(8,128)(2,1)}, u32[]{:S(2)}) copy-start(bf16[128,512]{1,0:T(8,128)(2,1)} %add_convert_fusion.x_ref) | copy-start | bytes 393220
  287.8 9.0 %copy-start.14 = (f32[512]{0:T(512)S(1)}, f32[512]{0:T(512)}, u32[]{:S(2)}) copy-start(f32[512]{0:T(512)} %param.27) | copy-start | bytes 6148
  289.8 7.7 %copy-start.6 = (bf16[128,512]{1,0:T(8,128)(2,1)}, bf16[128,512]{1,0:T(8,128)(2,1)S(1)}, u32[]{:S(2)}) copy-start(bf16[128,512]{1,0:T(8,128)(2,1)S(1)} %get-tuple-element.11) | copy-start | bytes 393220
Sparse Core Ops, SparseCore 0:
  110.1 86.3 all-gather.1
